TPU v7x, 128 devices: a whole 4x4x4 slice. The times are simulated.
128 devices in a mesh: dp: 8 (over y, core), expert: 16 (over z, x).
Axes of the slice: x: 4, y: 4, z: 4, core: 2. Of those that a mesh axis runs over, the one named last changes fastest.
Arguments:
- text: bfloat16 [16384, 5120], P(('dp', 'expert')), may hold values from -6 to 6
- patches: bfloat16 [8, 24, 24, 1408], P('dp', None, None, 'expert'), may hold values from -6 to 6
- vis_start: int32 [8], P('dp'), may hold values from 0 to 1904
- fc1: bfloat16 [4, 1408, 4096], P(None, 'expert', 'dp'), may hold values from -0.078125 to 0.078125
- fc2: bfloat16 [4096, 4096], P('expert', 'dp'), may hold values from -0.09375 to 0.09375
- proj: bfloat16 [4096, 5120], P('expert', 'dp'), may hold values from -0.09375 to 0.09375
- norm_gain: bfloat16 [5120], replicated, may hold values from 0.099609375 to 1.8984375
- router: bfloat16 [5120, 16], replicated, may hold values from -0.078125 to 0.078125
- routes: int32 [16384, 1], P(('dp', 'expert')), may hold values from 0 to 15; in each aligned block of 128 rows (0 to 127, 128 to 255, ...) at most 10 rows name the same one
- gate_w: bfloat16 [16, 5120, 4096], P('expert', None, 'dp'), may hold values from -0.15625 to 0.15625
- up_w: bfloat16 [16, 5120, 4096], P('expert', None, 'dp'), may hold values from -0.15625 to 0.15625
- down_w: bfloat16 [16, 4096, 5120], P('expert', 'dp'), may hold values from -0.09375 to 0.09375
Outputs:
- layer_out: bfloat16 [16384, 5120], P(('dp', 'expert'))
Inputs may be any that keep to these rules, and one draw needn't show every extreme that they name: `routes`: among the 128 positions of one device each expert is named at most 10 times. The image of sequence n fills the 144 positions from vis_start[n] on.
All inputs are finite; a program needn't handle non-finite values.
Results may differ from a plain program's by a relative error of at most 0.024.
Values may be sent and summed in bfloat16 or wider, within the bound.
No kernel may reach another device: no remote copies, remote signals or barrier semaphores. Data moves between devices by JAX's collectives and lax.ppermute only.
A program may use at most 128 MiB of HBM per device.

v0:
```python
import functools

import jax
import jax.numpy as jnp
from jax import lax
from jax.experimental import pallas as pl
from jax.experimental.pallas import tpu as pltpu
from jax.sharding import PartitionSpec as P

EPSILON = 1e-05
F32 = jnp.float32
BF16 = jnp.bfloat16
I32 = jnp.int32


def mm(a, b):
    return jnp.dot(a, b, preferred_element_type=F32)


def exchange(blocks):
    return lax.all_to_all(blocks, "expert", 0, 0, tiled=True)


def cut_columns(value, size):
    rows, cols = value.shape
    return value.reshape(rows, size, cols // size).transpose(1, 0, 2)


def earlier(mask):
    n = mask.shape[-1]
    tri = (jnp.arange(n)[:, None] < jnp.arange(n)[None, :]).astype(BF16)
    return mm(mask.astype(BF16), tri).astype(I32)


def norm_and_gate(rows, norm_gain, router, expert_id):
    wide = rows.astype(F32)
    mean_square = jnp.mean(wide * wide, axis=-1, keepdims=True)
    normed = (wide * lax.rsqrt(mean_square + EPSILON) * norm_gain.astype(F32)).astype(BF16)
    logits = mm(normed, router)
    named = expert_id[:, None] == jnp.arange(router.shape[1], dtype=I32)[None, :]
    score = jax.nn.sigmoid(jnp.sum(jnp.where(named, logits, 0.0), axis=-1))
    return (normed.astype(F32) * score[:, None]).astype(BF16)


def adapter_first(patches, fc1, size):
    half = patches.shape[1] // 2
    channels = patches.shape[3]
    vis_count = half * half
    shuffled = patches.reshape(half, 2, half, 2, channels)
    shuffled = shuffled.transpose(0, 2, 1, 3, 4).reshape(vis_count, 4 * channels)
    first = lax.all_gather(fc1, "dp", axis=2, tiled=True)
    first = first.reshape(4 * channels, first.shape[2])
    return cut_columns(mm(shuffled, first).astype(BF16), size)


def layer_kernel(at, row_cut, blocks_ref, weights_ref, out_ref, active):
    @pl.when(pl.program_id(0) == 0)
    def _():
        total = blocks_ref[0].astype(F32)
        for i in range(1, blocks_ref.shape[0]):
            total += blocks_ref[i].astype(F32)
        active[...] = (0.5 * total * (1.0 + lax.erf(total * (0.5**0.5)))).astype(BF16)

    width = out_ref.shape[-1]
    if row_cut:
        rows = out_ref.shape[2]
        part = mm(active[...], weights_ref[:, at : at + width]).astype(BF16)
        for i in range(row_cut):
            out_ref[i, 0] = part[i * rows : (i + 1) * rows]
    else:
        for i in range(out_ref.shape[0]):
            out_ref[i] = mm(active[...], weights_ref[:, at + i * width : at + (i + 1) * width]).astype(BF16)


def layer(blocks, weights, at, width, row_cut):
    size, tokens, inner = blocks.shape
    parts = weights.shape[0] // inner
    if row_cut:
        shape = (row_cut, parts, tokens // row_cut, width)
        out_spec = pl.BlockSpec((row_cut, 1, tokens // row_cut, width), lambda d: (0, d, 0, 0))
    else:
        shape = (size, tokens, parts * width // size)
        out_spec = pl.BlockSpec((size // parts, tokens, parts * width // size), lambda d: (d, 0, 0))
    return pl.pallas_call(
        functools.partial(layer_kernel, at, row_cut),
        grid=(parts,),
        in_specs=[
            pl.BlockSpec(blocks.shape, lambda d: (0, 0, 0)),
            pl.BlockSpec((inner, weights.shape[1]), lambda d: (d, 0)),
        ],
        out_specs=out_spec,
        out_shape=jax.ShapeDtypeStruct(shape, BF16),
        scratch_shapes=[pltpu.VMEM((tokens, inner), BF16)],
        compiler_params=pltpu.CompilerParams(dimension_semantics=("arbitrary",), vmem_limit_bytes=16 << 20),
        cost_estimate=pl.CostEstimate(
            flops=2 * tokens * inner * parts * width,
            bytes_accessed=2 * weights.size + 4 * blocks.size,
            transcendentals=tokens * inner,
        ),
        name="layer",
    )(blocks, weights)


def token_order(blocks):
    size, rows, cols = blocks.shape
    blocks = blocks.reshape(2, size // 2, rows, cols).transpose(0, 2, 1, 3)
    return blocks.reshape(2 * rows, size // 2 * cols)


CHUNK = 1280
ROW_TILE = 256


def span(index, length):
    return pl.ds(pl.multiple_of(index * length, length), length)


def expert_kernel(in_count, *refs):
    blocks = refs[:in_count]
    weights = refs[in_count : in_count + 3]
    outs = refs[in_count + 3 : -10]
    rows, gate_v, up_v, down_v, gate_acc, up_acc, hidden, in_sem, w_sem, out_sem = refs[-10:]
    feature = rows.shape[1]
    chunks = feature // CHUNK
    tiles = rows.shape[0] // ROW_TILE

    def blocks_in():
        at = 0
        for i, block in enumerate(blocks):
            yield pltpu.make_async_copy(block, rows.at[pl.ds(at, block.shape[0])], in_sem.at[i])
            at += block.shape[0]

    def inner(which, k):
        held = (gate_v, up_v)[which]
        return pltpu.make_async_copy(weights[which].at[span(k, CHUNK)], held.at[span(k, CHUNK)], w_sem.at[which, k])

    def outer(k):
        return pltpu.make_async_copy(weights[2].at[:, span(k, CHUNK)], down_v.at[:, span(k, CHUNK)], w_sem.at[2, k])

    def leaving(k):
        at = 0
        for i, out in enumerate(outs):
            count = out.shape[0]
            yield pltpu.make_async_copy(
                rows.at[pl.ds(at, count), span(k, CHUNK)], out.at[:, span(k, CHUNK)], out_sem.at[i, k]
            )
            at += count

    for copy in blocks_in():
        copy.start()

    @pl.loop(0, chunks)
    def _(k):
        inner(0, k).start()
        inner(1, k).start()

    @pl.loop(0, chunks)
    def _(k):
        outer(k).start()

    for copy in blocks_in():
        copy.wait()
    gate_acc[...] = jnp.zeros_like(gate_acc)
    up_acc[...] = jnp.zeros_like(up_acc)

    @pl.loop(0, chunks)
    def _(k):
        inner(0, k).wait()
        inner(1, k).wait()

        @pl.loop(0, tiles)
        def _(t):
            part = rows[span(t, ROW_TILE), span(k, CHUNK)]
            gate_acc[span(t, ROW_TILE), :] += mm(part, gate_v[span(k, CHUNK), :])
            up_acc[span(t, ROW_TILE), :] += mm(part, up_v[span(k, CHUNK), :])

    hidden[...] = (jax.nn.silu(gate_acc[...]) * up_acc[...]).astype(BF16)

    @pl.loop(0, chunks)
    def _(k):
        outer(k).wait()

        @pl.loop(0, tiles)
        def _(t):
            made = mm(hidden[span(t, ROW_TILE), :], down_v[:, span(k, CHUNK)])
            rows[span(t, ROW_TILE), span(k, CHUNK)] = made.astype(BF16)

        for copy in leaving(k):
            copy.start()

    @pl.loop(0, chunks)
    def _(k):
        for copy in leaving(k):
            copy.wait()


def expert_part(blocks, out_rows, gate_w, up_w, down_w):
    feature, width = gate_w.shape
    count = sum(block.shape[0] for block in blocks)
    chunks = feature // CHUNK
    weights = [pltpu.with_memory_space_constraint(w, pltpu.HBM) for w in (gate_w, up_w, down_w)]
    anywhere = pl.BlockSpec(memory_space=pl.ANY)
    return pl.pallas_call(
        functools.partial(expert_kernel, len(blocks)),
        in_specs=[anywhere] * (len(blocks) + 3),
        out_specs=[anywhere] * len(out_rows),
        out_shape=[jax.ShapeDtypeStruct((rows, feature), BF16) for rows in out_rows],
        scratch_shapes=[
            pltpu.VMEM((count, feature), BF16),
            pltpu.VMEM((feature, width), BF16),
            pltpu.VMEM((feature, width), BF16),
            pltpu.VMEM((width, feature), BF16),
            pltpu.VMEM((count, width), F32),
            pltpu.VMEM((count, width), F32),
            pltpu.VMEM((count, width), BF16),
            pltpu.SemaphoreType.DMA((len(blocks),)),
            pltpu.SemaphoreType.DMA((3, chunks)),
            pltpu.SemaphoreType.DMA((len(out_rows), chunks)),
        ],
        compiler_params=pltpu.CompilerParams(vmem_limit_bytes=28 << 20),
        cost_estimate=pl.CostEstimate(
            flops=6 * count * feature * width,
            bytes_accessed=6 * feature * width + 4 * count * feature,
            transcendentals=count * width,
        ),
        name="expert_part",
    )(*blocks, *weights)


def ring(value, step):
    size = lax.axis_size("dp")
    return lax.ppermute(value, "dp", [(i, (i + 2 * step) % size) for i in range(size)])


def swap(value):
    size = lax.axis_size("dp")
    return lax.ppermute(value, "dp", [(i, i ^ 1) for i in range(size)])


def tie(*values):
    return lax.optimization_barrier(values)


def after(first, *values):
    return lax.optimization_barrier((*values, first))[:-1]


def add(*terms):
    total = terms[0].astype(F32)
    for term in terms[1:]:
        total = total + term.astype(F32)
    return total.astype(BF16)


def on_device(
    text, patches, vis_start, fc1, fc2, proj, norm_gain, router, routes, gate_w, up_w, down_w
):
    size = lax.axis_size("expert")
    me = lax.axis_index("expert")
    row_count, feature = text.shape
    experts_all = router.shape[1]
    vis_count = (patches.shape[1] // 2) ** 2
    capacity = max(2, row_count * 5 // (4 * size))
    first = vis_start[0]
    expert_id = routes[:, 0]
    total = size * capacity
    rows_a = size * (capacity // 8 * 8)
    rows_b = total - rows_a

    lanes = jnp.arange(row_count, dtype=I32)
    offsets = me * row_count + lanes - first
    in_image = (offsets >= 0) & (offsets < vis_count)
    named = jnp.arange(experts_all, dtype=I32)[:, None] == expert_id[None, :]
    named_text = named & ~in_image[None, :]
    named_img = named & in_image[None, :]
    text_total = jnp.sum(named_text.astype(I32), axis=1, keepdims=True)
    before = jnp.where(in_image[None, :], earlier(named_img) + text_total, earlier(named_text))
    rank = jnp.sum(jnp.where(named, before, 0), axis=0)
    key = expert_id * capacity + rank
    slots = jnp.arange(total, dtype=I32)
    home = slots[:, None] == key[None, :]

    routed = norm_and_gate(text, norm_gain, router, expert_id)
    leaving = mm((home & ~in_image[None, :]).astype(BF16), routed).astype(BF16)
    spare = jnp.broadcast_to(expert_id.astype(BF16), (size, 8, row_count))
    slab = capacity * feature // row_count
    leaving = jnp.concatenate([leaving.reshape(size, slab, row_count), spare], axis=1)
    arrived = exchange(leaving)
    all_routes = arrived[:, slab, :].astype(I32).reshape(size * row_count)
    pre_blocks, arrived = lax.optimization_barrier((adapter_first(patches, fc1, size), arrived))
    arrived = arrived[:, :slab, :].reshape(total, feature)
    later = lax.all_gather(jnp.concatenate([fc2, proj], axis=1), "dp", axis=0, tiled=True)
    second_blocks = layer(exchange(pre_blocks), later, 0, fc2.shape[1], 0)

    mine = (all_routes == me).reshape(size, row_count)
    spots = jnp.arange(size * row_count, dtype=I32).reshape(size, row_count) - first
    row_image = (spots >= 0) & (spots < vis_count)
    text_count = jnp.sum((mine & ~row_image).astype(I32), axis=1)
    img_count = jnp.sum((mine & row_image).astype(I32), axis=1)
    blocks_before = jnp.arange(size)[:, None] > jnp.arange(size)[None, :]
    text_before = jnp.sum(jnp.where(blocks_before, text_count[None, :], 0), axis=1)
    img_before = jnp.sum(jnp.where(blocks_before, img_count[None, :], 0), axis=1)
    base = rows_a + jnp.maximum(jnp.sum(text_count) - rows_a, 0)
    ranks = jnp.arange(capacity, dtype=I32)[None, :]
    text_slot = ranks < text_count[:, None]
    img_slot = ~text_slot & (ranks < (text_count + img_count)[:, None])
    text_row = text_before[:, None] + ranks
    img_row = base + (img_before - text_count)[:, None] + ranks
    row_of = jnp.where(text_slot, text_row, jnp.where(img_slot, img_row, -1))
    row_of_text = jnp.where(text_slot, text_row, -1).reshape(total)
    row_of = row_of.reshape(total)
    pack = (slots[:, None] == row_of_text[None, :]).astype(BF16)
    unpack = (row_of[:, None] == slots[None, :]).astype(BF16)

    run = lambda blocks, out_rows: expert_part(blocks, out_rows, gate_w[0], up_w[0], down_w[0])
    chunk_a = mm(pack[:rows_a], arrived).astype(BF16)
    half = rows_a // 2
    below, above, other = ring(chunk_a, 1), ring(chunk_a, -1), swap(chunk_a)
    own, other = after(second_blocks, chunk_a, other)
    mine, theirs = run([own, other], (rows_a, rows_a))
    below, above = after(theirs, below, above)
    far_top, far_low = ring(below[:half], 1), ring(above[half:], -1)
    below_pair, above_pair = swap(below), swap(above)
    second_blocks, mine, theirs = tie(exchange(second_blocks), mine, theirs)
    third_blocks = layer(second_blocks, later, fc2.shape[1], proj.shape[1], 2)
    third_blocks = third_blocks.reshape(size, vis_count // 2, proj.shape[1])

    below, above, below_pair, above_pair = after(third_blocks, below, above, below_pair, above_pair)
    below_top, below_low, below_other, above_top, above_low, above_other = run(
        [below, below_pair, above, above_pair], (half, half, rows_a, half, half, rows_a)
    )
    far_top_pair, far_low_pair = swap(far_top), swap(far_low)
    mine_too = swap(theirs)
    visual_blocks, below_other, above_other, mine_too = tie(
        exchange(third_blocks), below_other, above_other, mine_too
    )
    visual_mine = jnp.sum(visual_blocks.astype(F32), axis=0).astype(BF16)

    visual_blocks = jnp.broadcast_to(visual_mine[None], (size, *visual_mine.shape))
    far_top, far_low, far_top_pair, far_low_pair = after(
        visual_blocks, far_top, far_low, far_top_pair, far_low_pair
    )
    below_too, above_too = swap(below_other), swap(above_other)
    far_mine_top, far_mine_low, far_theirs = run(
        [far_top, far_low, far_top_pair, far_low_pair], (half, half, rows_a)
    )
    from_below_low = ring(add(above_low, above_too[half:]), 1)
    from_above_top = ring(add(below_top, below_too[:half]), -1)
    far_too = swap(far_theirs)
    visual = token_order(exchange(visual_blocks))
    visual, far_too = tie(visual, far_too)
    pass_up = ring(add(far_mine_top, far_too[:half]), 1)
    pass_down = ring(add(far_mine_low, far_too[half:]), -1)
    img_routes = lax.dynamic_slice(all_routes, (first,), (vis_count,))
    routed_img = norm_and_gate(visual, norm_gain, router, img_routes)
    mine_img = img_routes == me
    img_rank = earlier(mine_img[None, :])[0] + (base - rows_a)
    take = (jnp.arange(rows_b, dtype=I32)[:, None] == jnp.where(mine_img, img_rank, -1)[None, :]).astype(BF16)
    chunk_b = (mm(pack[rows_a:], arrived) + mm(take, routed_img)).astype(BF16)
    gathered_b = lax.all_gather(chunk_b, "dp", axis=0, tiled=True)
    gathered_b, pass_up, pass_down = tie(gathered_b, pass_up, pass_down)
    from_below_top = ring(add(above_top, above_too[:half], pass_up), 1)
    from_above_low = ring(add(below_low, below_too[half:], pass_down), -1)
    (part_b,) = run([gathered_b], (gathered_b.shape[0],))
    done_b = lax.psum_scatter(part_b, "dp", scatter_dimension=0, tiled=True)
    top = add(mine[:half], mine_too[:half], from_below_top, from_above_top)
    low = add(mine[half:], mine_too[half:], from_below_low, from_above_low)
    done_a = jnp.concatenate([top, low])

    back = (mm(unpack[:, :rows_a], done_a) + mm(unpack[:, rows_a:], done_b)).astype(BF16)
    back = exchange(back.reshape(size, slab, row_count)).reshape(total, feature)
    turn = (((0,), (0,)), ((), ()))
    combined = lax.dot_general(home.astype(BF16), back, turn, preferred_element_type=F32)
    pick = (offsets[:, None] == jnp.arange(vis_count, dtype=I32)[None, :]).astype(BF16)
    embedded = jnp.where(in_image[:, None], mm(pick, visual), text.astype(F32))
    return (embedded + combined).astype(BF16)


def solution(mesh):
    return jax.shard_map(
        on_device,
        mesh=mesh,
        in_specs=(
            P(("dp", "expert"), None),
            P("dp", None, None, "expert"),
            P("dp"),
            P(None, "expert", "dp"),
            P("expert", "dp"),
            P("expert", "dp"),
            P(),
            P(),
            P(("dp", "expert"), None),
            P("expert", None, "dp"),
            P("expert", None, "dp"),
            P("expert", "dp", None),
        ),
        out_specs=P(("dp", "expert"), None),
        check_vma=False,
    )
```

profile of v0, /device:TPU:17, one launch (start us, length us, event | category | flops | bytes accessed | tf_op | source)
XLA Modules:
  0.0 316.3 jit_solution(11470036135920074439)
XLA Ops:
  7.3 1.9 pad_maximum_fusion.1
  12.9 1.4 pad_maximum_fusion
  14.3 7.7 %all-to-all-start = ((bf16[16,408,128]{2,1,0:T(8,128)(2,1)}), bf16[16,408,128]{2,1,0:T(8,128)(2,1)S(1)}, u32[]{:S(2)}, u32[]{:S(2)}) async-start(bf16[16,408,128]{2,1,0:T(8,128)(2,1)} %pad_maximum_fusion), calls=%async_computation | async-start | bytes 3342336 | tf_op jit(solution)/shard_map/all_to_all | solution.py:21
  22.3 24.0 %all-to-all-done = bf16[16,408,128]{2,1,0:T(8,128)(2,1)S(1)} async-done(((bf16[16,408,128]{2,1,0:T(8,128)(2,1)}), bf16[16,408,128]{2,1,0:T(8,128)(2,1)S(1)}, u32[]{:S(2)}, u32[]{:S(2)}) %all-to-all-start) | async-done | bytes 1671200 | tf_op jit(solution)/shard_map/all_to_all | solution.py:21
  48.5 2.8 convolution_convert_fusion.2
  52.4 1.3 slice.56
  53.7 2.6 reshape.229
  57.5 2.6 collective-permute-start
  60.2 3.7 %all-to-all-start.1 = ((bf16[16,144,256]{2,1,0:T(8,128)(2,1)}), bf16[16,144,256]{2,1,0:T(8,128)(2,1)S(1)}, u32[]{:S(2)}, u32[]{:S(2)}) async-start(bf16[16,144,256]{2,1,0:T(8,128)(2,1)} %bitcast.64), calls=%async_computation.1 | async-start | bytes 2359296 | tf_op jit(solution)/shard_map/all_to_all | solution.py:21
  65.4 19.8 %all-to-all-done.1.blocks_ref = bf16[16,144,256]{2,1,0:T(8,128)(2,1)S(1)} async-done(((bf16[16,144,256]{2,1,0:T(8,128)(2,1)}), bf16[16,144,256]{2,1,0:T(8,128)(2,1)S(1)}, u32[]{:S(2)}, u32[]{:S(2)}) %all-to-all-start.1) | async-done | bytes 1179680 | tf_op jit(solution)/shard_map/all_to_all | solution.py:21
  85.2 2.3 copy-done.1
  87.5 1.8 layer.2
  90.3 3.7 %all-to-all-start.2 = ((bf16[16,144,256]{2,1,0:T(8,128)(2,1)}), bf16[16,144,256]{2,1,0:T(8,128)(2,1)S(1)}, u32[]{:S(2)}, u32[]{:S(2)}) async-start(bf16[16,144,256]{2,1,0:T(8,128)(2,1)} %copy-done.3), calls=%async_computation.2 | async-start | bytes 2359296 | tf_op jit(solution)/shard_map/all_to_all | solution.py:21
  94.1 8.8 %expert_part.4 = (bf16[128,5120]{1,0:T(8,128)(2,1)S(1)}, bf16[128,5120]{1,0:T(8,128)(2,1)}) custom-call(bf16[128,5120]{1,0:T(8,128)(2,1)S(1)} %convolution_convert_fusion.1.refs_0_, bf16[128,5120]{1,0:T(8,128)(2,1)} %collective-permute-done.refs_1_, bf16[5120,512]{1,0:T(8,128)(2,1)} %bitcast.46, bf16[5120,512]{1,0:T(8,128)(2,1)} %bitcast.50, ...), custom_call_target="tpu_custom_call" | custom-call | flops 4026531840 | bytes 20971520 | tf_op jit(solution)/shard_map/expert_part/pallas_call | solution.py:203
  103.9 2.0 slice.57
  108.5 3.0 all-to-all-done.2.blocks_ref
  111.6 2.3 copy-done.2
  113.9 4.0 %layer.3 = bf16[2,8,72,640]{3,2,1,0:T(8,128)(2,1)} custom-call(bf16[16,144,256]{2,1,0:T(8,128)(2,1)S(1)} %all-to-all-done.2.blocks_ref, bf16[2048,1152]{1,0:T(8,128)(2,1)S(1)} %copy-done.2), custom_call_target="tpu_custom_call" | custom-call | flops 377487360 | bytes 7077888 | tf_op jit(solution)/shard_map/layer/pallas_call | solution.py:84
  118.0 5.0 %all-to-all-start.3 = ((bf16[16,72,640]{2,1,0:T(8,128)(2,1)}), bf16[16,72,640]{2,1,0:T(8,128)(2,1)}, u32[]{:S(2)}, u32[]{:S(2)}) async-start(bf16[16,72,640]{2,1,0:T(8,128)(2,1)} %bitcast.10), calls=%async_computation.3 | async-start | bytes 2949120 | tf_op jit(solution)/shard_map/all_to_all | solution.py:21
  123.0 2.1 collective-permute-start.5
  125.6 16.0 %expert_part.5 = (bf16[64,5120]{1,0:T(8,128)(2,1)S(1)}, bf16[64,5120]{1,0:T(8,128)(2,1)S(1)}, bf16[128,5120]{1,0:T(8,128)(2,1)}, bf16[64,5120]{1,0:T(8,128)(2,1)...) custom-call(bf16[128,5120]{1,0:T(8,128)(2,1)} %collective-permute-done.1.refs_0_, ...), custom_call_target="tpu_custom_call" | custom-call | flops 8053063680 | bytes 26214400 | tf_op jit(solution)/shard_map/expert_part/pallas_call | solution.py:203
  145.3 1.6 reduce_sum.117
  146.9 1.2 broadcast_in_dim.63
  148.1 6.8 %all-to-all-start.4 = ((bf16[16,72,640]{2,1,0:T(8,128)(2,1)}), bf16[16,72,640]{2,1,0:T(8,128)(2,1)}, u32[]{:S(2)}, u32[]{:S(2)}) async-start(bf16[16,72,640]{2,1,0:T(8,128)(2,1)} %broadcast_in_dim.63), calls=%async_computation.4 | async-start | bytes 2949120 | tf_op jit(solution)/shard_map/all_to_all | solution.py:21
  155.0 9.4 %expert_part.6 = (bf16[64,5120]{1,0:T(8,128)(2,1)S(1)}, bf16[64,5120]{1,0:T(8,128)(2,1)S(1)}, bf16[128,5120]{1,0:T(8,128)(2,1)}) custom-call(bf16[64,5120]{1,0:T(8,128)(2,1)S(1)} %collective-permute-done.6.refs_0_, bf16[64,5120]{1,0:T(8,128)(2,1)S(1)} %collective-permute-done.7.refs_1_, bf16[64,5120]{1,0:T(8,128)(2,1)S(1)} %collective-permute-done.8.refs_2_, ...), custom_call_target="tpu_custom_call" | custom-call | flops 4026531840 | bytes 20971520 | tf_op jit(solution)/shard_map/expert_part/pallas_call | solution.py:203
  166.8 2.6 fusion.37
  169.4 8.7 %all-to-all-done.4 = bf16[16,72,640]{2,1,0:T(8,128)(2,1)} async-done(((bf16[16,72,640]{2,1,0:T(8,128)(2,1)}), bf16[16,72,640]{2,1,0:T(8,128)(2,1)}, u32[]{:S(2)}, u32[]{:S(2)}) %all-to-all-start.4) | async-done | bytes 1474592 | tf_op jit(solution)/shard_map/all_to_all | solution.py:21
  178.1 1.6 copy.29
  181.5 1.4 fusion.3
  183.4 1.3 collective-permute-start.12
  184.9 1.9 collective-permute-start.15
  186.8 16.9 %collective-permute-done.12 = bf16[64,5120]{1,0:T(8,128)(2,1)} collective-permute-done((bf16[64,5120]{1,0:T(8,128)(2,1)S(1)}, bf16[64,5120]{1,0:T(8,128)(2,1)}, u32[]{:S(2)}, u32[]{:S(2)}) %collective-permute-start.12) | collective-permute-done | bytes 655392 | tf_op jit(solution)/shard_map/ppermute | solution.py:232
  204.9 8.7 %all-gather.8.cloned.1.call-done.refs_0_ = bf16[256,5120]{1,0:T(8,128)(2,1)} async-done(((bf16[32,5120]{1,0:T(8,128)(2,1)}), bf16[256,5120]{1,0:T(8,128)(2,1)}) %all-gather.8.cloned.1.call-update) | async-done | bytes 2621456 | tf_op jit(solution)/shard_map/all_gather | solution.py:360
  213.6 1.7 copy-done.4
  215.3 8.5 %expert_part.7 = bf16[256,5120]{1,0:T(8,128)(2,1)} custom-call(bf16[256,5120]{1,0:T(8,128)(2,1)S(1)} %copy-done.4, bf16[5120,512]{1,0:T(8,128)(2,1)} %bitcast.49, bf16[5120,512]{1,0:T(8,128)(2,1)} %bitcast.53, bf16[512,5120]{1,0:T(8,128)(2,1)} %bitcast.57), custom_call_target="tpu_custom_call" | custom-call | flops 4026531840 | bytes 20971520 | tf_op jit(solution)/shard_map/expert_part/pallas_call | solution.py:203
  223.9 1.3 copy-done.18
  225.5 2.0 add_convert_fusion.4
  228.2 1.6 add_convert_fusion.5
  231.3 1.9 collective-permute-start.17
  233.3 15.6 %collective-permute-done.16 = bf16[64,5120]{1,0:T(8,128)(2,1)S(1)} collective-permute-done((bf16[64,5120]{1,0:T(8,128)(2,1)S(1)}, bf16[64,5120]{1,0:T(8,128)(2,1)S(1)}, u32[]{:S(2)}, u32[]{:S(2)}) %collective-permute-start.16) | collective-permute-done | bytes 655392 | tf_op jit(solution)/shard_map/ppermute | solution.py:232
  248.9 4.2 %collective-permute-done.14 = bf16[64,5120]{1,0:T(8,128)(2,1)S(1)} collective-permute-done((bf16[64,5120]{1,0:T(8,128)(2,1)S(1)}, bf16[64,5120]{1,0:T(8,128)(2,1)S(1)}, u32[]{:S(2)}, u32[]{:S(2)}) %collective-permute-start.14) | collective-permute-done | bytes 655392 | tf_op jit(solution)/shard_map/ppermute | solution.py:232
  253.1 16.8 %collective-permute-done.18 = bf16[64,5120]{1,0:T(8,128)(2,1)S(1)} collective-permute-done((bf16[64,5120]{1,0:T(8,128)(2,1)S(1)}, bf16[64,5120]{1,0:T(8,128)(2,1)S(1)}, u32[]{:S(2)}, u32[]{:S(2)}) %collective-permute-start.18) | collective-permute-done | bytes 655392 | tf_op jit(solution)/shard_map/ppermute | solution.py:232
  269.9 2.2 collective-permute-done.17
  272.1 2.1 add_convert_fusion.3
  274.2 1.5 fusion.30
  277.2 26.6 %all_to_all.30 = bf16[16,400,128]{2,1,0:T(8,128)(2,1)} all-to-all(bf16[16,400,128]{2,1,0:T(8,128)(2,1)S(1)} %reshape.233), channel_id=1, replica_groups=mesh['dp'=8,'expert'=16] {'expert'}, dimensions={0} | all-to-all | bytes 3276800 | tf_op jit(solution)/shard_map/all_to_all | solution.py:21
  303.8 2.6 reshape.234
  308.1 1.7 fusion.2
  (151 shorter events, 29.9 us)
Async XLA Ops:
  6.5 4.2 %copy-start = (bf16[5120,16]{0,1:T(8,128)(2,1)S(1)}, bf16[5120,16]{0,1:T(8,128)(2,1)}, u32[]{:S(2)}) copy-start(bf16[5120,16]{0,1:T(8,128)(2,1)} %param.19) | copy-start | bytes 491524
  6.5 2.7 copy-start.29
  6.5 3.5 %copy-start.32 = (s32[128,1]{0,1:T(1,128)S(1)}, s32[128,1]{0,1:T(1,128)}, u32[]{:S(2)}) copy-start(s32[128,1]{0,1:T(1,128)} %param.20) | copy-start | bytes 1540
  6.5 3.9 %copy-start.22 = (bf16[128,5120]{1,0:T(8,128)(2,1)S(1)}, bf16[128,5120]{1,0:T(8,128)(2,1)}, u32[]{:S(2)}) copy-start(bf16[128,5120]{1,0:T(8,128)(2,1)} %param.12) | copy-start | bytes 3932164
  6.5 42.0 %all-gather.4.cloned.1.call-start = ((), (), s32[]{:S(2)}) async-start(), calls=%async_computation.7 | async-start | bytes 3244032 | tf_op jit(solution)/shard_map/all_gather | solution.py:51
  7.3 77.9 %all-gather.6.cloned.1.call-start = ((), (), s32[]{:S(2)}) async-start(), calls=%async_computation.8 | async-start | bytes 5308416 | tf_op jit(solution)/shard_map/all_gather | solution.py:292
  9.3 2.0 copy-start.27
  14.3 7.7 %copy-start.26 = (bf16[1,24,24,88]{3,2,1,0:T(8,128)(2,1)S(1)}, bf16[1,24,24,88]{3,2,1,0:T(8,128)(2,1)}, u32[]{:S(2)}) copy-start(bf16[1,24,24,88]{3,2,1,0:T(8,128)(2,1)} %param.13) | copy-start | bytes 304132
  14.3 32.0 %all-to-all-start = ((bf16[16,408,128]{2,1,0:T(8,128)(2,1)}), bf16[16,408,128]{2,1,0:T(8,128)(2,1)S(1)}, u32[]{:S(2)}, u32[]{:S(2)}) async-start(bf16[16,408,128]{2,1,0:T(8,128)(2,1)} %pad_maximum_fusion), calls=%async_computation | async-start | bytes 3342336 | tf_op jit(solution)/shard_map/all_to_all | solution.py:21
  48.5 7.8 %copy-start.25 = (pred[160,160]{1,0:T(32,128)(4,1)}, pred[160,160]{1,0:T(32,128)(4,1)S(1)}, u32[]{:S(2)}) copy-start(pred[160,160]{1,0:T(32,128)(4,1)S(1)} %iota_compare_fusion.1) | copy-start | bytes 76804
  57.5 36.5 %collective-permute-start = (bf16[128,5120]{1,0:T(8,128)(2,1)S(1)}, bf16[128,5120]{1,0:T(8,128)(2,1)}, u32[]{:S(2)}, u32[]{:S(2)}) collective-permute-start(bf16[128,5120]{1,0:T(8,128)(2,1)S(1)} %convolution_convert_fusion.1.refs_0_), channel_id=1, source_target_pairs={{0,16},{16,0},{32,48},{48,32},{64,80},{80,64},{96,112},{112,96},{1... | collective-permute-start | bytes 3932168 | tf_op jit(solution)/shard_map/ppermute | solution.py:237
  60.2 25.0 %all-to-all-start.1 = ((bf16[16,144,256]{2,1,0:T(8,128)(2,1)}), bf16[16,144,256]{2,1,0:T(8,128)(2,1)S(1)}, u32[]{:S(2)}, u32[]{:S(2)}) async-start(bf16[16,144,256]{2,1,0:T(8,128)(2,1)} %bitcast.64), calls=%async_computation.1 | async-start | bytes 2359296 | tf_op jit(solution)/shard_map/all_to_all | solution.py:21
  63.9 39.0 %collective-permute-start.1 = (bf16[128,5120]{1,0:T(8,128)(2,1)S(1)}, bf16[128,5120]{1,0:T(8,128)(2,1)}, u32[]{:S(2)}, u32[]{:S(2)}) collective-permute-start(bf16[128,5120]{1,0:T(8,128)(2,1)S(1)} %convolution_convert_fusion.1.refs_0_), channel_id=1, source_target_pairs={{0,32},{16,48},{32,64},{48,80},{64,96},{80,112},{96,0},{112,16},{1... | collective-permute-start | bytes 3932168 | tf_op jit(solution)/shard_map/ppermute | solution.py:232
  64.9 38.0 %collective-permute-start.2 = (bf16[128,5120]{1,0:T(8,128)(2,1)S(1)}, bf16[128,5120]{1,0:T(8,128)(2,1)}, u32[]{:S(2)}, u32[]{:S(2)}) collective-permute-start(bf16[128,5120]{1,0:T(8,128)(2,1)S(1)} %convolution_convert_fusion.1.refs_0_), channel_id=1, source_target_pairs={{0,96},{16,112},{32,0},{48,16},{64,32},{80,48},{96,64},{112,80},{1... | collective-permute-start | bytes 3932168 | tf_op jit(solution)/shard_map/ppermute | solution.py:232
  85.2 2.3 copy-start.1
  90.3 21.2 %all-to-all-start.2 = ((bf16[16,144,256]{2,1,0:T(8,128)(2,1)}), bf16[16,144,256]{2,1,0:T(8,128)(2,1)S(1)}, u32[]{:S(2)}, u32[]{:S(2)}) async-start(bf16[16,144,256]{2,1,0:T(8,128)(2,1)} %copy-done.3), calls=%async_computation.2 | async-start | bytes 2359296 | tf_op jit(solution)/shard_map/all_to_all | solution.py:21
  102.9 5.2 %copy-start.5 = (bf16[128,5120]{1,0:T(8,128)(2,1)}, bf16[128,5120]{1,0:T(8,128)(2,1)S(1)}, u32[]{:S(2)}) copy-start(bf16[128,5120]{1,0:T(8,128)(2,1)S(1)} %get-tuple-element.65) | copy-start | bytes 3932164
  102.9 22.7 %collective-permute-start.3 = (bf16[128,5120]{1,0:T(8,128)(2,1)}, bf16[128,5120]{1,0:T(8,128)(2,1)}, u32[]{:S(2)}, u32[]{:S(2)}) collective-permute-start(bf16[128,5120]{1,0:T(8,128)(2,1)} %collective-permute-done.1.refs_0_), channel_id=1, source_target_pairs={{0,16},{16,0},{32,48},{48,32},{64,80},{80,64},{96,112},{112,96},{1... | collective-permute-start | bytes 3932168 | tf_op jit(solution)/shard_map/ppermute | solution.py:237
  103.8 21.8 %collective-permute-start.4 = (bf16[128,5120]{1,0:T(8,128)(2,1)}, bf16[128,5120]{1,0:T(8,128)(2,1)}, u32[]{:S(2)}, u32[]{:S(2)}) collective-permute-start(bf16[128,5120]{1,0:T(8,128)(2,1)} %collective-permute-done.2.refs_2_), channel_id=1, source_target_pairs={{0,16},{16,0},{32,48},{48,32},{64,80},{80,64},{96,112},{112,96},{1... | collective-permute-start | bytes 3932168 | tf_op jit(solution)/shard_map/ppermute | solution.py:237
  107.0 18.1 %collective-permute-start.6 = (bf16[64,5120]{1,0:T(8,128)(2,1)}, bf16[64,5120]{1,0:T(8,128)(2,1)S(1)}, u32[]{:S(2)}, u32[]{:S(2)}) collective-permute-start(bf16[64,5120]{1,0:T(8,128)(2,1)} %slice.57), channel_id=1, source_target_pairs={{0,32},{16,48},{32,64},{48,80},{64,96},{80,112},{96,0},{112,16},{1... | collective-permute-start | bytes 1966088 | tf_op jit(solution)/shard_map/ppermute | solution.py:232
  108.1 17.1 %collective-permute-start.7 = (bf16[64,5120]{1,0:T(8,128)(2,1)S(1)}, bf16[64,5120]{1,0:T(8,128)(2,1)S(1)}, u32[]{:S(2)}, u32[]{:S(2)}) collective-permute-start(bf16[64,5120]{1,0:T(8,128)(2,1)S(1)} %slice.58), channel_id=1, source_target_pairs={{0,96},{16,112},{32,0},{48,16},{64,32},{80,48},{96,64},{112,80},{1... | collective-permute-start | bytes 1966088 | tf_op jit(solution)/shard_map/ppermute | solution.py:232
  111.6 2.3 copy-start.2
  118.0 27.3 %all-to-all-start.3 = ((bf16[16,72,640]{2,1,0:T(8,128)(2,1)}), bf16[16,72,640]{2,1,0:T(8,128)(2,1)}, u32[]{:S(2)}, u32[]{:S(2)}) async-start(bf16[16,72,640]{2,1,0:T(8,128)(2,1)} %bitcast.10), calls=%async_computation.3 | async-start | bytes 2949120 | tf_op jit(solution)/shard_map/all_to_all | solution.py:21
  123.0 22.3 %collective-permute-start.5 = (bf16[128,5120]{1,0:T(8,128)(2,1)}, bf16[128,5120]{1,0:T(8,128)(2,1)}, u32[]{:S(2)}, u32[]{:S(2)}) collective-permute-start(bf16[128,5120]{1,0:T(8,128)(2,1)} %get-tuple-element.57), channel_id=1, source_target_pairs={{0,16},{16,0},{32,48},{48,32},{64,80},{80,64},{96,112},{112,96},{1... | collective-permute-start | bytes 3932168 | tf_op jit(solution)/shard_map/ppermute | solution.py:237
  125.1 29.9 %collective-permute-start.8 = (bf16[64,5120]{1,0:T(8,128)(2,1)S(1)}, bf16[64,5120]{1,0:T(8,128)(2,1)S(1)}, u32[]{:S(2)}, u32[]{:S(2)}) collective-permute-start(bf16[64,5120]{1,0:T(8,128)(2,1)S(1)} %collective-permute-done.6.refs_0_), channel_id=1, source_target_pairs={{0,16},{16,0},{32,48},{48,32},{64,80},{80,64},{96,112},{112,96},{1... | collective-permute-start | bytes 1966088 | tf_op jit(solution)/shard_map/ppermute | solution.py:237
  125.2 29.8 %collective-permute-start.9 = (bf16[64,5120]{1,0:T(8,128)(2,1)S(1)}, bf16[64,5120]{1,0:T(8,128)(2,1)S(1)}, u32[]{:S(2)}, u32[]{:S(2)}) collective-permute-start(bf16[64,5120]{1,0:T(8,128)(2,1)S(1)} %collective-permute-done.7.refs_1_), channel_id=1, source_target_pairs={{0,16},{16,0},{32,48},{48,32},{64,80},{80,64},{96,112},{112,96},{1... | collective-permute-start | bytes 1966088 | tf_op jit(solution)/shard_map/ppermute | solution.py:237
  148.1 30.0 %all-to-all-start.4 = ((bf16[16,72,640]{2,1,0:T(8,128)(2,1)}), bf16[16,72,640]{2,1,0:T(8,128)(2,1)}, u32[]{:S(2)}, u32[]{:S(2)}) async-start(bf16[16,72,640]{2,1,0:T(8,128)(2,1)} %broadcast_in_dim.63), calls=%async_computation.4 | async-start | bytes 2949120 | tf_op jit(solution)/shard_map/all_to_all | solution.py:21
  154.9 58.7 %all-gather.8.cloned.1.call-start = ((), (), s32[]{:S(2)}) async-start(), calls=%async_computation.9 | async-start | bytes 2949120 | tf_op jit(solution)/shard_map/all_gather | solution.py:360
  166.0 13.9 %collective-permute-start.10 = (bf16[128,5120]{1,0:T(8,128)(2,1)}, bf16[128,5120]{1,0:T(8,128)(2,1)S(1)}, u32[]{:S(2)}, u32[]{:S(2)}) collective-permute-start(bf16[128,5120]{1,0:T(8,128)(2,1)} %get-tuple-element.63), channel_id=1, source_target_pairs={{0,16},{16,0},{32,48},{48,32},{64,80},{80,64},{96,112},{112,96},{1... | collective-permute-start | bytes 3932168 | tf_op jit(solution)/shard_map/ppermute | solution.py:237
  181.5 1.5 copy-start.14
  181.5 1.5 copy-start.16
  183.0 91.2 %reduce-scatter.2.cloned.1.call-start = ((), (), s32[]{:S(2)}) async-start(), calls=%async_computation.10 | async-start | bytes 2949120 | tf_op jit(solution)/shard_map/reduce_scatter | solution.py:365
  183.4 20.4 %collective-permute-start.12 = (bf16[64,5120]{1,0:T(8,128)(2,1)S(1)}, bf16[64,5120]{1,0:T(8,128)(2,1)}, u32[]{:S(2)}, u32[]{:S(2)}) collective-permute-start(bf16[64,5120]{1,0:T(8,128)(2,1)S(1)} %get-tuple-element.93), channel_id=1, source_target_pairs={{0,32},{16,48},{32,64},{48,80},{64,96},{80,112},{96,0},{112,16},{1... | collective-permute-start | bytes 1966088 | tf_op jit(solution)/shard_map/ppermute | solution.py:232
  184.6 20.2 %collective-permute-start.13 = (bf16[64,5120]{1,0:T(8,128)(2,1)S(1)}, bf16[64,5120]{1,0:T(8,128)(2,1)}, u32[]{:S(2)}, u32[]{:S(2)}) collective-permute-start(bf16[64,5120]{1,0:T(8,128)(2,1)S(1)} %get-tuple-element.92), channel_id=1, source_target_pairs={{0,96},{16,112},{32,0},{48,16},{64,32},{80,48},{96,64},{112,80},{1... | collective-permute-start | bytes 1966088 | tf_op jit(solution)/shard_map/ppermute | solution.py:232
  184.9 40.5 %collective-permute-start.15 = (bf16[128,5120]{1,0:T(8,128)(2,1)}, bf16[128,5120]{1,0:T(8,128)(2,1)}, u32[]{:S(2)}, u32[]{:S(2)}) collective-permute-start(bf16[128,5120]{1,0:T(8,128)(2,1)} %get-tuple-element.74), channel_id=1, source_target_pairs={{0,16},{16,0},{32,48},{48,32},{64,80},{80,64},{96,112},{112,96},{1... | collective-permute-start | bytes 3932168 | tf_op jit(solution)/shard_map/ppermute | solution.py:237
  213.6 1.7 copy-start.4
  223.8 1.6 copy-start.10
  223.8 1.7 copy-start.12
  225.1 3.0 collective-permute-start.11
  225.5 2.7 copy-start.8
  227.5 21.4 %collective-permute-start.16 = (bf16[64,5120]{1,0:T(8,128)(2,1)S(1)}, bf16[64,5120]{1,0:T(8,128)(2,1)S(1)}, u32[]{:S(2)}, u32[]{:S(2)}) collective-permute-start(bf16[64,5120]{1,0:T(8,128)(2,1)S(1)} %get-tuple-element.90), channel_id=1, source_target_pairs={{0,96},{16,112},{32,0},{48,16},{64,32},{80,48},{96,64},{112,80},{1... | collective-permute-start | bytes 1966088 | tf_op jit(solution)/shard_map/ppermute | solution.py:232
  228.2 43.9 %copy-start.6 = (bf16[128,5120]{1,0:T(8,128)(2,1)S(1)}, bf16[128,5120]{1,0:T(8,128)(2,1)}, u32[]{:S(2)}) copy-start(bf16[128,5120]{1,0:T(8,128)(2,1)} %copy-done.5) | copy-start | bytes 3932164
  229.8 23.3 %collective-permute-start.14 = (bf16[64,5120]{1,0:T(8,128)(2,1)S(1)}, bf16[64,5120]{1,0:T(8,128)(2,1)S(1)}, u32[]{:S(2)}, u32[]{:S(2)}) collective-permute-start(bf16[64,5120]{1,0:T(8,128)(2,1)S(1)} %get-tuple-element.88), channel_id=1, source_target_pairs={{0,32},{16,48},{32,64},{48,80},{64,96},{80,112},{96,0},{112,16},{1... | collective-permute-start | bytes 1966088 | tf_op jit(solution)/shard_map/ppermute | solution.py:232
  231.0 38.9 %collective-permute-start.18 = (bf16[64,5120]{1,0:T(8,128)(2,1)S(1)}, bf16[64,5120]{1,0:T(8,128)(2,1)S(1)}, u32[]{:S(2)}, u32[]{:S(2)}) collective-permute-start(bf16[64,5120]{1,0:T(8,128)(2,1)S(1)} %get-tuple-element.91), channel_id=1, source_target_pairs={{0,96},{16,112},{32,0},{48,16},{64,32},{80,48},{96,64},{112,80},{1... | collective-permute-start | bytes 1966088 | tf_op jit(solution)/shard_map/ppermute | solution.py:232
  231.3 40.7 %collective-permute-start.17 = (bf16[64,5120]{1,0:T(8,128)(2,1)S(1)}, bf16[64,5120]{1,0:T(8,128)(2,1)S(1)}, u32[]{:S(2)}, u32[]{:S(2)}) collective-permute-start(bf16[64,5120]{1,0:T(8,128)(2,1)S(1)} %get-tuple-element.89), channel_id=1, source_target_pairs={{0,32},{16,48},{32,64},{48,80},{64,96},{80,112},{96,0},{112,16},{1... | collective-permute-start | bytes 1966088 | tf_op jit(solution)/shard_map/ppermute | solution.py:232
  303.8 2.6 copy-start.31
  306.3 1.4 copy-start.21
  306.4 1.8 copy-start.23
  (13 other events, 12.9 us)
Sparse Core Ops, SparseCore 0:
  9.1 28.4 all-gather.3
  39.3 38.5 all-gather.5
  183.1 30.4 all-gather.7
  224.0 46.9 reduce-scatter.1
where the time goes:
time: 322 us; the launch traced here: 316 us
  waiting for transfers between devices  122 us (38%)
  Pallas kernels  48.5 us (15%)
  starting transfers between devices  44.4 us (14%)
  local copies, waits for them, and re-layouts  32.6 us (10%)
  blocking collectives  26.6 us (8%)
  between operations  15.1 us (5%)
  matrix products  14 us (4%)
  other arithmetic  13.1 us (4%)
    ppermute x10, waiting for transfers between devices, ring(): lax.ppermute(value, 'dp', [(i, (i + 2 * step) % size) for i in range(size)])  56.8 us
    all_to_all x5, waiting for transfers between devices, exchange(): return lax.all_to_all(blocks, 'expert', 0, 0, tiled=True)  55.5 us
    pallas_call x4, Pallas kernels, expert_part(): pl.pallas_call(functools.partial(expert_kernel, len(blocks)), in_specs=[a...  42.6 us
    all_to_all x5, starting transfers between devices, exchange(): return lax.all_to_all(blocks, 'expert', 0, 0, tiled=True)  26.9 us
    all_to_all x1, blocking collectives, exchange(): return lax.all_to_all(blocks, 'expert', 0, 0, tiled=True)  26.6 us
    unnamed x67, local copies, waits for them, and re-layouts  16.9 us
    dot_general x13, matrix products, mm(): return jnp.dot(a, b, preferred_element_type=F32)  13.4 us
    ppermute x9, starting transfers between devices, swap(): return lax.ppermute(value, 'dp', [(i, i ^ 1) for i in range(size)])  8.93 us
  transfers between devices with their start and end apart: 28, of which 12 were waited for; matrix products, arithmetic and copies ran while one was open for 10% of the time, Pallas kernels for 15%

commit v1 on v0

--- a/solution.py
+++ b/solution.py
@@ -53,58 +53,94 @@
     return cut_columns(mm(shuffled, first).astype(BF16), size)
 
 
-def layer_kernel(at, row_cut, blocks_ref, weights_ref, out_ref, active):
-    @pl.when(pl.program_id(0) == 0)
-    def _():
-        total = blocks_ref[0].astype(F32)
-        for i in range(1, blocks_ref.shape[0]):
-            total += blocks_ref[i].astype(F32)
-        active[...] = (0.5 * total * (1.0 + lax.erf(total * (0.5**0.5)))).astype(BF16)
-
-    width = out_ref.shape[-1]
-    if row_cut:
-        rows = out_ref.shape[2]
-        part = mm(active[...], weights_ref[:, at : at + width]).astype(BF16)
-        for i in range(row_cut):
-            out_ref[i, 0] = part[i * rows : (i + 1) * rows]
-    else:
-        for i in range(out_ref.shape[0]):
-            out_ref[i] = mm(active[...], weights_ref[:, at + i * width : at + (i + 1) * width]).astype(BF16)
+def layer_kernel(at, blocks_ref, weights_ref, out_ref, active, held, sems):
+    parts, inner, width = held.shape
+
+    def columns(d):
+        rows = pl.ds(pl.multiple_of(d * inner, inner), inner)
+        return pltpu.make_async_copy(weights_ref.at[rows, pl.ds(at, width)], held.at[d], sems.at[d])
+
+    @pl.loop(0, parts)
+    def _(d):
+        columns(d).start()
+
+    total = blocks_ref[0].astype(F32)
+    for i in range(1, blocks_ref.shape[0]):
+        total += blocks_ref[i].astype(F32)
+    active[...] = (0.5 * total * (1.0 + lax.erf(total * (0.5**0.5)))).astype(BF16)
+    size, rows, cols = out_ref.shape
+
+    @pl.loop(0, parts)
+    def _(d):
+        columns(d).wait()
+        part = mm(active[...], held[d]).astype(BF16)
+        for i in range(size // parts):
+            if cols == width:
+                out_ref[i * parts + d] = part[i * rows : (i + 1) * rows]
+            else:
+                out_ref[d * (size // parts) + i] = part[:, i * cols : (i + 1) * cols]
 
 
 def layer(blocks, weights, at, width, row_cut):
     size, tokens, inner = blocks.shape
     parts = weights.shape[0] // inner
-    if row_cut:
-        shape = (row_cut, parts, tokens // row_cut, width)
-        out_spec = pl.BlockSpec((row_cut, 1, tokens // row_cut, width), lambda d: (0, d, 0, 0))
-    else:
-        shape = (size, tokens, parts * width // size)
-        out_spec = pl.BlockSpec((size // parts, tokens, parts * width // size), lambda d: (d, 0, 0))
+    shape = (size, tokens // row_cut, parts * width * row_cut // size)
     return pl.pallas_call(
-        functools.partial(layer_kernel, at, row_cut),
-        grid=(parts,),
-        in_specs=[
-            pl.BlockSpec(blocks.shape, lambda d: (0, 0, 0)),
-            pl.BlockSpec((inner, weights.shape[1]), lambda d: (d, 0)),
+        functools.partial(layer_kernel, at),
+        in_specs=[pl.BlockSpec(memory_space=pltpu.VMEM), pl.BlockSpec(memory_space=pl.ANY)],
+        out_specs=pl.BlockSpec(memory_space=pltpu.VMEM),
+        out_shape=jax.ShapeDtypeStruct(shape, BF16),
+        scratch_shapes=[
+            pltpu.VMEM((tokens, inner), BF16),
+            pltpu.VMEM((parts, inner, width), BF16),
+            pltpu.SemaphoreType.DMA((parts,)),
         ],
-        out_specs=out_spec,
-        out_shape=jax.ShapeDtypeStruct(shape, BF16),
-        scratch_shapes=[pltpu.VMEM((tokens, inner), BF16)],
-        compiler_params=pltpu.CompilerParams(dimension_semantics=("arbitrary",), vmem_limit_bytes=16 << 20),
+        compiler_params=pltpu.CompilerParams(vmem_limit_bytes=16 << 20),
         cost_estimate=pl.CostEstimate(
             flops=2 * tokens * inner * parts * width,
-            bytes_accessed=2 * weights.size + 4 * blocks.size,
+            bytes_accessed=2 * inner * parts * width + 4 * blocks.size,
             transcendentals=tokens * inner,
         ),
         name="layer",
-    )(blocks, weights)
-
-
-def token_order(blocks):
+    )(blocks, pltpu.with_memory_space_constraint(weights, pltpu.HBM))
+
+
+def visual_kernel(blocks_ref, gain_ref, router_ref, named_ref, take_ref, base_ref, visual_ref, chunk_ref):
+    size, rows, cols = blocks_ref.shape
+    halves = visual_ref.shape[0] // rows
+    across = size // halves
+    parts = [
+        jnp.concatenate([blocks_ref[r * across + c].astype(F32) for c in range(across)], axis=1)
+        for r in range(halves)
+    ]
+    wide = jnp.concatenate(parts, axis=0)
+    visual_ref[...] = wide.astype(BF16)
+    mean_square = jnp.mean(wide * wide, axis=-1, keepdims=True)
+    normed = (wide * lax.rsqrt(mean_square + EPSILON) * gain_ref[...].astype(F32)).astype(BF16)
+    logits = mm(normed, router_ref[...])
+    score = jax.nn.sigmoid(jnp.sum(named_ref[...] * logits, axis=-1, keepdims=True))
+    routed = (normed.astype(F32) * score).astype(BF16)
+    chunk_ref[...] = (base_ref[...].astype(F32) + mm(take_ref[...], routed)).astype(BF16)
+
+
+def visual_chunk(blocks, norm_gain, router, named, take, base):
     size, rows, cols = blocks.shape
-    blocks = blocks.reshape(2, size // 2, rows, cols).transpose(0, 2, 1, 3)
-    return blocks.reshape(2 * rows, size // 2 * cols)
+    feature = router.shape[0]
+    tokens = size * rows * cols // feature
+    return pl.pallas_call(
+        visual_kernel,
+        in_specs=[pl.BlockSpec(memory_space=pltpu.VMEM)] * 6,
+        out_specs=[pl.BlockSpec(memory_space=pltpu.VMEM)] * 2,
+        out_shape=[
+            jax.ShapeDtypeStruct((tokens, feature), BF16),
+            jax.ShapeDtypeStruct((take.shape[0], feature), BF16),
+        ],
+        compiler_params=pltpu.CompilerParams(vmem_limit_bytes=24 << 20),
+        cost_estimate=pl.CostEstimate(
+            flops=2 * tokens * feature * 64, bytes_accessed=8 * tokens * feature, transcendentals=tokens
+        ),
+        name="visual_chunk",
+    )(blocks, norm_gain[None, :], router, named, take, base)
 
 
 CHUNK = 1280
@@ -203,8 +239,8 @@
     return pl.pallas_call(
         functools.partial(expert_kernel, len(blocks)),
         in_specs=[anywhere] * (len(blocks) + 3),
-        out_specs=[anywhere] * len(out_rows),
-        out_shape=[jax.ShapeDtypeStruct((rows, feature), BF16) for rows in out_rows],
+        out_specs=[pl.BlockSpec(memory_space=pltpu.HBM)] * len(out_rows),
+        out_shape=[pltpu.HBM((rows, feature), BF16) for rows in out_rows],
         scratch_shapes=[
             pltpu.VMEM((count, feature), BF16),
             pltpu.VMEM((feature, width), BF16),
@@ -224,7 +260,7 @@
             transcendentals=count * width,
         ),
         name="expert_part",
-    )(*blocks, *weights)
+    )(*[pltpu.with_memory_space_constraint(block, pltpu.HBM) for block in blocks], *weights)
 
 
 def ring(value, step):
@@ -286,11 +322,13 @@
     slab = capacity * feature // row_count
     leaving = jnp.concatenate([leaving.reshape(size, slab, row_count), spare], axis=1)
     arrived = exchange(leaving)
+    pre_blocks, arrived = lax.optimization_barrier((adapter_first(patches, fc1, size), arrived))
     all_routes = arrived[:, slab, :].astype(I32).reshape(size * row_count)
-    pre_blocks, arrived = lax.optimization_barrier((adapter_first(patches, fc1, size), arrived))
     arrived = arrived[:, :slab, :].reshape(total, feature)
-    later = lax.all_gather(jnp.concatenate([fc2, proj], axis=1), "dp", axis=0, tiled=True)
-    second_blocks = layer(exchange(pre_blocks), later, 0, fc2.shape[1], 0)
+    later = lax.all_gather(
+        jnp.concatenate(after(leaving, fc2, proj), axis=1), "dp", axis=0, tiled=True
+    )
+    second_blocks = layer(exchange(pre_blocks), later, 0, fc2.shape[1], 1)
 
     mine = (all_routes == me).reshape(size, row_count)
     spots = jnp.arange(size * row_count, dtype=I32).reshape(size, row_count) - first
@@ -323,9 +361,10 @@
     below_pair, above_pair = swap(below), swap(above)
     second_blocks, mine, theirs = tie(exchange(second_blocks), mine, theirs)
     third_blocks = layer(second_blocks, later, fc2.shape[1], proj.shape[1], 2)
-    third_blocks = third_blocks.reshape(size, vis_count // 2, proj.shape[1])
-
-    below, above, below_pair, above_pair = after(third_blocks, below, above, below_pair, above_pair)
+
+    below, above, below_pair, above_pair, far_top, far_low = after(
+        third_blocks, below, above, below_pair, above_pair, far_top, far_low
+    )
     below_top, below_low, below_other, above_top, above_low, above_other = run(
         [below, below_pair, above, above_pair], (half, half, rows_a, half, half, rows_a)
     )
@@ -337,30 +376,29 @@
     visual_mine = jnp.sum(visual_blocks.astype(F32), axis=0).astype(BF16)
 
     visual_blocks = jnp.broadcast_to(visual_mine[None], (size, *visual_mine.shape))
-    far_top, far_low, far_top_pair, far_low_pair = after(
-        visual_blocks, far_top, far_low, far_top_pair, far_low_pair
-    )
-    below_too, above_too = swap(below_other), swap(above_other)
-    far_mine_top, far_mine_low, far_theirs = run(
-        [far_top, far_low, far_top_pair, far_low_pair], (half, half, rows_a)
-    )
-    from_below_low = ring(add(above_low, above_too[half:]), 1)
-    from_above_top = ring(add(below_top, below_too[:half]), -1)
+    below_too, above_too = after(visual_blocks, swap(below_other), swap(above_other))
+    to_above, to_below = add(above_low, above_too[half:]), add(below_top, below_too[:half])
+    from_below_low, from_above_top = ring(to_above, 1), ring(to_below, -1)
+    far = after(visual_blocks, far_top, far_low, far_top_pair, far_low_pair)
+    far_mine_top, far_mine_low, far_theirs = run(far, (half, half, rows_a))
+    visual_blocks, far_theirs, from_below_low, from_above_top = tie(
+        exchange(visual_blocks), far_theirs, from_below_low, from_above_top
+    )
     far_too = swap(far_theirs)
-    visual = token_order(exchange(visual_blocks))
-    visual, far_too = tie(visual, far_too)
     pass_up = ring(add(far_mine_top, far_too[:half]), 1)
     pass_down = ring(add(far_mine_low, far_too[half:]), -1)
     img_routes = lax.dynamic_slice(all_routes, (first,), (vis_count,))
-    routed_img = norm_and_gate(visual, norm_gain, router, img_routes)
+    named_img = (img_routes[:, None] == jnp.arange(experts_all, dtype=I32)[None, :]).astype(F32)
     mine_img = img_routes == me
     img_rank = earlier(mine_img[None, :])[0] + (base - rows_a)
     take = (jnp.arange(rows_b, dtype=I32)[:, None] == jnp.where(mine_img, img_rank, -1)[None, :]).astype(BF16)
-    chunk_b = (mm(pack[rows_a:], arrived) + mm(take, routed_img)).astype(BF16)
+    overflow = mm(pack[rows_a:], arrived).astype(BF16)
+    visual, chunk_b = visual_chunk(visual_blocks, norm_gain, router, named_img, take, overflow)
     gathered_b = lax.all_gather(chunk_b, "dp", axis=0, tiled=True)
-    gathered_b, pass_up, pass_down = tie(gathered_b, pass_up, pass_down)
-    from_below_top = ring(add(above_top, above_too[:half], pass_up), 1)
-    from_above_low = ring(add(below_low, below_too[half:], pass_down), -1)
+    on_above = add(above_top, above_too[:half], pass_up)
+    on_below = add(below_low, below_too[half:], pass_down)
+    gathered_b, on_above, on_below = tie(gathered_b, on_above, on_below)
+    from_below_top, from_above_low = ring(on_above, 1), ring(on_below, -1)
     (part_b,) = run([gathered_b], (gathered_b.shape[0],))
     done_b = lax.psum_scatter(part_b, "dp", scatter_dimension=0, tiled=True)
     top = add(mine[:half], mine_too[:half], from_below_top, from_above_top)

time: 322 us -> 314 us (0.975); the launches traced: 316 us -> 312 us
  blocking collectives: 26.6 us -> 0 us
  waiting for transfers between devices: 122 us -> 137 us
  local copies, waits for them, and re-layouts: 32.6 us -> 19.5 us
  other arithmetic: 13.1 us -> 21.7 us
  starting transfers between devices: 44.4 us -> 50.8 us
  Pallas kernels: 48.5 us -> 53.4 us
    all_to_all x1 -> x0, blocking collectives: 26.6 us -> none  [exchange(): return lax.all_to_all(blocks, 'expert', 0, 0, tiled=True)]
    reduce_scatter x1, waiting for transfers between devices: 0.02 us -> 13.5 us  [on_device(): done_b = lax.psum_scatter(part_b, 'dp', scatter_dimension=0, tiled=True)]
    unnamed x67 -> x55, local copies, waits for them, and re-layouts: 16.9 us -> 4.02 us
    all_gather x1, waiting for transfers between devices: 0.02 us -> 11.3 us  [adapter_first(): first = lax.all_gather(fc1, 'dp', axis=2, tiled=True)]
    ppermute x10, waiting for transfers between devices: 56.8 us -> 46 us  [ring(): lax.ppermute(value, 'dp', [(i, (i + 2 * step) % size) for i in range(size)])]
    all_to_all x5 -> x6, waiting for transfers between devices: 55.5 us -> 62.1 us  [exchange(): return lax.all_to_all(blocks, 'expert', 0, 0, tiled=True)]
    all_gather x1, waiting for transfers between devices: 8.73 us -> 3.06 us  [on_device(): gathered_b = lax.all_gather(chunk_b, 'dp', axis=0, tiled=True)]
    convert_element_type x4 -> x6, other arithmetic: 6.02 us -> 11.5 us  [add(): return total.astype(BF16)]
  transfers between devices with their start and end apart: 28 -> 29, of which waited for: 12 -> 15; matrix products, arithmetic and copies ran while one was open for 10% -> 14% of each run, Pallas kernels for 15% -> 14%
where the time goes in v1:
time: 314 us; the launch traced here: 312 us
  waiting for transfers between devices  137 us (44%)
  Pallas kernels  53.4 us (17%)
  starting transfers between devices  50.8 us (16%)
  other arithmetic  21.7 us (7%)
  local copies, waits for them, and re-layouts  19.5 us (6%)
  matrix products  15.2 us (5%)
  between operations  15 us (5%)
    all_to_all x6, waiting for transfers between devices, exchange(): return lax.all_to_all(blocks, 'expert', 0, 0, tiled=True)  62.1 us
    ppermute x10, waiting for transfers between devices, ring(): lax.ppermute(value, 'dp', [(i, (i + 2 * step) % size) for i in range(size)])  46 us
    pallas_call x4, Pallas kernels, expert_part(): pl.pallas_call(functools.partial(expert_kernel, len(blocks)), in_specs=[a...  43.4 us
    all_to_all x6, starting transfers between devices, exchange(): return lax.all_to_all(blocks, 'expert', 0, 0, tiled=True)  31 us
    reduce_scatter x1, waiting for transfers between devices, on_device(): done_b = lax.psum_scatter(part_b, 'dp', scatter_dimension=0, tiled=True)  13.5 us
    dot_general x11, matrix products, mm(): return jnp.dot(a, b, preferred_element_type=F32)  12.1 us
    convert_element_type x6, other arithmetic, add(): return total.astype(BF16)  11.5 us
    all_gather x1, waiting for transfers between devices, adapter_first(): first = lax.all_gather(fc1, 'dp', axis=2, tiled=True)  11.3 us
  transfers between devices with their start and end apart: 29, of which 15 were waited for; matrix products, arithmetic and copies ran while one was open for 14% of the time, Pallas kernels for 14%

profile of v1, /device:TPU:17, one launch (start us, length us, event | category | flops | bytes accessed | tf_op | source)
XLA Modules:
  0.0 312.4 jit_solution(18302653205738076915)
XLA Ops:
  11.7 1.7 fusion.2
  18.3 7.7 %all-to-all-start = ((bf16[16,408,128]{2,1,0:T(8,128)(2,1)}), bf16[16,408,128]{2,1,0:T(8,128)(2,1)S(1)}, u32[]{:S(2)}, u32[]{:S(2)}) async-start(bf16[16,408,128]{2,1,0:T(8,128)(2,1)} %pad_maximum_fusion), calls=%async_computation | async-start | bytes 3342336 | tf_op jit(solution)/shard_map/all_to_all | solution.py:21
  26.3 11.3 %all-gather.4.cloned.1.call-done = bf16[4,88,4096]{2,1,0:T(8,128)(2,1)} async-done(((bf16[4,88,512]{2,1,0:T(8,128)(2,1)}), bf16[4,88,4096]{2,1,0:T(8,128)(2,1)}) %all-gather.4.cloned.1.call-update) | async-done | bytes 2883600 | tf_op jit(solution)/shard_map/all_gather | solution.py:51
  37.6 2.6 convolution_convert_fusion.3
  41.3 8.9 %all-to-all-done = bf16[16,408,128]{2,1,0:T(8,128)(2,1)S(1)} async-done(((bf16[16,408,128]{2,1,0:T(8,128)(2,1)}), bf16[16,408,128]{2,1,0:T(8,128)(2,1)S(1)}, u32[]{:S(2)}, u32[]{:S(2)}) %all-to-all-start) | async-done | bytes 1671200 | tf_op jit(solution)/shard_map/all_to_all | solution.py:21
  56.6 2.4 collective-permute-start
  59.0 3.7 %all-to-all-start.1 = ((bf16[16,144,256]{2,1,0:T(8,128)(2,1)}), bf16[16,144,256]{2,1,0:T(8,128)(2,1)S(1)}, u32[]{:S(2)}, u32[]{:S(2)}) async-start(bf16[16,144,256]{2,1,0:T(8,128)(2,1)} %bitcast.51), calls=%async_computation.1 | async-start | bytes 2359296 | tf_op jit(solution)/shard_map/all_to_all | solution.py:21
  64.2 19.5 %all-to-all-done.1.blocks_ref = bf16[16,144,256]{2,1,0:T(8,128)(2,1)S(1)} async-done(((bf16[16,144,256]{2,1,0:T(8,128)(2,1)}), bf16[16,144,256]{2,1,0:T(8,128)(2,1)S(1)}, u32[]{:S(2)}, u32[]{:S(2)}) %all-to-all-start.1) | async-done | bytes 1179680 | tf_op jit(solution)/shard_map/all_to_all | solution.py:21
  83.8 3.6 %layer.2 = bf16[16,144,256]{2,1,0:T(8,128)(2,1)} custom-call(bf16[16,144,256]{2,1,0:T(8,128)(2,1)S(1)} %all-to-all-done.1.blocks_ref, bf16[2048,1152]{1,0:T(8,128)(2,1)} %all-gather.6.cloned.1.call-done.weights_ref), custom_call_target="tpu_custom_call" | custom-call | flops 301989888 | bytes 4456448 | tf_op jit(solution)/shard_map/layer/pallas_call | solution.py:88
  87.4 3.7 %all-to-all-start.2 = ((bf16[16,144,256]{2,1,0:T(8,128)(2,1)}), bf16[16,144,256]{2,1,0:T(8,128)(2,1)S(1)}, u32[]{:S(2)}, u32[]{:S(2)}) async-start(bf16[16,144,256]{2,1,0:T(8,128)(2,1)} %layer.2), calls=%async_computation.2 | async-start | bytes 2359296 | tf_op jit(solution)/shard_map/all_to_all | solution.py:21
  91.2 9.1 %expert_part.4 = (bf16[128,5120]{1,0:T(8,128)(2,1)}, bf16[128,5120]{1,0:T(8,128)(2,1)}) custom-call(bf16[128,5120]{1,0:T(8,128)(2,1)} %copy-done.4, bf16[128,5120]{1,0:T(8,128)(2,1)} %collective-permute-done.refs_1_, bf16[5120,512]{1,0:T(8,128)(2,1)} %bitcast.38, bf16[5120,512]{1,0:T(8,128)(2,1)} %bitcast.42, bf16[512,5120]{1,0:T(8,128)(2,1)} %bitcast.46), custom_call_target="tpu_custom_call" | custom-call | flops 4026531840 | bytes 20971520 | tf_op jit(solution)/shard_map/expert_part/pallas_call | solution.py:239
  101.3 2.0 slice.57
  103.2 2.0 slice.58
  106.7 2.0 all-to-all-done.2.blocks_ref
  108.7 4.0 %layer.3 = bf16[16,72,640]{2,1,0:T(8,128)(2,1)} custom-call(bf16[16,144,256]{2,1,0:T(8,128)(2,1)S(1)} %all-to-all-done.2.blocks_ref, bf16[2048,1152]{1,0:T(8,128)(2,1)} %all-gather.6.cloned.1.call-done.weights_ref), custom_call_target="tpu_custom_call" | custom-call | flops 377487360 | bytes 4980736 | tf_op jit(solution)/shard_map/layer/pallas_call | solution.py:88
  112.7 5.0 %all-to-all-start.3 = ((bf16[16,72,640]{2,1,0:T(8,128)(2,1)}), bf16[16,72,640]{2,1,0:T(8,128)(2,1)S(1)}, u32[]{:S(2)}, u32[]{:S(2)}) async-start(bf16[16,72,640]{2,1,0:T(8,128)(2,1)} %layer.3), calls=%async_computation.3 | async-start | bytes 2949120 | tf_op jit(solution)/shard_map/all_to_all | solution.py:21
  117.7 1.7 collective-permute-start.7
  119.3 2.1 collective-permute-done.6.refs_1_
  121.5 16.0 %expert_part.5 = (bf16[64,5120]{1,0:T(8,128)(2,1)}, bf16[64,5120]{1,0:T(8,128)(2,1)}, bf16[128,5120]{1,0:T(8,128)(2,1)}, bf16[64,5120]{1,0:T(8,128)(2,1)}, bf16[...) custom-call(bf16[128,5120]{1,0:T(8,128)(2,1)} %collective-permute-done.1.refs_0_, ...), custom_call_target="tpu_custom_call" | custom-call | flops 8053063680 | bytes 26214400 | tf_op jit(solution)/shard_map/expert_part/pallas_call | solution.py:239
  137.8 3.5 %collective-permute-start.10 = (bf16[128,5120]{1,0:T(8,128)(2,1)}, bf16[128,5120]{1,0:T(8,128)(2,1)}, u32[]{:S(2)}, u32[]{:S(2)}) collective-permute-start(bf16[128,5120]{1,0:T(8,128)(2,1)} %get-tuple-element.79), channel_id=1, source_target_pairs={{0,16},{16,0},{32,48},{48,32},{64,80},{80,64},{96,112},{112,96},{1... | collective-permute-start | bytes 3932168 | tf_op jit(solution)/shard_map/ppermute | solution.py:273
  141.3 1.6 copy.26.router_ref
  146.2 4.5 %all-to-all-start.4 = ((bf16[16,72,640]{2,1,0:T(8,128)(2,1)}), bf16[16,72,640]{2,1,0:T(8,128)(2,1)S(1)}, u32[]{:S(2)}, u32[]{:S(2)}) async-start(bf16[16,72,640]{2,1,0:T(8,128)(2,1)} %broadcast_in_dim.62), calls=%async_computation.4 | async-start | bytes 2949120 | tf_op jit(solution)/shard_map/all_to_all | solution.py:21
  150.8 2.3 add_convert_fusion.6
  153.1 1.5 collective-permute-start.13
  154.6 2.1 add_convert_fusion.7
  158.4 9.2 %expert_part.6 = (bf16[64,5120]{1,0:T(8,128)(2,1)}, bf16[64,5120]{1,0:T(8,128)(2,1)}, bf16[128,5120]{1,0:T(8,128)(2,1)}) custom-call(bf16[64,5120]{1,0:T(8,128)(2,1)} %collective-permute-done.5.refs_0_, bf16[64,5120]{1,0:T(8,128)(2,1)} %copy-done.8, bf16[64,5120]{1,0:T(8,128)(2,1)} %collective-permute-done.8.refs_2_, ...), custom_call_target="tpu_custom_call" | custom-call | flops 4026531840 | bytes 20971520 | tf_op jit(solution)/shard_map/expert_part/pallas_call | solution.py:239
  167.5 5.5 %all-to-all-done.4.blocks_ref = bf16[16,72,640]{2,1,0:T(8,128)(2,1)S(1)} async-done(((bf16[16,72,640]{2,1,0:T(8,128)(2,1)}), bf16[16,72,640]{2,1,0:T(8,128)(2,1)S(1)}, u32[]{:S(2)}, u32[]{:S(2)}) %all-to-all-start.4) | async-done | bytes 1474592 | tf_op jit(solution)/shard_map/all_to_all | solution.py:21
  173.8 1.6 collective-permute-start.14
  175.5 1.8 convolution_convert_fusion.2.base_ref
  177.3 2.3 visual_chunk.1
  180.9 1.9 add_convert_fusion.3
  182.7 1.5 collective-permute-start.16
  184.8 20.8 %collective-permute-done.16 = bf16[64,5120]{1,0:T(8,128)(2,1)S(1)} collective-permute-done((bf16[64,5120]{1,0:T(8,128)(2,1)S(1)}, bf16[64,5120]{1,0:T(8,128)(2,1)S(1)}, u32[]{:S(2)}, u32[]{:S(2)}) %collective-permute-start.16) | collective-permute-done | bytes 655392 | tf_op jit(solution)/shard_map/ppermute | solution.py:268
  205.6 1.4 add_convert_fusion.2
  207.0 2.8 collective-permute-done.15
  211.1 3.1 all-gather.8.cloned.1.call-done.refs_0_
  214.2 9.1 %expert_part.7 = bf16[256,5120]{1,0:T(8,128)(2,1)} custom-call(bf16[256,5120]{1,0:T(8,128)(2,1)} %all-gather.8.cloned.1.call-done.refs_0_, bf16[5120,512]{1,0:T(8,128)(2,1)} %bitcast.41, bf16[5120,512]{1,0:T(8,128)(2,1)} %bitcast.45, bf16[512,5120]{1,0:T(8,128)(2,1)} %bitcast.49), custom_call_target="tpu_custom_call" | custom-call | flops 4026531840 | bytes 20971520 | tf_op jit(solution)/shard_map/expert_part/pallas_call | solution.py:239
  225.2 17.2 %collective-permute-done.17 = bf16[64,5120]{1,0:T(8,128)(2,1)S(1)} collective-permute-done((bf16[64,5120]{1,0:T(8,128)(2,1)S(1)}, bf16[64,5120]{1,0:T(8,128)(2,1)S(1)}, u32[]{:S(2)}, u32[]{:S(2)}) %collective-permute-start.17) | collective-permute-done | bytes 655392 | tf_op jit(solution)/shard_map/ppermute | solution.py:268
  242.4 2.4 collective-permute-done.18
  244.8 2.5 add_convert_fusion.1
  247.3 13.5 %reduce-scatter.2.cloned.1.call-done = bf16[32,5120]{1,0:T(8,128)(2,1)} async-done(((bf16[256,5120]{1,0:T(8,128)(2,1)}), bf16[32,5120]{1,0:T(8,128)(2,1)}) %reduce-scatter.2.cloned.1.call-update) | async-done | bytes 327696 | tf_op jit(solution)/shard_map/reduce_scatter | solution.py:403
  260.8 1.5 fusion.20
  263.0 1.7 reshape.207
  264.7 6.4 %all-to-all-start.5 = ((bf16[16,400,128]{2,1,0:T(8,128)(2,1)}), bf16[16,400,128]{2,1,0:T(8,128)(2,1)}, u32[]{:S(2)}, u32[]{:S(2)}) async-start(bf16[16,400,128]{2,1,0:T(8,128)(2,1)} %reshape.207), calls=%async_computation.6 | async-start | bytes 3276800 | tf_op jit(solution)/shard_map/all_to_all | solution.py:21
  271.2 2.0 convolution_select_fusion
  273.2 25.9 %all-to-all-done.5 = bf16[16,400,128]{2,1,0:T(8,128)(2,1)} async-done(((bf16[16,400,128]{2,1,0:T(8,128)(2,1)}), bf16[16,400,128]{2,1,0:T(8,128)(2,1)}, u32[]{:S(2)}, u32[]{:S(2)}) %all-to-all-start.5) | async-done | bytes 1638432 | tf_op jit(solution)/shard_map/all_to_all | solution.py:21
  299.1 3.7 %reshape.208 = bf16[160,5120]{1,0:T(8,128)(2,1)} reshape(bf16[16,400,128]{2,1,0:T(8,128)(2,1)} %all-to-all-done.5) | data formatting | bytes 3276800 | tf_op jit(solution)/shard_map/reshape | solution.py:409
  302.8 3.0 fusion.1
  (140 shorter events, 31.9 us)
Async XLA Ops:
  6.5 6.8 %copy-start.26 = (s32[128,1]{0,1:T(1,128)S(1)}, s32[128,1]{0,1:T(1,128)}, u32[]{:S(2)}) copy-start(s32[128,1]{0,1:T(1,128)} %param.20) | copy-start | bytes 1540
  6.5 6.8 %copy-start.5 = (bf16[128,5120]{1,0:T(8,128)(2,1)S(1)}, bf16[128,5120]{1,0:T(8,128)(2,1)}, u32[]{:S(2)}) copy-start(bf16[128,5120]{1,0:T(8,128)(2,1)} %param.12) | copy-start | bytes 3932164
  6.5 6.9 %copy-start.16 = (bf16[5120,16]{0,1:T(8,128)(2,1)S(1)}, bf16[5120,16]{0,1:T(8,128)(2,1)}, u32[]{:S(2)}) copy-start(bf16[5120,16]{0,1:T(8,128)(2,1)} %param.19) | copy-start | bytes 491524
  6.5 31.1 %all-gather.4.cloned.1.call-start = ((), (), s32[]{:S(2)}) async-start(), calls=%async_computation.7 | async-start | bytes 3244032 | tf_op jit(solution)/shard_map/all_gather | solution.py:51
  7.3 76.5 %all-gather.6.cloned.1.call-start = ((), (), s32[]{:S(2)}) async-start(), calls=%async_computation.8 | async-start | bytes 5308416 | tf_op jit(solution)/shard_map/all_gather | solution.py:328
  18.3 7.8 %copy-start.17 = (bf16[1,24,24,88]{3,2,1,0:T(8,128)(2,1)S(1)}, bf16[1,24,24,88]{3,2,1,0:T(8,128)(2,1)}, u32[]{:S(2)}) copy-start(bf16[1,24,24,88]{3,2,1,0:T(8,128)(2,1)} %param.13) | copy-start | bytes 304132
  18.3 32.0 %all-to-all-start = ((bf16[16,408,128]{2,1,0:T(8,128)(2,1)}), bf16[16,408,128]{2,1,0:T(8,128)(2,1)S(1)}, u32[]{:S(2)}, u32[]{:S(2)}) async-start(bf16[16,408,128]{2,1,0:T(8,128)(2,1)} %pad_maximum_fusion), calls=%async_computation | async-start | bytes 3342336 | tf_op jit(solution)/shard_map/all_to_all | solution.py:21
  52.5 4.0 %copy-start.2 = (bf16[160,5120]{1,0:T(8,128)(2,1)}, bf16[160,5120]{1,0:T(8,128)(2,1)S(1)}, u32[]{:S(2)}) copy-start(bf16[160,5120]{1,0:T(8,128)(2,1)S(1)} %reshape.206) | copy-start | bytes 4915204
  56.6 30.8 %copy-start.4 = (bf16[128,5120]{1,0:T(8,128)(2,1)}, bf16[128,5120]{1,0:T(8,128)(2,1)S(1)}, u32[]{:S(2)}) copy-start(bf16[128,5120]{1,0:T(8,128)(2,1)S(1)} %convolution_convert_fusion.1.refs_0_) | copy-start | bytes 3932164
  56.6 34.6 %collective-permute-start = (bf16[128,5120]{1,0:T(8,128)(2,1)S(1)}, bf16[128,5120]{1,0:T(8,128)(2,1)}, u32[]{:S(2)}, u32[]{:S(2)}) collective-permute-start(bf16[128,5120]{1,0:T(8,128)(2,1)S(1)} %convolution_convert_fusion.1.refs_0_), channel_id=1, source_target_pairs={{0,16},{16,0},{32,48},{48,32},{64,80},{80,64},{96,112},{112,96},{1... | collective-permute-start | bytes 3932168 | tf_op jit(solution)/shard_map/ppermute | solution.py:273
  59.0 24.8 %all-to-all-start.1 = ((bf16[16,144,256]{2,1,0:T(8,128)(2,1)}), bf16[16,144,256]{2,1,0:T(8,128)(2,1)S(1)}, u32[]{:S(2)}, u32[]{:S(2)}) async-start(bf16[16,144,256]{2,1,0:T(8,128)(2,1)} %bitcast.51), calls=%async_computation.1 | async-start | bytes 2359296 | tf_op jit(solution)/shard_map/all_to_all | solution.py:21
  62.7 37.6 %collective-permute-start.2 = (bf16[128,5120]{1,0:T(8,128)(2,1)S(1)}, bf16[128,5120]{1,0:T(8,128)(2,1)}, u32[]{:S(2)}, u32[]{:S(2)}) collective-permute-start(bf16[128,5120]{1,0:T(8,128)(2,1)S(1)} %convolution_convert_fusion.1.refs_0_), channel_id=1, source_target_pairs={{0,96},{16,112},{32,0},{48,16},{64,32},{80,48},{96,64},{112,80},{1... | collective-permute-start | bytes 3932168 | tf_op jit(solution)/shard_map/ppermute | solution.py:268
  62.9 37.3 %collective-permute-start.1 = (bf16[128,5120]{1,0:T(8,128)(2,1)S(1)}, bf16[128,5120]{1,0:T(8,128)(2,1)}, u32[]{:S(2)}, u32[]{:S(2)}) collective-permute-start(bf16[128,5120]{1,0:T(8,128)(2,1)S(1)} %convolution_convert_fusion.1.refs_0_), channel_id=1, source_target_pairs={{0,32},{16,48},{32,64},{48,80},{64,96},{80,112},{96,0},{112,16},{1... | collective-permute-start | bytes 3932168 | tf_op jit(solution)/shard_map/ppermute | solution.py:268
  87.4 21.2 %all-to-all-start.2 = ((bf16[16,144,256]{2,1,0:T(8,128)(2,1)}), bf16[16,144,256]{2,1,0:T(8,128)(2,1)S(1)}, u32[]{:S(2)}, u32[]{:S(2)}) async-start(bf16[16,144,256]{2,1,0:T(8,128)(2,1)} %layer.2), calls=%async_computation.2 | async-start | bytes 2359296 | tf_op jit(solution)/shard_map/all_to_all | solution.py:21
  100.3 21.2 %collective-permute-start.3 = (bf16[128,5120]{1,0:T(8,128)(2,1)}, bf16[128,5120]{1,0:T(8,128)(2,1)}, u32[]{:S(2)}, u32[]{:S(2)}) collective-permute-start(bf16[128,5120]{1,0:T(8,128)(2,1)} %collective-permute-done.1.refs_0_), channel_id=1, source_target_pairs={{0,16},{16,0},{32,48},{48,32},{64,80},{80,64},{96,112},{112,96},{1... | collective-permute-start | bytes 3932168 | tf_op jit(solution)/shard_map/ppermute | solution.py:273
  101.2 20.3 %collective-permute-start.4 = (bf16[128,5120]{1,0:T(8,128)(2,1)}, bf16[128,5120]{1,0:T(8,128)(2,1)}, u32[]{:S(2)}, u32[]{:S(2)}) collective-permute-start(bf16[128,5120]{1,0:T(8,128)(2,1)} %collective-permute-done.2.refs_2_), channel_id=1, source_target_pairs={{0,16},{16,0},{32,48},{48,32},{64,80},{80,64},{96,112},{112,96},{1... | collective-permute-start | bytes 3932168 | tf_op jit(solution)/shard_map/ppermute | solution.py:273
  105.2 16.2 %collective-permute-start.6 = (bf16[64,5120]{1,0:T(8,128)(2,1)}, bf16[64,5120]{1,0:T(8,128)(2,1)S(1)}, u32[]{:S(2)}, u32[]{:S(2)}) collective-permute-start(bf16[64,5120]{1,0:T(8,128)(2,1)} %slice.58), channel_id=1, source_target_pairs={{0,96},{16,112},{32,0},{48,16},{64,32},{80,48},{96,64},{112,80},{1... | collective-permute-start | bytes 1966088 | tf_op jit(solution)/shard_map/ppermute | solution.py:268
  105.4 16.0 %collective-permute-start.5 = (bf16[64,5120]{1,0:T(8,128)(2,1)}, bf16[64,5120]{1,0:T(8,128)(2,1)}, u32[]{:S(2)}, u32[]{:S(2)}) collective-permute-start(bf16[64,5120]{1,0:T(8,128)(2,1)} %slice.57), channel_id=1, source_target_pairs={{0,32},{16,48},{32,64},{48,80},{64,96},{80,112},{96,0},{112,16},{1... | collective-permute-start | bytes 1966088 | tf_op jit(solution)/shard_map/ppermute | solution.py:268
  112.7 25.1 %all-to-all-start.3 = ((bf16[16,72,640]{2,1,0:T(8,128)(2,1)}), bf16[16,72,640]{2,1,0:T(8,128)(2,1)S(1)}, u32[]{:S(2)}, u32[]{:S(2)}) async-start(bf16[16,72,640]{2,1,0:T(8,128)(2,1)} %layer.3), calls=%async_computation.3 | async-start | bytes 2949120 | tf_op jit(solution)/shard_map/all_to_all | solution.py:21
  117.7 23.7 %copy-start.18 = (bf16[5120]{0:T(1024)(128)(2,1)S(1)}, bf16[5120]{0:T(1024)(128)(2,1)}, u32[]{:S(2)}) copy-start(bf16[5120]{0:T(1024)(128)(2,1)} %param.18) | copy-start | bytes 30724
  117.7 19.8 %collective-permute-start.7 = (bf16[128,5120]{1,0:T(8,128)(2,1)}, bf16[128,5120]{1,0:T(8,128)(2,1)}, u32[]{:S(2)}, u32[]{:S(2)}) collective-permute-start(bf16[128,5120]{1,0:T(8,128)(2,1)} %get-tuple-element.69), channel_id=1, source_target_pairs={{0,16},{16,0},{32,48},{48,32},{64,80},{80,64},{96,112},{112,96},{1... | collective-permute-start | bytes 3932168 | tf_op jit(solution)/shard_map/ppermute | solution.py:273
  121.4 23.3 %copy-start.8 = (bf16[64,5120]{1,0:T(8,128)(2,1)}, bf16[64,5120]{1,0:T(8,128)(2,1)S(1)}, u32[]{:S(2)}) copy-start(bf16[64,5120]{1,0:T(8,128)(2,1)S(1)} %collective-permute-done.6.refs_1_) | copy-start | bytes 1966084
  137.8 12.9 %collective-permute-start.10 = (bf16[128,5120]{1,0:T(8,128)(2,1)}, bf16[128,5120]{1,0:T(8,128)(2,1)}, u32[]{:S(2)}, u32[]{:S(2)}) collective-permute-start(bf16[128,5120]{1,0:T(8,128)(2,1)} %get-tuple-element.79), channel_id=1, source_target_pairs={{0,16},{16,0},{32,48},{48,32},{64,80},{80,64},{96,112},{112,96},{1... | collective-permute-start | bytes 3932168 | tf_op jit(solution)/shard_map/ppermute | solution.py:273
  141.3 9.4 %collective-permute-start.11 = (bf16[128,5120]{1,0:T(8,128)(2,1)}, bf16[128,5120]{1,0:T(8,128)(2,1)}, u32[]{:S(2)}, u32[]{:S(2)}) collective-permute-start(bf16[128,5120]{1,0:T(8,128)(2,1)} %get-tuple-element.80), channel_id=1, source_target_pairs={{0,16},{16,0},{32,48},{48,32},{64,80},{80,64},{96,112},{112,96},{1... | collective-permute-start | bytes 3932168 | tf_op jit(solution)/shard_map/ppermute | solution.py:273
  144.2 14.1 %collective-permute-start.8 = (bf16[64,5120]{1,0:T(8,128)(2,1)}, bf16[64,5120]{1,0:T(8,128)(2,1)}, u32[]{:S(2)}, u32[]{:S(2)}) collective-permute-start(bf16[64,5120]{1,0:T(8,128)(2,1)} %collective-permute-done.5.refs_0_), channel_id=1, source_target_pairs={{0,16},{16,0},{32,48},{48,32},{64,80},{80,64},{96,112},{112,96},{1... | collective-permute-start | bytes 1966088 | tf_op jit(solution)/shard_map/ppermute | solution.py:273
  144.8 13.6 %collective-permute-start.9 = (bf16[64,5120]{1,0:T(8,128)(2,1)S(1)}, bf16[64,5120]{1,0:T(8,128)(2,1)}, u32[]{:S(2)}, u32[]{:S(2)}) collective-permute-start(bf16[64,5120]{1,0:T(8,128)(2,1)S(1)} %collective-permute-done.6.refs_1_), channel_id=1, source_target_pairs={{0,16},{16,0},{32,48},{48,32},{64,80},{80,64},{96,112},{112,96},{1... | collective-permute-start | bytes 1966088 | tf_op jit(solution)/shard_map/ppermute | solution.py:273
  146.2 26.8 %all-to-all-start.4 = ((bf16[16,72,640]{2,1,0:T(8,128)(2,1)}), bf16[16,72,640]{2,1,0:T(8,128)(2,1)S(1)}, u32[]{:S(2)}, u32[]{:S(2)}) async-start(bf16[16,72,640]{2,1,0:T(8,128)(2,1)} %broadcast_in_dim.62), calls=%async_computation.4 | async-start | bytes 2949120 | tf_op jit(solution)/shard_map/all_to_all | solution.py:21
  150.7 63.5 %all-gather.8.cloned.1.call-start = ((), (), s32[]{:S(2)}) async-start(), calls=%async_computation.9 | async-start | bytes 2949120 | tf_op jit(solution)/shard_map/all_gather | solution.py:397
  150.7 3.9 %copy-start.11 = (bf16[64,5120]{1,0:T(8,128)(2,1)S(1)}, bf16[64,5120]{1,0:T(8,128)(2,1)}, u32[]{:S(2)}) copy-start(bf16[64,5120]{1,0:T(8,128)(2,1)} %get-tuple-element.78) | copy-start | bytes 1966084
  153.1 19.9 %collective-permute-start.13 = (bf16[64,5120]{1,0:T(8,128)(2,1)}, bf16[64,5120]{1,0:T(8,128)(2,1)}, u32[]{:S(2)}, u32[]{:S(2)}) collective-permute-start(bf16[64,5120]{1,0:T(8,128)(2,1)} %add_convert_fusion.6), channel_id=1, source_target_pairs={{0,96},{16,112},{32,0},{48,16},{64,32},{80,48},{96,64},{112,80},{1... | collective-permute-start | bytes 1966088 | tf_op jit(solution)/shard_map/ppermute | solution.py:268
  156.7 17.1 %collective-permute-start.12 = (bf16[64,5120]{1,0:T(8,128)(2,1)}, bf16[64,5120]{1,0:T(8,128)(2,1)}, u32[]{:S(2)}, u32[]{:S(2)}) collective-permute-start(bf16[64,5120]{1,0:T(8,128)(2,1)} %add_convert_fusion.7), channel_id=1, source_target_pairs={{0,32},{16,48},{32,64},{48,80},{64,96},{80,112},{96,0},{112,16},{1... | collective-permute-start | bytes 1966088 | tf_op jit(solution)/shard_map/ppermute | solution.py:268
  173.8 7.0 %collective-permute-start.14 = (bf16[128,5120]{1,0:T(8,128)(2,1)}, bf16[128,5120]{1,0:T(8,128)(2,1)}, u32[]{:S(2)}, u32[]{:S(2)}) collective-permute-start(bf16[128,5120]{1,0:T(8,128)(2,1)} %get-tuple-element.91), channel_id=1, source_target_pairs={{0,16},{16,0},{32,48},{48,32},{64,80},{80,64},{96,112},{112,96},{1... | collective-permute-start | bytes 3932168 | tf_op jit(solution)/shard_map/ppermute | solution.py:273
  177.3 3.6 %copy-start.12 = (bf16[64,5120]{1,0:T(8,128)(2,1)S(1)}, bf16[64,5120]{1,0:T(8,128)(2,1)}, u32[]{:S(2)}) copy-start(bf16[64,5120]{1,0:T(8,128)(2,1)} %get-tuple-element.90) | copy-start | bytes 1966084
  180.8 80.0 %reduce-scatter.2.cloned.1.call-start = ((), (), s32[]{:S(2)}) async-start(), calls=%async_computation.10 | async-start | bytes 2949120 | tf_op jit(solution)/shard_map/reduce_scatter | solution.py:403
  180.8 24.7 %copy-start.10 = (bf16[64,5120]{1,0:T(8,128)(2,1)S(1)}, bf16[64,5120]{1,0:T(8,128)(2,1)}, u32[]{:S(2)}) copy-start(bf16[64,5120]{1,0:T(8,128)(2,1)} %get-tuple-element.92) | copy-start | bytes 1966084
  182.7 22.8 %collective-permute-start.16 = (bf16[64,5120]{1,0:T(8,128)(2,1)S(1)}, bf16[64,5120]{1,0:T(8,128)(2,1)S(1)}, u32[]{:S(2)}, u32[]{:S(2)}) collective-permute-start(bf16[64,5120]{1,0:T(8,128)(2,1)S(1)} %get-tuple-element.108), channel_id=1, source_target_pairs={{0,96},{16,112},{32,0},{48,16},{64,32},{80,48},{96,64},{112,80},{1... | collective-permute-start | bytes 1966088 | tf_op jit(solution)/shard_map/ppermute | solution.py:268
  184.3 25.5 %collective-permute-start.15 = (bf16[64,5120]{1,0:T(8,128)(2,1)S(1)}, bf16[64,5120]{1,0:T(8,128)(2,1)S(1)}, u32[]{:S(2)}, u32[]{:S(2)}) collective-permute-start(bf16[64,5120]{1,0:T(8,128)(2,1)S(1)} %get-tuple-element.109), channel_id=1, source_target_pairs={{0,32},{16,48},{32,64},{48,80},{64,96},{80,112},{96,0},{112,16},{1... | collective-permute-start | bytes 1966088 | tf_op jit(solution)/shard_map/ppermute | solution.py:268
  205.6 4.2 %copy-start.9 = (bf16[64,5120]{1,0:T(8,128)(2,1)S(1)}, bf16[64,5120]{1,0:T(8,128)(2,1)}, u32[]{:S(2)}) copy-start(bf16[64,5120]{1,0:T(8,128)(2,1)} %get-tuple-element.89) | copy-start | bytes 1966084
  223.3 21.4 %copy-start.7 = (bf16[128,5120]{1,0:T(8,128)(2,1)S(1)}, bf16[128,5120]{1,0:T(8,128)(2,1)}, u32[]{:S(2)}) copy-start(bf16[128,5120]{1,0:T(8,128)(2,1)} %get-tuple-element.86) | copy-start | bytes 3932164
  223.4 19.0 %collective-permute-start.17 = (bf16[64,5120]{1,0:T(8,128)(2,1)S(1)}, bf16[64,5120]{1,0:T(8,128)(2,1)S(1)}, u32[]{:S(2)}, u32[]{:S(2)}) collective-permute-start(bf16[64,5120]{1,0:T(8,128)(2,1)S(1)} %add_convert_fusion.4), channel_id=1, source_target_pairs={{0,32},{16,48},{32,64},{48,80},{64,96},{80,112},{96,0},{112,16},{1... | collective-permute-start | bytes 1966088 | tf_op jit(solution)/shard_map/ppermute | solution.py:268
  224.2 20.5 %collective-permute-start.18 = (bf16[64,5120]{1,0:T(8,128)(2,1)S(1)}, bf16[64,5120]{1,0:T(8,128)(2,1)S(1)}, u32[]{:S(2)}, u32[]{:S(2)}) collective-permute-start(bf16[64,5120]{1,0:T(8,128)(2,1)S(1)} %add_convert_fusion.2), channel_id=1, source_target_pairs={{0,96},{16,112},{32,0},{48,16},{64,32},{80,48},{96,64},{112,80},{1... | collective-permute-start | bytes 1966088 | tf_op jit(solution)/shard_map/ppermute | solution.py:268
  264.7 6.4 %copy-start.1 = (bf16[144,5120]{1,0:T(8,128)(2,1)S(1)}, bf16[144,5120]{1,0:T(8,128)(2,1)}, u32[]{:S(2)}) copy-start(bf16[144,5120]{1,0:T(8,128)(2,1)} %copy-done) | copy-start | bytes 4423684
  264.7 6.5 %copy-start.6 = (bf16[128,5120]{1,0:T(8,128)(2,1)S(1)}, bf16[128,5120]{1,0:T(8,128)(2,1)}, u32[]{:S(2)}) copy-start(bf16[128,5120]{1,0:T(8,128)(2,1)} %param.12) | copy-start | bytes 3932164
  264.7 6.5 %copy-start.21 = (pred[128]{0:T(512)(128)(4,1)S(1)}, pred[128]{0:T(512)(128)(4,1)}, u32[]{:S(2)}) copy-start(pred[128]{0:T(512)(128)(4,1)} %copy-done.20) | copy-start | bytes 388
  264.7 6.5 %copy-start.23 = (s32[128]{0:T(128)S(1)}, s32[128]{0:T(128)}, u32[]{:S(2)}) copy-start(s32[128]{0:T(128)} %copy-done.22) | copy-start | bytes 1540
  264.7 34.4 %all-to-all-start.5 = ((bf16[16,400,128]{2,1,0:T(8,128)(2,1)}), bf16[16,400,128]{2,1,0:T(8,128)(2,1)}, u32[]{:S(2)}, u32[]{:S(2)}) async-start(bf16[16,400,128]{2,1,0:T(8,128)(2,1)} %reshape.207), calls=%async_computation.6 | async-start | bytes 3276800 | tf_op jit(solution)/shard_map/all_to_all | solution.py:21
  273.2 29.6 %copy-start.3 = (f32[128,5120]{1,0:T(8,128)S(1)}, f32[128,5120]{1,0:T(8,128)}, u32[]{:S(2)}) copy-start(f32[128,5120]{1,0:T(8,128)} %convolution_select_fusion) | copy-start | bytes 7864324
  273.2 29.6 %copy-start.25 = (s32[128]{0:T(128)S(1)}, s32[128]{0:T(128)}, u32[]{:S(2)}) copy-start(s32[128]{0:T(128)} %copy-done.24) | copy-start | bytes 1540
  (8 other events, 9.3 us)
Sparse Core Ops, SparseCore 0:
  9.1 28.4 all-gather.3
  39.3 40.7 all-gather.5
  180.9 33.2 all-gather.7
  223.5 37.2 reduce-scatter.1

commit v2 on v1

--- a/solution.py
+++ b/solution.py
@@ -117,7 +117,8 @@
     visual_ref[...] = wide.astype(BF16)
     mean_square = jnp.mean(wide * wide, axis=-1, keepdims=True)
     normed = (wide * lax.rsqrt(mean_square + EPSILON) * gain_ref[...].astype(F32)).astype(BF16)
-    logits = mm(normed, router_ref[...])
+    turn = (((1,), (1,)), ((), ()))
+    logits = lax.dot_general(normed, router_ref[...], turn, preferred_element_type=F32)
     score = jax.nn.sigmoid(jnp.sum(named_ref[...] * logits, axis=-1, keepdims=True))
     routed = (normed.astype(F32) * score).astype(BF16)
     chunk_ref[...] = (base_ref[...].astype(F32) + mm(take_ref[...], routed)).astype(BF16)
@@ -140,7 +141,7 @@
             flops=2 * tokens * feature * 64, bytes_accessed=8 * tokens * feature, transcendentals=tokens
         ),
         name="visual_chunk",
-    )(blocks, norm_gain[None, :], router, named, take, base)
+    )(blocks, norm_gain[None, :], router.T, named, take, base)
 
 
 CHUNK = 1280
@@ -230,7 +231,7 @@
             copy.wait()
 
 
-def expert_part(blocks, out_rows, gate_w, up_w, down_w):
+def expert_part(blocks, out_rows, gate_w, up_w, down_w, share=1):
     feature, width = gate_w.shape
     count = sum(block.shape[0] for block in blocks)
     chunks = feature // CHUNK
@@ -255,9 +256,9 @@
         ],
         compiler_params=pltpu.CompilerParams(vmem_limit_bytes=28 << 20),
         cost_estimate=pl.CostEstimate(
-            flops=6 * count * feature * width,
-            bytes_accessed=6 * feature * width + 4 * count * feature,
-            transcendentals=count * width,
+            flops=6 * count * feature * width // share,
+            bytes_accessed=(6 * feature * width + 4 * count * feature) // share,
+            transcendentals=count * width // share,
         ),
         name="expert_part",
     )(*[pltpu.with_memory_space_constraint(block, pltpu.HBM) for block in blocks], *weights)
@@ -350,12 +351,13 @@
     pack = (slots[:, None] == row_of_text[None, :]).astype(BF16)
     unpack = (row_of[:, None] == slots[None, :]).astype(BF16)
 
-    run = lambda blocks, out_rows: expert_part(blocks, out_rows, gate_w[0], up_w[0], down_w[0])
+    run = lambda blocks, out_rows, share=1: expert_part(blocks, out_rows, gate_w[0], up_w[0], down_w[0], share)
     chunk_a = mm(pack[:rows_a], arrived).astype(BF16)
+    overflow = mm(pack[rows_a:], arrived).astype(BF16)
     half = rows_a // 2
     below, above, other = ring(chunk_a, 1), ring(chunk_a, -1), swap(chunk_a)
     own, other = after(second_blocks, chunk_a, other)
-    mine, theirs = run([own, other], (rows_a, rows_a))
+    mine, theirs = run([own, other], (rows_a, rows_a), 2)
     below, above = after(theirs, below, above)
     far_top, far_low = ring(below[:half], 1), ring(above[half:], -1)
     below_pair, above_pair = swap(below), swap(above)
@@ -381,8 +383,8 @@
     from_below_low, from_above_top = ring(to_above, 1), ring(to_below, -1)
     far = after(visual_blocks, far_top, far_low, far_top_pair, far_low_pair)
     far_mine_top, far_mine_low, far_theirs = run(far, (half, half, rows_a))
-    visual_blocks, far_theirs, from_below_low, from_above_top = tie(
-        exchange(visual_blocks), far_theirs, from_below_low, from_above_top
+    visual_blocks, far_theirs, from_below_low, from_above_top, overflow = tie(
+        exchange(visual_blocks), far_theirs, from_below_low, from_above_top, overflow
     )
     far_too = swap(far_theirs)
     pass_up = ring(add(far_mine_top, far_too[:half]), 1)
@@ -392,7 +394,6 @@
     mine_img = img_routes == me
     img_rank = earlier(mine_img[None, :])[0] + (base - rows_a)
     take = (jnp.arange(rows_b, dtype=I32)[:, None] == jnp.where(mine_img, img_rank, -1)[None, :]).astype(BF16)
-    overflow = mm(pack[rows_a:], arrived).astype(BF16)
     visual, chunk_b = visual_chunk(visual_blocks, norm_gain, router, named_img, take, overflow)
     gathered_b = lax.all_gather(chunk_b, "dp", axis=0, tiled=True)
     on_above = add(above_top, above_too[:half], pass_up)

time: 314 us -> 310 us (0.987)
  waiting for transfers between devices: 137 us -> 132 us
    all_to_all x6, waiting for transfers between devices: 62.1 us -> 48.8 us  [exchange(): return lax.all_to_all(blocks, 'expert', 0, 0, tiled=True)]
    all_to_all x6, starting transfers between devices: 31 us -> 36.3 us  [exchange(): return lax.all_to_all(blocks, 'expert', 0, 0, tiled=True)]
    all_gather x1, waiting for transfers between devices: 0.01 us -> 4.57 us  [on_device(): lax.all_gather(jnp.concatenate(after(leaving, fc2, proj), axis=1), 'dp',...]
  transfers between devices with their start and end apart: 29 -> 29, of which waited for: 15 -> 18; matrix products, arithmetic and copies ran while one was open for 14% -> 13% of each run, Pallas kernels for 14% -> 14%
where the time goes in v2:
time: 310 us; the launch traced here: 309 us
  waiting for transfers between devices  132 us (43%)
  starting transfers between devices  52.7 us (17%)
  Pallas kernels  52.6 us (17%)
  local copies, waits for them, and re-layouts  21.3 us (7%)
  other arithmetic  18.9 us (6%)
  matrix products  16.4 us (5%)
  between operations  14.9 us (5%)
    all_to_all x6, waiting for transfers between devices, exchange(): return lax.all_to_all(blocks, 'expert', 0, 0, tiled=True)  48.8 us
    ppermute x10, waiting for transfers between devices, ring(): lax.ppermute(value, 'dp', [(i, (i + 2 * step) % size) for i in range(size)])  48.6 us
    pallas_call x4, Pallas kernels, expert_part(): pl.pallas_call(functools.partial(expert_kernel, len(blocks)), in_specs=[a...  43.2 us
    all_to_all x6, starting transfers between devices, exchange(): return lax.all_to_all(blocks, 'expert', 0, 0, tiled=True)  36.3 us
    dot_general x11, matrix products, mm(): return jnp.dot(a, b, preferred_element_type=F32)  13.3 us
    reduce_scatter x1, waiting for transfers between devices, on_device(): done_b = lax.psum_scatter(part_b, 'dp', scatter_dimension=0, tiled=True)  12.6 us
    all_gather x1, waiting for transfers between devices, adapter_first(): first = lax.all_gather(fc1, 'dp', axis=2, tiled=True)  12.3 us
    convert_element_type x6, other arithmetic, add(): return total.astype(BF16)  10.5 us
  transfers between devices with their start and end apart: 29, of which 18 were waited for; matrix products, arithmetic and copies ran while one was open for 13% of the time, Pallas kernels for 14%

profile of v2, /device:TPU:17, one launch (start us, length us, event | category | flops | bytes accessed | tf_op | source)
XLA Modules:
  0.0 308.6 jit_solution(17124745792658153085)
XLA Ops:
  11.1 1.7 fusion.2
  17.2 7.7 %all-to-all-start = ((bf16[16,408,128]{2,1,0:T(8,128)(2,1)}), bf16[16,408,128]{2,1,0:T(8,128)(2,1)S(1)}, u32[]{:S(2)}, u32[]{:S(2)}) async-start(bf16[16,408,128]{2,1,0:T(8,128)(2,1)} %pad_maximum_fusion), calls=%async_computation | async-start | bytes 3342336 | tf_op jit(solution)/shard_map/all_to_all | solution.py:21
  25.3 12.3 %all-gather.4.cloned.1.call-done = bf16[4,88,4096]{2,1,0:T(8,128)(2,1)} async-done(((bf16[4,88,512]{2,1,0:T(8,128)(2,1)}), bf16[4,88,4096]{2,1,0:T(8,128)(2,1)}) %all-gather.4.cloned.1.call-update) | async-done | bytes 2883600 | tf_op jit(solution)/shard_map/all_gather | solution.py:51
  37.6 2.6 convolution_convert_fusion.3
  41.3 7.9 %all-to-all-done = bf16[16,408,128]{2,1,0:T(8,128)(2,1)S(1)} async-done(((bf16[16,408,128]{2,1,0:T(8,128)(2,1)}), bf16[16,408,128]{2,1,0:T(8,128)(2,1)S(1)}, u32[]{:S(2)}, u32[]{:S(2)}) %all-to-all-start) | async-done | bytes 1671200 | tf_op jit(solution)/shard_map/all_to_all | solution.py:21
  50.5 1.4 copy.22
  51.9 4.7 %all-to-all-start.1 = ((bf16[16,144,256]{2,1,0:T(8,128)(2,1)}), bf16[16,144,256]{2,1,0:T(8,128)(2,1)S(1)}, u32[]{:S(2)}, u32[]{:S(2)}) async-start(bf16[16,144,256]{2,1,0:T(8,128)(2,1)} %bitcast.53), calls=%async_computation.1 | async-start | bytes 2359296 | tf_op jit(solution)/shard_map/all_to_all | solution.py:21
  56.6 1.7 reshape.206
  61.2 2.0 convolution_convert_fusion.1.refs_0_
  63.2 1.6 collective-permute-start
  66.3 7.2 %all-to-all-done.1.blocks_ref = bf16[16,144,256]{2,1,0:T(8,128)(2,1)S(1)} async-done(((bf16[16,144,256]{2,1,0:T(8,128)(2,1)}), bf16[16,144,256]{2,1,0:T(8,128)(2,1)S(1)}, u32[]{:S(2)}, u32[]{:S(2)}) %all-to-all-start.1) | async-done | bytes 1179680 | tf_op jit(solution)/shard_map/all_to_all | solution.py:21
  73.5 4.6 %all-gather.6.cloned.1.call-done.weights_ref = bf16[2048,1152]{1,0:T(8,128)(2,1)} async-done(((bf16[256,1152]{1,0:T(8,128)(2,1)}), bf16[2048,1152]{1,0:T(8,128)(2,1)}) %all-gather.6.cloned.1.call-update) | async-done | bytes 4718608 | tf_op jit(solution)/shard_map/all_gather | solution.py:329
  78.0 3.6 %layer.2 = bf16[16,144,256]{2,1,0:T(8,128)(2,1)} custom-call(bf16[16,144,256]{2,1,0:T(8,128)(2,1)S(1)} %all-to-all-done.1.blocks_ref, bf16[2048,1152]{1,0:T(8,128)(2,1)} %all-gather.6.cloned.1.call-done.weights_ref), custom_call_target="tpu_custom_call" | custom-call | flops 301989888 | bytes 4456448 | tf_op jit(solution)/shard_map/layer/pallas_call | solution.py:88
  81.7 6.5 %all-to-all-start.2 = ((bf16[16,144,256]{2,1,0:T(8,128)(2,1)}), bf16[16,144,256]{2,1,0:T(8,128)(2,1)S(1)}, u32[]{:S(2)}, u32[]{:S(2)}) async-start(bf16[16,144,256]{2,1,0:T(8,128)(2,1)} %layer.2), calls=%async_computation.2 | async-start | bytes 2359296 | tf_op jit(solution)/shard_map/all_to_all | solution.py:21
  88.1 9.1 %expert_part.4 = (bf16[128,5120]{1,0:T(8,128)(2,1)}, bf16[128,5120]{1,0:T(8,128)(2,1)}) custom-call(bf16[128,5120]{1,0:T(8,128)(2,1)} %copy-done.5, bf16[128,5120]{1,0:T(8,128)(2,1)} %collective-permute-done.refs_1_, bf16[5120,512]{1,0:T(8,128)(2,1)} %bitcast.40, bf16[5120,512]{1,0:T(8,128)(2,1)} %bitcast.44, bf16[512,5120]{1,0:T(8,128)(2,1)} %bitcast.48), custom_call_target="tpu_custom_call" | custom-call | flops 2013265920 | bytes 10485760 | tf_op jit(solution)/shard_map/expert_part/pallas_call | solution.py:240
  97.3 2.6 collective-permute-done.2.refs_2_
  100.5 2.0 slice.57
  102.5 2.0 slice.58
  106.6 4.1 %layer.3 = bf16[16,72,640]{2,1,0:T(8,128)(2,1)} custom-call(bf16[16,144,256]{2,1,0:T(8,128)(2,1)S(1)} %all-to-all-done.2.blocks_ref, bf16[2048,1152]{1,0:T(8,128)(2,1)} %all-gather.6.cloned.1.call-done.weights_ref), custom_call_target="tpu_custom_call" | custom-call | flops 377487360 | bytes 4980736 | tf_op jit(solution)/shard_map/layer/pallas_call | solution.py:88
  110.6 6.0 %all-to-all-start.3 = ((bf16[16,72,640]{2,1,0:T(8,128)(2,1)}), bf16[16,72,640]{2,1,0:T(8,128)(2,1)S(1)}, u32[]{:S(2)}, u32[]{:S(2)}) async-start(bf16[16,72,640]{2,1,0:T(8,128)(2,1)} %layer.3), calls=%async_computation.3 | async-start | bytes 2949120 | tf_op jit(solution)/shard_map/all_to_all | solution.py:21
  116.7 1.4 collective-permute-start.7
  118.1 2.4 collective-permute-done.6.refs_1_
  120.8 15.8 %expert_part.5 = (bf16[64,5120]{1,0:T(8,128)(2,1)}, bf16[64,5120]{1,0:T(8,128)(2,1)}, bf16[128,5120]{1,0:T(8,128)(2,1)}, bf16[64,5120]{1,0:T(8,128)(2,1)}, bf16[...) custom-call(bf16[128,5120]{1,0:T(8,128)(2,1)} %collective-permute-done.1.refs_0_, ...), custom_call_target="tpu_custom_call" | custom-call | flops 8053063680 | bytes 26214400 | tf_op jit(solution)/shard_map/expert_part/pallas_call | solution.py:240
  137.7 2.6 collective-permute-start.10
  142.5 5.7 %all-to-all-start.4 = ((bf16[16,72,640]{2,1,0:T(8,128)(2,1)}), bf16[16,72,640]{2,1,0:T(8,128)(2,1)S(1)}, u32[]{:S(2)}, u32[]{:S(2)}) async-start(bf16[16,72,640]{2,1,0:T(8,128)(2,1)} %broadcast_in_dim.62), calls=%async_computation.4 | async-start | bytes 2949120 | tf_op jit(solution)/shard_map/all_to_all | solution.py:21
  148.3 2.8 add_convert_fusion.6
  154.6 9.2 %expert_part.6 = (bf16[64,5120]{1,0:T(8,128)(2,1)}, bf16[64,5120]{1,0:T(8,128)(2,1)}, bf16[128,5120]{1,0:T(8,128)(2,1)}) custom-call(bf16[64,5120]{1,0:T(8,128)(2,1)} %collective-permute-done.5.refs_0_, bf16[64,5120]{1,0:T(8,128)(2,1)} %collective-permute-done.6.refs_1_, bf16[64,5120]{1,0:T(8,128)(2,1)} %collective-permute-done.8.refs_2_, ...), custom_call_target="tpu_custom_call" | custom-call | flops 4026531840 | bytes 20971520 | tf_op jit(solution)/shard_map/expert_part/pallas_call | solution.py:240
  163.8 6.8 %all-to-all-done.4.blocks_ref = bf16[16,72,640]{2,1,0:T(8,128)(2,1)S(1)} async-done(((bf16[16,72,640]{2,1,0:T(8,128)(2,1)}), bf16[16,72,640]{2,1,0:T(8,128)(2,1)S(1)}, u32[]{:S(2)}, u32[]{:S(2)}) %all-to-all-start.4) | async-done | bytes 1474592 | tf_op jit(solution)/shard_map/all_to_all | solution.py:21
  170.6 2.0 collective-permute-start.14
  172.9 1.8 visual_chunk.1
  175.6 2.1 add_convert_fusion.3
  179.2 20.9 %collective-permute-done.16 = bf16[64,5120]{1,0:T(8,128)(2,1)S(1)} collective-permute-done((bf16[64,5120]{1,0:T(8,128)(2,1)S(1)}, bf16[64,5120]{1,0:T(8,128)(2,1)S(1)}, u32[]{:S(2)}, u32[]{:S(2)}) %collective-permute-start.16) | collective-permute-done | bytes 655392 | tf_op jit(solution)/shard_map/ppermute | solution.py:269
  200.1 1.5 add_convert_fusion.2
  201.6 2.3 collective-permute-done.15
  204.1 4.1 %all-gather.8.cloned.1.call-done.refs_0_ = bf16[256,5120]{1,0:T(8,128)(2,1)} async-done(((bf16[32,5120]{1,0:T(8,128)(2,1)}), bf16[256,5120]{1,0:T(8,128)(2,1)}) %all-gather.8.cloned.1.call-update) | async-done | bytes 2621456 | tf_op jit(solution)/shard_map/all_gather | solution.py:398
  208.2 9.1 %expert_part.7 = bf16[256,5120]{1,0:T(8,128)(2,1)} custom-call(bf16[256,5120]{1,0:T(8,128)(2,1)} %all-gather.8.cloned.1.call-done.refs_0_, bf16[5120,512]{1,0:T(8,128)(2,1)} %bitcast.43, bf16[5120,512]{1,0:T(8,128)(2,1)} %bitcast.47, bf16[512,5120]{1,0:T(8,128)(2,1)} %bitcast.51), custom_call_target="tpu_custom_call" | custom-call | flops 4026531840 | bytes 20971520 | tf_op jit(solution)/shard_map/expert_part/pallas_call | solution.py:240
  219.0 17.9 %collective-permute-done.17 = bf16[64,5120]{1,0:T(8,128)(2,1)S(1)} collective-permute-done((bf16[64,5120]{1,0:T(8,128)(2,1)S(1)}, bf16[64,5120]{1,0:T(8,128)(2,1)S(1)}, u32[]{:S(2)}, u32[]{:S(2)}) %collective-permute-start.17) | collective-permute-done | bytes 655392 | tf_op jit(solution)/shard_map/ppermute | solution.py:269
  236.8 2.2 collective-permute-done.18
  239.0 2.9 add_convert_fusion.1
  241.9 12.6 %reduce-scatter.2.cloned.1.call-done = bf16[32,5120]{1,0:T(8,128)(2,1)} async-done(((bf16[256,5120]{1,0:T(8,128)(2,1)}), bf16[32,5120]{1,0:T(8,128)(2,1)}) %reduce-scatter.2.cloned.1.call-update) | async-done | bytes 327696 | tf_op jit(solution)/shard_map/reduce_scatter | solution.py:404
  254.5 1.5 fusion.20
  256.1 1.8 fusion
  257.9 3.7 %reshape.207 = bf16[16,400,128]{2,1,0:T(8,128)(2,1)} reshape(bf16[160,5120]{1,0:T(8,128)(2,1)} %fusion) | data formatting | bytes 3276800 | tf_op jit(solution)/shard_map/reshape | solution.py:410
  261.6 5.6 %all-to-all-start.5 = ((bf16[16,400,128]{2,1,0:T(8,128)(2,1)}), bf16[16,400,128]{2,1,0:T(8,128)(2,1)}, u32[]{:S(2)}, u32[]{:S(2)}) async-start(bf16[16,400,128]{2,1,0:T(8,128)(2,1)} %reshape.207), calls=%async_computation.6 | async-start | bytes 3276800 | tf_op jit(solution)/shard_map/all_to_all | solution.py:21
  267.3 2.0 convolution_select_fusion
  269.3 26.0 %all-to-all-done.5 = bf16[16,400,128]{2,1,0:T(8,128)(2,1)} async-done(((bf16[16,400,128]{2,1,0:T(8,128)(2,1)}), bf16[16,400,128]{2,1,0:T(8,128)(2,1)}, u32[]{:S(2)}, u32[]{:S(2)}) %all-to-all-start.5) | async-done | bytes 1638432 | tf_op jit(solution)/shard_map/all_to_all | solution.py:21
  295.3 3.7 %reshape.208 = bf16[160,5120]{1,0:T(8,128)(2,1)} reshape(bf16[16,400,128]{2,1,0:T(8,128)(2,1)} %all-to-all-done.5) | data formatting | bytes 3276800 | tf_op jit(solution)/shard_map/reshape | solution.py:410
  299.1 3.0 fusion.1
  (124 shorter events, 28.9 us)
Async XLA Ops:
  6.5 6.3 %copy-start.18 = (s32[128,1]{0,1:T(1,128)S(1)}, s32[128,1]{0,1:T(1,128)}, u32[]{:S(2)}) copy-start(s32[128,1]{0,1:T(1,128)} %param.20) | copy-start | bytes 1540
  6.5 6.3 %copy-start.6 = (bf16[128,5120]{1,0:T(8,128)(2,1)S(1)}, bf16[128,5120]{1,0:T(8,128)(2,1)}, u32[]{:S(2)}) copy-start(bf16[128,5120]{1,0:T(8,128)(2,1)} %param.12) | copy-start | bytes 3932164
  6.5 6.3 %copy-start.1 = (bf16[5120,16]{0,1:T(8,128)(2,1)S(1)}, bf16[5120,16]{0,1:T(8,128)(2,1)}, u32[]{:S(2)}) copy-start(bf16[5120,16]{0,1:T(8,128)(2,1)} %param.19) | copy-start | bytes 491524
  6.5 31.1 %all-gather.4.cloned.1.call-start = ((), (), s32[]{:S(2)}) async-start(), calls=%async_computation.7 | async-start | bytes 3244032 | tf_op jit(solution)/shard_map/all_gather | solution.py:51
  7.3 70.8 %all-gather.6.cloned.1.call-start = ((), (), s32[]{:S(2)}) async-start(), calls=%async_computation.8 | async-start | bytes 5308416 | tf_op jit(solution)/shard_map/all_gather | solution.py:329
  14.9 1.4 copy-start.14
  15.0 1.4 copy-start.15
  17.2 7.8 %copy-start.16 = (bf16[1,24,24,88]{3,2,1,0:T(8,128)(2,1)S(1)}, bf16[1,24,24,88]{3,2,1,0:T(8,128)(2,1)}, u32[]{:S(2)}) copy-start(bf16[1,24,24,88]{3,2,1,0:T(8,128)(2,1)} %param.13) | copy-start | bytes 304132
  17.2 32.0 %all-to-all-start = ((bf16[16,408,128]{2,1,0:T(8,128)(2,1)}), bf16[16,408,128]{2,1,0:T(8,128)(2,1)S(1)}, u32[]{:S(2)}, u32[]{:S(2)}) async-start(bf16[16,408,128]{2,1,0:T(8,128)(2,1)} %pad_maximum_fusion), calls=%async_computation | async-start | bytes 3342336 | tf_op jit(solution)/shard_map/all_to_all | solution.py:21
  49.2 1.2 copy-start.2
  51.9 4.7 %slice-start = ((bf16[16,408,128]{2,1,0:T(8,128)(2,1)}), bf16[16,400,128]{2,1,0:T(8,128)(2,1)S(1)}, s32[]{:S(2)}) async-start(bf16[16,408,128]{2,1,0:T(8,128)(2,1)} %copy-done.2), calls=%async_computation.11 | async-start | bytes 3276800 | tf_op jit(solution)/shard_map/slice | solution.py:328
  51.9 21.5 %all-to-all-start.1 = ((bf16[16,144,256]{2,1,0:T(8,128)(2,1)}), bf16[16,144,256]{2,1,0:T(8,128)(2,1)S(1)}, u32[]{:S(2)}, u32[]{:S(2)}) async-start(bf16[16,144,256]{2,1,0:T(8,128)(2,1)} %bitcast.53), calls=%async_computation.1 | async-start | bytes 2359296 | tf_op jit(solution)/shard_map/all_to_all | solution.py:21
  63.2 18.4 %copy-start.5 = (bf16[128,5120]{1,0:T(8,128)(2,1)}, bf16[128,5120]{1,0:T(8,128)(2,1)S(1)}, u32[]{:S(2)}) copy-start(bf16[128,5120]{1,0:T(8,128)(2,1)S(1)} %convolution_convert_fusion.1.refs_0_) | copy-start | bytes 3932164
  63.2 24.9 %collective-permute-start = (bf16[128,5120]{1,0:T(8,128)(2,1)S(1)}, bf16[128,5120]{1,0:T(8,128)(2,1)}, u32[]{:S(2)}, u32[]{:S(2)}) collective-permute-start(bf16[128,5120]{1,0:T(8,128)(2,1)S(1)} %convolution_convert_fusion.1.refs_0_), channel_id=1, source_target_pairs={{0,16},{16,0},{32,48},{48,32},{64,80},{80,64},{96,112},{112,96},{1... | collective-permute-start | bytes 3932168 | tf_op jit(solution)/shard_map/ppermute | solution.py:274
  64.8 35.1 %collective-permute-start.2 = (bf16[128,5120]{1,0:T(8,128)(2,1)S(1)}, bf16[128,5120]{1,0:T(8,128)(2,1)}, u32[]{:S(2)}, u32[]{:S(2)}) collective-permute-start(bf16[128,5120]{1,0:T(8,128)(2,1)S(1)} %convolution_convert_fusion.1.refs_0_), channel_id=1, source_target_pairs={{0,96},{16,112},{32,0},{48,16},{64,32},{80,48},{96,64},{112,80},{1... | collective-permute-start | bytes 3932168 | tf_op jit(solution)/shard_map/ppermute | solution.py:269
  65.0 34.9 %collective-permute-start.1 = (bf16[128,5120]{1,0:T(8,128)(2,1)S(1)}, bf16[128,5120]{1,0:T(8,128)(2,1)}, u32[]{:S(2)}, u32[]{:S(2)}) collective-permute-start(bf16[128,5120]{1,0:T(8,128)(2,1)S(1)} %convolution_convert_fusion.1.refs_0_), channel_id=1, source_target_pairs={{0,32},{16,48},{32,64},{48,80},{64,96},{80,112},{96,0},{112,16},{1... | collective-permute-start | bytes 3932168 | tf_op jit(solution)/shard_map/ppermute | solution.py:269
  81.7 24.9 %all-to-all-start.2 = ((bf16[16,144,256]{2,1,0:T(8,128)(2,1)}), bf16[16,144,256]{2,1,0:T(8,128)(2,1)S(1)}, u32[]{:S(2)}, u32[]{:S(2)}) async-start(bf16[16,144,256]{2,1,0:T(8,128)(2,1)} %layer.2), calls=%async_computation.2 | async-start | bytes 2359296 | tf_op jit(solution)/shard_map/all_to_all | solution.py:21
  99.9 20.8 %collective-permute-start.3 = (bf16[128,5120]{1,0:T(8,128)(2,1)}, bf16[128,5120]{1,0:T(8,128)(2,1)}, u32[]{:S(2)}, u32[]{:S(2)}) collective-permute-start(bf16[128,5120]{1,0:T(8,128)(2,1)} %collective-permute-done.1.refs_0_), channel_id=1, source_target_pairs={{0,16},{16,0},{32,48},{48,32},{64,80},{80,64},{96,112},{112,96},{1... | collective-permute-start | bytes 3932168 | tf_op jit(solution)/shard_map/ppermute | solution.py:274
  100.5 20.3 %collective-permute-start.4 = (bf16[128,5120]{1,0:T(8,128)(2,1)}, bf16[128,5120]{1,0:T(8,128)(2,1)}, u32[]{:S(2)}, u32[]{:S(2)}) collective-permute-start(bf16[128,5120]{1,0:T(8,128)(2,1)} %collective-permute-done.2.refs_2_), channel_id=1, source_target_pairs={{0,16},{16,0},{32,48},{48,32},{64,80},{80,64},{96,112},{112,96},{1... | collective-permute-start | bytes 3932168 | tf_op jit(solution)/shard_map/ppermute | solution.py:274
  104.4 16.1 %collective-permute-start.6 = (bf16[64,5120]{1,0:T(8,128)(2,1)}, bf16[64,5120]{1,0:T(8,128)(2,1)}, u32[]{:S(2)}, u32[]{:S(2)}) collective-permute-start(bf16[64,5120]{1,0:T(8,128)(2,1)} %slice.58), channel_id=1, source_target_pairs={{0,96},{16,112},{32,0},{48,16},{64,32},{80,48},{96,64},{112,80},{1... | collective-permute-start | bytes 1966088 | tf_op jit(solution)/shard_map/ppermute | solution.py:269
  105.0 15.8 %collective-permute-start.5 = (bf16[64,5120]{1,0:T(8,128)(2,1)}, bf16[64,5120]{1,0:T(8,128)(2,1)}, u32[]{:S(2)}, u32[]{:S(2)}) collective-permute-start(bf16[64,5120]{1,0:T(8,128)(2,1)} %slice.57), channel_id=1, source_target_pairs={{0,32},{16,48},{32,64},{48,80},{64,96},{80,112},{96,0},{112,16},{1... | collective-permute-start | bytes 1966088 | tf_op jit(solution)/shard_map/ppermute | solution.py:269
  110.6 26.2 %all-to-all-start.3 = ((bf16[16,72,640]{2,1,0:T(8,128)(2,1)}), bf16[16,72,640]{2,1,0:T(8,128)(2,1)S(1)}, u32[]{:S(2)}, u32[]{:S(2)}) async-start(bf16[16,72,640]{2,1,0:T(8,128)(2,1)} %layer.3), calls=%async_computation.3 | async-start | bytes 2949120 | tf_op jit(solution)/shard_map/all_to_all | solution.py:21
  116.7 23.7 %copy-start.17 = (bf16[5120]{0:T(1024)(128)(2,1)S(1)}, bf16[5120]{0:T(1024)(128)(2,1)}, u32[]{:S(2)}) copy-start(bf16[5120]{0:T(1024)(128)(2,1)} %param.18) | copy-start | bytes 30724
  116.7 19.9 %collective-permute-start.7 = (bf16[128,5120]{1,0:T(8,128)(2,1)}, bf16[128,5120]{1,0:T(8,128)(2,1)S(1)}, u32[]{:S(2)}, u32[]{:S(2)}) collective-permute-start(bf16[128,5120]{1,0:T(8,128)(2,1)} %get-tuple-element.70), channel_id=1, source_target_pairs={{0,16},{16,0},{32,48},{48,32},{64,80},{80,64},{96,112},{112,96},{1... | collective-permute-start | bytes 3932168 | tf_op jit(solution)/shard_map/ppermute | solution.py:274
  136.6 1.1 copy-start.10
  137.7 10.6 %collective-permute-start.10 = (bf16[128,5120]{1,0:T(8,128)(2,1)}, bf16[128,5120]{1,0:T(8,128)(2,1)}, u32[]{:S(2)}, u32[]{:S(2)}) collective-permute-start(bf16[128,5120]{1,0:T(8,128)(2,1)} %get-tuple-element.80), channel_id=1, source_target_pairs={{0,16},{16,0},{32,48},{48,32},{64,80},{80,64},{96,112},{112,96},{1... | collective-permute-start | bytes 3932168 | tf_op jit(solution)/shard_map/ppermute | solution.py:274
  140.3 8.0 %collective-permute-start.11 = (bf16[128,5120]{1,0:T(8,128)(2,1)}, bf16[128,5120]{1,0:T(8,128)(2,1)S(1)}, u32[]{:S(2)}, u32[]{:S(2)}) collective-permute-start(bf16[128,5120]{1,0:T(8,128)(2,1)} %get-tuple-element.81), channel_id=1, source_target_pairs={{0,16},{16,0},{32,48},{48,32},{64,80},{80,64},{96,112},{112,96},{1... | collective-permute-start | bytes 3932168 | tf_op jit(solution)/shard_map/ppermute | solution.py:274
  140.3 14.3 %collective-permute-start.8 = (bf16[64,5120]{1,0:T(8,128)(2,1)}, bf16[64,5120]{1,0:T(8,128)(2,1)}, u32[]{:S(2)}, u32[]{:S(2)}) collective-permute-start(bf16[64,5120]{1,0:T(8,128)(2,1)} %collective-permute-done.5.refs_0_), channel_id=1, source_target_pairs={{0,16},{16,0},{32,48},{48,32},{64,80},{80,64},{96,112},{112,96},{1... | collective-permute-start | bytes 1966088 | tf_op jit(solution)/shard_map/ppermute | solution.py:274
  140.9 13.7 %collective-permute-start.9 = (bf16[64,5120]{1,0:T(8,128)(2,1)}, bf16[64,5120]{1,0:T(8,128)(2,1)}, u32[]{:S(2)}, u32[]{:S(2)}) collective-permute-start(bf16[64,5120]{1,0:T(8,128)(2,1)} %collective-permute-done.6.refs_1_), channel_id=1, source_target_pairs={{0,16},{16,0},{32,48},{48,32},{64,80},{80,64},{96,112},{112,96},{1... | collective-permute-start | bytes 1966088 | tf_op jit(solution)/shard_map/ppermute | solution.py:274
  142.5 28.1 %all-to-all-start.4 = ((bf16[16,72,640]{2,1,0:T(8,128)(2,1)}), bf16[16,72,640]{2,1,0:T(8,128)(2,1)S(1)}, u32[]{:S(2)}, u32[]{:S(2)}) async-start(bf16[16,72,640]{2,1,0:T(8,128)(2,1)} %broadcast_in_dim.62), calls=%async_computation.4 | async-start | bytes 2949120 | tf_op jit(solution)/shard_map/all_to_all | solution.py:21
  148.2 60.0 %all-gather.8.cloned.1.call-start = ((), (), s32[]{:S(2)}) async-start(), calls=%async_computation.9 | async-start | bytes 2949120 | tf_op jit(solution)/shard_map/all_gather | solution.py:398
  148.3 4.0 %copy-start.13 = (bf16[64,5120]{1,0:T(8,128)(2,1)S(1)}, bf16[64,5120]{1,0:T(8,128)(2,1)}, u32[]{:S(2)}) copy-start(bf16[64,5120]{1,0:T(8,128)(2,1)} %get-tuple-element.79) | copy-start | bytes 1966084
  148.3 5.0 %copy-start.8 = (bf16[128,5120]{1,0:T(8,128)(2,1)}, bf16[128,5120]{1,0:T(8,128)(2,1)S(1)}, u32[]{:S(2)}) copy-start(bf16[128,5120]{1,0:T(8,128)(2,1)S(1)} %collective-permute-done.11) | copy-start | bytes 3932164
  151.1 3.2 %copy-start.3 = (bf16[160,5120]{1,0:T(8,128)(2,1)S(1)}, bf16[160,5120]{1,0:T(8,128)(2,1)}, u32[]{:S(2)}) copy-start(bf16[160,5120]{1,0:T(8,128)(2,1)} %reshape.206) | copy-start | bytes 4915204
  151.1 19.5 %collective-permute-start.13 = (bf16[64,5120]{1,0:T(8,128)(2,1)}, bf16[64,5120]{1,0:T(8,128)(2,1)}, u32[]{:S(2)}, u32[]{:S(2)}) collective-permute-start(bf16[64,5120]{1,0:T(8,128)(2,1)} %add_convert_fusion.6), channel_id=1, source_target_pairs={{0,96},{16,112},{32,0},{48,16},{64,32},{80,48},{96,64},{112,80},{1... | collective-permute-start | bytes 1966088 | tf_op jit(solution)/shard_map/ppermute | solution.py:269
  153.3 17.3 %collective-permute-start.12 = (bf16[64,5120]{1,0:T(8,128)(2,1)}, bf16[64,5120]{1,0:T(8,128)(2,1)}, u32[]{:S(2)}, u32[]{:S(2)}) collective-permute-start(bf16[64,5120]{1,0:T(8,128)(2,1)} %add_convert_fusion.7), channel_id=1, source_target_pairs={{0,32},{16,48},{32,64},{48,80},{64,96},{80,112},{96,0},{112,16},{1... | collective-permute-start | bytes 1966088 | tf_op jit(solution)/shard_map/ppermute | solution.py:269
  170.6 5.0 %collective-permute-start.14 = (bf16[128,5120]{1,0:T(8,128)(2,1)}, bf16[128,5120]{1,0:T(8,128)(2,1)}, u32[]{:S(2)}, u32[]{:S(2)}) collective-permute-start(bf16[128,5120]{1,0:T(8,128)(2,1)} %get-tuple-element.93), channel_id=1, source_target_pairs={{0,16},{16,0},{32,48},{48,32},{64,80},{80,64},{96,112},{112,96},{1... | collective-permute-start | bytes 3932168 | tf_op jit(solution)/shard_map/ppermute | solution.py:274
  175.5 79.1 %reduce-scatter.2.cloned.1.call-start = ((), (), s32[]{:S(2)}) async-start(), calls=%async_computation.10 | async-start | bytes 2949120 | tf_op jit(solution)/shard_map/reduce_scatter | solution.py:404
  175.6 24.5 %copy-start.12 = (bf16[64,5120]{1,0:T(8,128)(2,1)S(1)}, bf16[64,5120]{1,0:T(8,128)(2,1)}, u32[]{:S(2)}) copy-start(bf16[64,5120]{1,0:T(8,128)(2,1)} %get-tuple-element.94) | copy-start | bytes 1966084
  177.6 22.4 %collective-permute-start.16 = (bf16[64,5120]{1,0:T(8,128)(2,1)S(1)}, bf16[64,5120]{1,0:T(8,128)(2,1)S(1)}, u32[]{:S(2)}, u32[]{:S(2)}) collective-permute-start(bf16[64,5120]{1,0:T(8,128)(2,1)S(1)} %get-tuple-element.110), channel_id=1, source_target_pairs={{0,96},{16,112},{32,0},{48,16},{64,32},{80,48},{96,64},{112,80},{1... | collective-permute-start | bytes 1966088 | tf_op jit(solution)/shard_map/ppermute | solution.py:269
  178.9 25.0 %collective-permute-start.15 = (bf16[64,5120]{1,0:T(8,128)(2,1)S(1)}, bf16[64,5120]{1,0:T(8,128)(2,1)S(1)}, u32[]{:S(2)}, u32[]{:S(2)}) collective-permute-start(bf16[64,5120]{1,0:T(8,128)(2,1)S(1)} %get-tuple-element.111), channel_id=1, source_target_pairs={{0,32},{16,48},{32,64},{48,80},{64,96},{80,112},{96,0},{112,16},{1... | collective-permute-start | bytes 1966088 | tf_op jit(solution)/shard_map/ppermute | solution.py:269
  200.1 3.8 %copy-start.9 = (bf16[128,5120]{1,0:T(8,128)(2,1)S(1)}, bf16[128,5120]{1,0:T(8,128)(2,1)}, u32[]{:S(2)}) copy-start(bf16[128,5120]{1,0:T(8,128)(2,1)} %copy-done.8) | copy-start | bytes 3932164
  200.1 3.8 %copy-start.11 = (bf16[64,5120]{1,0:T(8,128)(2,1)S(1)}, bf16[64,5120]{1,0:T(8,128)(2,1)}, u32[]{:S(2)}) copy-start(bf16[64,5120]{1,0:T(8,128)(2,1)} %get-tuple-element.91) | copy-start | bytes 1966084
  217.3 19.5 %collective-permute-start.17 = (bf16[64,5120]{1,0:T(8,128)(2,1)S(1)}, bf16[64,5120]{1,0:T(8,128)(2,1)S(1)}, u32[]{:S(2)}, u32[]{:S(2)}) collective-permute-start(bf16[64,5120]{1,0:T(8,128)(2,1)S(1)} %add_convert_fusion.4), channel_id=1, source_target_pairs={{0,32},{16,48},{32,64},{48,80},{64,96},{80,112},{96,0},{112,16},{1... | collective-permute-start | bytes 1966088 | tf_op jit(solution)/shard_map/ppermute | solution.py:269
  218.0 21.1 %collective-permute-start.18 = (bf16[64,5120]{1,0:T(8,128)(2,1)S(1)}, bf16[64,5120]{1,0:T(8,128)(2,1)S(1)}, u32[]{:S(2)}, u32[]{:S(2)}) collective-permute-start(bf16[64,5120]{1,0:T(8,128)(2,1)S(1)} %add_convert_fusion.2), channel_id=1, source_target_pairs={{0,96},{16,112},{32,0},{48,16},{64,32},{80,48},{96,64},{112,80},{1... | collective-permute-start | bytes 1966088 | tf_op jit(solution)/shard_map/ppermute | solution.py:269
  261.6 5.6 %copy-start.7 = (bf16[128,5120]{1,0:T(8,128)(2,1)S(1)}, bf16[128,5120]{1,0:T(8,128)(2,1)}, u32[]{:S(2)}) copy-start(bf16[128,5120]{1,0:T(8,128)(2,1)} %param.12) | copy-start | bytes 3932164
  261.6 33.7 %all-to-all-start.5 = ((bf16[16,400,128]{2,1,0:T(8,128)(2,1)}), bf16[16,400,128]{2,1,0:T(8,128)(2,1)}, u32[]{:S(2)}, u32[]{:S(2)}) async-start(bf16[16,400,128]{2,1,0:T(8,128)(2,1)} %reshape.207), calls=%async_computation.6 | async-start | bytes 3276800 | tf_op jit(solution)/shard_map/all_to_all | solution.py:21
  269.3 29.8 %copy-start.4 = (f32[128,5120]{1,0:T(8,128)S(1)}, f32[128,5120]{1,0:T(8,128)}, u32[]{:S(2)}) copy-start(f32[128,5120]{1,0:T(8,128)} %convolution_select_fusion) | copy-start | bytes 7864324
  (1 other events, 0.7 us)
Sparse Core Ops, SparseCore 0:
  9.1 28.4 all-gather.3
  39.3 38.7 all-gather.5
  175.6 32.5 all-gather.7
  217.4 37.0 reduce-scatter.1

commit v3 on v2

--- a/solution.py
+++ b/solution.py
@@ -406,7 +406,8 @@
     low = add(mine[half:], mine_too[half:], from_below_low, from_above_low)
     done_a = jnp.concatenate([top, low])
 
-    back = (mm(unpack[:, :rows_a], done_a) + mm(unpack[:, rows_a:], done_b)).astype(BF16)
+    (back_a,) = tie(mm(unpack[:, :rows_a], done_a))
+    back = (back_a + mm(unpack[:, rows_a:], done_b)).astype(BF16)
     back = exchange(back.reshape(size, slab, row_count)).reshape(total, feature)
     turn = (((0,), (0,)), ((), ()))
     combined = lax.dot_general(home.astype(BF16), back, turn, preferred_element_type=F32)

time: 310 us -> 311 us (level)
  waiting for transfers between devices: 132 us -> 128 us
  transfers between devices with their start and end apart: 29 -> 29, of which waited for: 18 -> 18; matrix products, arithmetic and copies ran while one was open for 13% -> 14% of each run, Pallas kernels for 14% -> 14%
where the time goes in v3:
time: 311 us; the launch traced here: 309 us
  waiting for transfers between devices  128 us (41%)
  starting transfers between devices  52.9 us (17%)
  Pallas kernels  52.6 us (17%)
  local copies, waits for them, and re-layouts  21.3 us (7%)
  other arithmetic  20.1 us (6%)
  matrix products  19.1 us (6%)
  between operations  14.9 us (5%)
    all_to_all x6, waiting for transfers between devices, exchange(): return lax.all_to_all(blocks, 'expert', 0, 0, tiled=True)  48.9 us
    ppermute x10, waiting for transfers between devices, ring(): lax.ppermute(value, 'dp', [(i, (i + 2 * step) % size) for i in range(size)])  47.4 us
    pallas_call x4, Pallas kernels, expert_part(): pl.pallas_call(functools.partial(expert_kernel, len(blocks)), in_specs=[a...  43.2 us
    all_to_all x6, starting transfers between devices, exchange(): return lax.all_to_all(blocks, 'expert', 0, 0, tiled=True)  36.5 us
    dot_general x11, matrix products, mm(): return jnp.dot(a, b, preferred_element_type=F32)  16.1 us
    all_gather x1, waiting for transfers between devices, adapter_first(): first = lax.all_gather(fc1, 'dp', axis=2, tiled=True)  12.3 us
    convert_element_type x6, other arithmetic, add(): return total.astype(BF16)  11.7 us
    reduce_scatter x1, waiting for transfers between devices, on_device(): done_b = lax.psum_scatter(part_b, 'dp', scatter_dimension=0, tiled=True)  11 us
  transfers between devices with their start and end apart: 29, of which 18 were waited for; matrix products, arithmetic and copies ran while one was open for 14% of the time, Pallas kernels for 14%

profile of v3, /device:TPU:17, one launch (start us, length us, event | category | flops | bytes accessed | tf_op | source)
XLA Modules:
  0.0 309.3 jit_solution(3313920311262527788)
XLA Ops:
  11.1 1.7 fusion.2
  17.3 7.7 %all-to-all-start = ((bf16[16,408,128]{2,1,0:T(8,128)(2,1)}), bf16[16,408,128]{2,1,0:T(8,128)(2,1)S(1)}, u32[]{:S(2)}, u32[]{:S(2)}) async-start(bf16[16,408,128]{2,1,0:T(8,128)(2,1)} %pad_maximum_fusion), calls=%async_computation | async-start | bytes 3342336 | tf_op jit(solution)/shard_map/all_to_all | solution.py:21
  25.3 12.3 %all-gather.4.cloned.1.call-done = bf16[4,88,4096]{2,1,0:T(8,128)(2,1)} async-done(((bf16[4,88,512]{2,1,0:T(8,128)(2,1)}), bf16[4,88,4096]{2,1,0:T(8,128)(2,1)}) %all-gather.4.cloned.1.call-update) | async-done | bytes 2883600 | tf_op jit(solution)/shard_map/all_gather | solution.py:51
  37.6 2.6 convolution_convert_fusion.3
  41.3 8.0 %all-to-all-done = bf16[16,408,128]{2,1,0:T(8,128)(2,1)S(1)} async-done(((bf16[16,408,128]{2,1,0:T(8,128)(2,1)}), bf16[16,408,128]{2,1,0:T(8,128)(2,1)S(1)}, u32[]{:S(2)}, u32[]{:S(2)}) %all-to-all-start) | async-done | bytes 1671200 | tf_op jit(solution)/shard_map/all_to_all | solution.py:21
  50.5 1.4 copy.22
  51.9 4.7 %all-to-all-start.1 = ((bf16[16,144,256]{2,1,0:T(8,128)(2,1)}), bf16[16,144,256]{2,1,0:T(8,128)(2,1)S(1)}, u32[]{:S(2)}, u32[]{:S(2)}) async-start(bf16[16,144,256]{2,1,0:T(8,128)(2,1)} %bitcast.53), calls=%async_computation.1 | async-start | bytes 2359296 | tf_op jit(solution)/shard_map/all_to_all | solution.py:21
  56.7 1.6 reshape.206
  61.2 2.0 convolution_convert_fusion.1.refs_0_
  63.2 1.6 collective-permute-start
  66.2 7.3 %all-to-all-done.1.blocks_ref = bf16[16,144,256]{2,1,0:T(8,128)(2,1)S(1)} async-done(((bf16[16,144,256]{2,1,0:T(8,128)(2,1)}), bf16[16,144,256]{2,1,0:T(8,128)(2,1)S(1)}, u32[]{:S(2)}, u32[]{:S(2)}) %all-to-all-start.1) | async-done | bytes 1179680 | tf_op jit(solution)/shard_map/all_to_all | solution.py:21
  73.5 4.6 %all-gather.6.cloned.1.call-done.weights_ref = bf16[2048,1152]{1,0:T(8,128)(2,1)} async-done(((bf16[256,1152]{1,0:T(8,128)(2,1)}), bf16[2048,1152]{1,0:T(8,128)(2,1)}) %all-gather.6.cloned.1.call-update) | async-done | bytes 4718608 | tf_op jit(solution)/shard_map/all_gather | solution.py:329
  78.1 3.6 %layer.2 = bf16[16,144,256]{2,1,0:T(8,128)(2,1)} custom-call(bf16[16,144,256]{2,1,0:T(8,128)(2,1)S(1)} %all-to-all-done.1.blocks_ref, bf16[2048,1152]{1,0:T(8,128)(2,1)} %all-gather.6.cloned.1.call-done.weights_ref), custom_call_target="tpu_custom_call" | custom-call | flops 301989888 | bytes 4456448 | tf_op jit(solution)/shard_map/layer/pallas_call | solution.py:88
  81.7 6.5 %all-to-all-start.2 = ((bf16[16,144,256]{2,1,0:T(8,128)(2,1)}), bf16[16,144,256]{2,1,0:T(8,128)(2,1)S(1)}, u32[]{:S(2)}, u32[]{:S(2)}) async-start(bf16[16,144,256]{2,1,0:T(8,128)(2,1)} %layer.2), calls=%async_computation.2 | async-start | bytes 2359296 | tf_op jit(solution)/shard_map/all_to_all | solution.py:21
  88.2 9.2 %expert_part.4 = (bf16[128,5120]{1,0:T(8,128)(2,1)}, bf16[128,5120]{1,0:T(8,128)(2,1)}) custom-call(bf16[128,5120]{1,0:T(8,128)(2,1)} %copy-done.5, bf16[128,5120]{1,0:T(8,128)(2,1)} %collective-permute-done.refs_1_, bf16[5120,512]{1,0:T(8,128)(2,1)} %bitcast.40, bf16[5120,512]{1,0:T(8,128)(2,1)} %bitcast.44, bf16[512,5120]{1,0:T(8,128)(2,1)} %bitcast.48), custom_call_target="tpu_custom_call" | custom-call | flops 2013265920 | bytes 10485760 | tf_op jit(solution)/shard_map/expert_part/pallas_call | solution.py:240
  97.4 2.5 collective-permute-done.2.refs_2_
  100.5 2.0 slice.57
  102.5 2.0 slice.58
  106.6 4.0 %layer.3 = bf16[16,72,640]{2,1,0:T(8,128)(2,1)} custom-call(bf16[16,144,256]{2,1,0:T(8,128)(2,1)S(1)} %all-to-all-done.2.blocks_ref, bf16[2048,1152]{1,0:T(8,128)(2,1)} %all-gather.6.cloned.1.call-done.weights_ref), custom_call_target="tpu_custom_call" | custom-call | flops 377487360 | bytes 4980736 | tf_op jit(solution)/shard_map/layer/pallas_call | solution.py:88
  110.7 5.9 %all-to-all-start.3 = ((bf16[16,72,640]{2,1,0:T(8,128)(2,1)}), bf16[16,72,640]{2,1,0:T(8,128)(2,1)S(1)}, u32[]{:S(2)}, u32[]{:S(2)}) async-start(bf16[16,72,640]{2,1,0:T(8,128)(2,1)} %layer.3), calls=%async_computation.3 | async-start | bytes 2949120 | tf_op jit(solution)/shard_map/all_to_all | solution.py:21
  116.6 1.4 collective-permute-start.7
  118.1 2.5 collective-permute-done.6.refs_1_
  120.8 15.8 %expert_part.5 = (bf16[64,5120]{1,0:T(8,128)(2,1)}, bf16[64,5120]{1,0:T(8,128)(2,1)}, bf16[128,5120]{1,0:T(8,128)(2,1)}, bf16[64,5120]{1,0:T(8,128)(2,1)}, bf16[...) custom-call(bf16[128,5120]{1,0:T(8,128)(2,1)} %collective-permute-done.1.refs_0_, ...), custom_call_target="tpu_custom_call" | custom-call | flops 8053063680 | bytes 26214400 | tf_op jit(solution)/shard_map/expert_part/pallas_call | solution.py:240
  137.7 2.5 collective-permute-start.10
  142.4 5.8 %all-to-all-start.4 = ((bf16[16,72,640]{2,1,0:T(8,128)(2,1)}), bf16[16,72,640]{2,1,0:T(8,128)(2,1)S(1)}, u32[]{:S(2)}, u32[]{:S(2)}) async-start(bf16[16,72,640]{2,1,0:T(8,128)(2,1)} %broadcast_in_dim.62), calls=%async_computation.4 | async-start | bytes 2949120 | tf_op jit(solution)/shard_map/all_to_all | solution.py:21
  148.3 2.8 add_convert_fusion.6
  154.6 9.2 %expert_part.6 = (bf16[64,5120]{1,0:T(8,128)(2,1)}, bf16[64,5120]{1,0:T(8,128)(2,1)}, bf16[128,5120]{1,0:T(8,128)(2,1)}) custom-call(bf16[64,5120]{1,0:T(8,128)(2,1)} %collective-permute-done.5.refs_0_, bf16[64,5120]{1,0:T(8,128)(2,1)} %collective-permute-done.6.refs_1_, bf16[64,5120]{1,0:T(8,128)(2,1)} %collective-permute-done.8.refs_2_, ...), custom_call_target="tpu_custom_call" | custom-call | flops 4026531840 | bytes 20971520 | tf_op jit(solution)/shard_map/expert_part/pallas_call | solution.py:240
  163.8 6.8 %all-to-all-done.4.blocks_ref = bf16[16,72,640]{2,1,0:T(8,128)(2,1)S(1)} async-done(((bf16[16,72,640]{2,1,0:T(8,128)(2,1)}), bf16[16,72,640]{2,1,0:T(8,128)(2,1)S(1)}, u32[]{:S(2)}, u32[]{:S(2)}) %all-to-all-start.4) | async-done | bytes 1474592 | tf_op jit(solution)/shard_map/all_to_all | solution.py:21
  170.6 2.0 collective-permute-start.14
  172.9 1.8 visual_chunk.1
  175.6 2.1 add_convert_fusion.3
  179.2 20.9 %collective-permute-done.16 = bf16[64,5120]{1,0:T(8,128)(2,1)S(1)} collective-permute-done((bf16[64,5120]{1,0:T(8,128)(2,1)S(1)}, bf16[64,5120]{1,0:T(8,128)(2,1)S(1)}, u32[]{:S(2)}, u32[]{:S(2)}) %collective-permute-start.16) | collective-permute-done | bytes 655392 | tf_op jit(solution)/shard_map/ppermute | solution.py:269
  200.1 2.3 add_convert_fusion.2
  202.4 1.5 collective-permute-done.15
  204.9 3.3 %all-gather.8.cloned.1.call-done.refs_0_ = bf16[256,5120]{1,0:T(8,128)(2,1)} async-done(((bf16[32,5120]{1,0:T(8,128)(2,1)}), bf16[256,5120]{1,0:T(8,128)(2,1)}) %all-gather.8.cloned.1.call-update) | async-done | bytes 2621456 | tf_op jit(solution)/shard_map/all_gather | solution.py:398
  208.2 9.1 %expert_part.7 = bf16[256,5120]{1,0:T(8,128)(2,1)} custom-call(bf16[256,5120]{1,0:T(8,128)(2,1)} %all-gather.8.cloned.1.call-done.refs_0_, bf16[5120,512]{1,0:T(8,128)(2,1)} %bitcast.43, bf16[5120,512]{1,0:T(8,128)(2,1)} %bitcast.47, bf16[512,5120]{1,0:T(8,128)(2,1)} %bitcast.51), custom_call_target="tpu_custom_call" | custom-call | flops 4026531840 | bytes 20971520 | tf_op jit(solution)/shard_map/expert_part/pallas_call | solution.py:240
  219.0 18.2 %collective-permute-done.17 = bf16[64,5120]{1,0:T(8,128)(2,1)S(1)} collective-permute-done((bf16[64,5120]{1,0:T(8,128)(2,1)}, bf16[64,5120]{1,0:T(8,128)(2,1)S(1)}, u32[]{:S(2)}, u32[]{:S(2)}) %collective-permute-start.17) | collective-permute-done | bytes 655392 | tf_op jit(solution)/shard_map/ppermute | solution.py:269
  237.1 1.7 collective-permute-done.18
  238.8 2.5 add_convert_fusion.1
  241.3 2.2 fusion.5
  243.5 11.0 %reduce-scatter.2.cloned.1.call-done = bf16[32,5120]{1,0:T(8,128)(2,1)} async-done(((bf16[256,5120]{1,0:T(8,128)(2,1)}), bf16[32,5120]{1,0:T(8,128)(2,1)}) %reduce-scatter.2.cloned.1.call-update) | async-done | bytes 327696 | tf_op jit(solution)/shard_map/reduce_scatter | solution.py:404
  254.5 3.8 %fusion = bf16[160,5120]{1,0:T(8,128)(2,1)} fusion(f32[160,5120]{1,0:T(8,128)} %fusion.5, bf16[32,5120]{1,0:T(8,128)(2,1)} %reduce-scatter.2.cloned.1.call-done, pred[160,160]{1,0:T(32,128)(4,1)S(1)} %iota_compare_fusion), kind=kOutput, calls=%fused_computation.3 | convolution fusion | flops 54067200 | bytes 5263360 | tf_op jit(solution)/shard_map/dot_general | solution.py:17
  258.3 3.8 %reshape.207 = bf16[16,400,128]{2,1,0:T(8,128)(2,1)} reshape(bf16[160,5120]{1,0:T(8,128)(2,1)} %fusion) | data formatting | bytes 3276800 | tf_op jit(solution)/shard_map/reshape | solution.py:411
  262.1 5.8 %all-to-all-start.5 = ((bf16[16,400,128]{2,1,0:T(8,128)(2,1)}), bf16[16,400,128]{2,1,0:T(8,128)(2,1)}, u32[]{:S(2)}, u32[]{:S(2)}) async-start(bf16[16,400,128]{2,1,0:T(8,128)(2,1)} %reshape.207), calls=%async_computation.6 | async-start | bytes 3276800 | tf_op jit(solution)/shard_map/all_to_all | solution.py:21
  267.9 2.0 convolution_select_fusion
  270.0 26.0 %all-to-all-done.5 = bf16[16,400,128]{2,1,0:T(8,128)(2,1)} async-done(((bf16[16,400,128]{2,1,0:T(8,128)(2,1)}), bf16[16,400,128]{2,1,0:T(8,128)(2,1)}, u32[]{:S(2)}, u32[]{:S(2)}) %all-to-all-start.5) | async-done | bytes 1638432 | tf_op jit(solution)/shard_map/all_to_all | solution.py:21
  296.0 3.7 %reshape.208 = bf16[160,5120]{1,0:T(8,128)(2,1)} reshape(bf16[16,400,128]{2,1,0:T(8,128)(2,1)} %all-to-all-done.5) | data formatting | bytes 3276800 | tf_op jit(solution)/shard_map/reshape | solution.py:411
  299.7 3.0 fusion.1
  (126 shorter events, 29.8 us)
Async XLA Ops:
  6.5 6.3 %copy-start.19 = (s32[128,1]{0,1:T(1,128)S(1)}, s32[128,1]{0,1:T(1,128)}, u32[]{:S(2)}) copy-start(s32[128,1]{0,1:T(1,128)} %param.20) | copy-start | bytes 1540
  6.5 6.3 %copy-start.6 = (bf16[128,5120]{1,0:T(8,128)(2,1)S(1)}, bf16[128,5120]{1,0:T(8,128)(2,1)}, u32[]{:S(2)}) copy-start(bf16[128,5120]{1,0:T(8,128)(2,1)} %param.12) | copy-start | bytes 3932164
  6.5 6.3 %copy-start.1 = (bf16[5120,16]{0,1:T(8,128)(2,1)S(1)}, bf16[5120,16]{0,1:T(8,128)(2,1)}, u32[]{:S(2)}) copy-start(bf16[5120,16]{0,1:T(8,128)(2,1)} %param.19) | copy-start | bytes 491524
  6.5 31.1 %all-gather.4.cloned.1.call-start = ((), (), s32[]{:S(2)}) async-start(), calls=%async_computation.7 | async-start | bytes 3244032 | tf_op jit(solution)/shard_map/all_gather | solution.py:51
  7.3 70.8 %all-gather.6.cloned.1.call-start = ((), (), s32[]{:S(2)}) async-start(), calls=%async_computation.8 | async-start | bytes 5308416 | tf_op jit(solution)/shard_map/all_gather | solution.py:329
  14.9 1.4 copy-start.15
  15.0 1.4 copy-start.16
  17.3 7.8 %copy-start.17 = (bf16[1,24,24,88]{3,2,1,0:T(8,128)(2,1)S(1)}, bf16[1,24,24,88]{3,2,1,0:T(8,128)(2,1)}, u32[]{:S(2)}) copy-start(bf16[1,24,24,88]{3,2,1,0:T(8,128)(2,1)} %param.13) | copy-start | bytes 304132
  17.3 32.0 %all-to-all-start = ((bf16[16,408,128]{2,1,0:T(8,128)(2,1)}), bf16[16,408,128]{2,1,0:T(8,128)(2,1)S(1)}, u32[]{:S(2)}, u32[]{:S(2)}) async-start(bf16[16,408,128]{2,1,0:T(8,128)(2,1)} %pad_maximum_fusion), calls=%async_computation | async-start | bytes 3342336 | tf_op jit(solution)/shard_map/all_to_all | solution.py:21
  49.3 1.3 copy-start.2
  51.9 4.7 %slice-start = ((bf16[16,408,128]{2,1,0:T(8,128)(2,1)}), bf16[16,400,128]{2,1,0:T(8,128)(2,1)S(1)}, s32[]{:S(2)}) async-start(bf16[16,408,128]{2,1,0:T(8,128)(2,1)} %copy-done.2), calls=%async_computation.11 | async-start | bytes 3276800 | tf_op jit(solution)/shard_map/slice | solution.py:328
  51.9 21.5 %all-to-all-start.1 = ((bf16[16,144,256]{2,1,0:T(8,128)(2,1)}), bf16[16,144,256]{2,1,0:T(8,128)(2,1)S(1)}, u32[]{:S(2)}, u32[]{:S(2)}) async-start(bf16[16,144,256]{2,1,0:T(8,128)(2,1)} %bitcast.53), calls=%async_computation.1 | async-start | bytes 2359296 | tf_op jit(solution)/shard_map/all_to_all | solution.py:21
  63.2 18.6 %copy-start.5 = (bf16[128,5120]{1,0:T(8,128)(2,1)}, bf16[128,5120]{1,0:T(8,128)(2,1)S(1)}, u32[]{:S(2)}) copy-start(bf16[128,5120]{1,0:T(8,128)(2,1)S(1)} %convolution_convert_fusion.1.refs_0_) | copy-start | bytes 3932164
  63.2 25.1 %collective-permute-start = (bf16[128,5120]{1,0:T(8,128)(2,1)S(1)}, bf16[128,5120]{1,0:T(8,128)(2,1)}, u32[]{:S(2)}, u32[]{:S(2)}) collective-permute-start(bf16[128,5120]{1,0:T(8,128)(2,1)S(1)} %convolution_convert_fusion.1.refs_0_), channel_id=1, source_target_pairs={{0,16},{16,0},{32,48},{48,32},{64,80},{80,64},{96,112},{112,96},{1... | collective-permute-start | bytes 3932168 | tf_op jit(solution)/shard_map/ppermute | solution.py:274
  64.8 35.2 %collective-permute-start.2 = (bf16[128,5120]{1,0:T(8,128)(2,1)S(1)}, bf16[128,5120]{1,0:T(8,128)(2,1)}, u32[]{:S(2)}, u32[]{:S(2)}) collective-permute-start(bf16[128,5120]{1,0:T(8,128)(2,1)S(1)} %convolution_convert_fusion.1.refs_0_), channel_id=1, source_target_pairs={{0,96},{16,112},{32,0},{48,16},{64,32},{80,48},{96,64},{112,80},{1... | collective-permute-start | bytes 3932168 | tf_op jit(solution)/shard_map/ppermute | solution.py:269
  65.0 35.0 %collective-permute-start.1 = (bf16[128,5120]{1,0:T(8,128)(2,1)S(1)}, bf16[128,5120]{1,0:T(8,128)(2,1)}, u32[]{:S(2)}, u32[]{:S(2)}) collective-permute-start(bf16[128,5120]{1,0:T(8,128)(2,1)S(1)} %convolution_convert_fusion.1.refs_0_), channel_id=1, source_target_pairs={{0,32},{16,48},{32,64},{48,80},{64,96},{80,112},{96,0},{112,16},{1... | collective-permute-start | bytes 3932168 | tf_op jit(solution)/shard_map/ppermute | solution.py:269
  81.7 24.9 %all-to-all-start.2 = ((bf16[16,144,256]{2,1,0:T(8,128)(2,1)}), bf16[16,144,256]{2,1,0:T(8,128)(2,1)S(1)}, u32[]{:S(2)}, u32[]{:S(2)}) async-start(bf16[16,144,256]{2,1,0:T(8,128)(2,1)} %layer.2), calls=%async_computation.2 | async-start | bytes 2359296 | tf_op jit(solution)/shard_map/all_to_all | solution.py:21
  99.9 20.9 %collective-permute-start.3 = (bf16[128,5120]{1,0:T(8,128)(2,1)}, bf16[128,5120]{1,0:T(8,128)(2,1)}, u32[]{:S(2)}, u32[]{:S(2)}) collective-permute-start(bf16[128,5120]{1,0:T(8,128)(2,1)} %collective-permute-done.1.refs_0_), channel_id=1, source_target_pairs={{0,16},{16,0},{32,48},{48,32},{64,80},{80,64},{96,112},{112,96},{1... | collective-permute-start | bytes 3932168 | tf_op jit(solution)/shard_map/ppermute | solution.py:274
  100.5 20.3 %collective-permute-start.4 = (bf16[128,5120]{1,0:T(8,128)(2,1)}, bf16[128,5120]{1,0:T(8,128)(2,1)}, u32[]{:S(2)}, u32[]{:S(2)}) collective-permute-start(bf16[128,5120]{1,0:T(8,128)(2,1)} %collective-permute-done.2.refs_2_), channel_id=1, source_target_pairs={{0,16},{16,0},{32,48},{48,32},{64,80},{80,64},{96,112},{112,96},{1... | collective-permute-start | bytes 3932168 | tf_op jit(solution)/shard_map/ppermute | solution.py:274
  104.4 16.1 %collective-permute-start.6 = (bf16[64,5120]{1,0:T(8,128)(2,1)}, bf16[64,5120]{1,0:T(8,128)(2,1)}, u32[]{:S(2)}, u32[]{:S(2)}) collective-permute-start(bf16[64,5120]{1,0:T(8,128)(2,1)} %slice.58), channel_id=1, source_target_pairs={{0,96},{16,112},{32,0},{48,16},{64,32},{80,48},{96,64},{112,80},{1... | collective-permute-start | bytes 1966088 | tf_op jit(solution)/shard_map/ppermute | solution.py:269
  105.0 15.8 %collective-permute-start.5 = (bf16[64,5120]{1,0:T(8,128)(2,1)}, bf16[64,5120]{1,0:T(8,128)(2,1)}, u32[]{:S(2)}, u32[]{:S(2)}) collective-permute-start(bf16[64,5120]{1,0:T(8,128)(2,1)} %slice.57), channel_id=1, source_target_pairs={{0,32},{16,48},{32,64},{48,80},{64,96},{80,112},{96,0},{112,16},{1... | collective-permute-start | bytes 1966088 | tf_op jit(solution)/shard_map/ppermute | solution.py:269
  110.7 26.1 %all-to-all-start.3 = ((bf16[16,72,640]{2,1,0:T(8,128)(2,1)}), bf16[16,72,640]{2,1,0:T(8,128)(2,1)S(1)}, u32[]{:S(2)}, u32[]{:S(2)}) async-start(bf16[16,72,640]{2,1,0:T(8,128)(2,1)} %layer.3), calls=%async_computation.3 | async-start | bytes 2949120 | tf_op jit(solution)/shard_map/all_to_all | solution.py:21
  116.6 23.7 %copy-start.18 = (bf16[5120]{0:T(1024)(128)(2,1)S(1)}, bf16[5120]{0:T(1024)(128)(2,1)}, u32[]{:S(2)}) copy-start(bf16[5120]{0:T(1024)(128)(2,1)} %param.18) | copy-start | bytes 30724
  116.6 20.0 %collective-permute-start.7 = (bf16[128,5120]{1,0:T(8,128)(2,1)}, bf16[128,5120]{1,0:T(8,128)(2,1)S(1)}, u32[]{:S(2)}, u32[]{:S(2)}) collective-permute-start(bf16[128,5120]{1,0:T(8,128)(2,1)} %get-tuple-element.70), channel_id=1, source_target_pairs={{0,16},{16,0},{32,48},{48,32},{64,80},{80,64},{96,112},{112,96},{1... | collective-permute-start | bytes 3932168 | tf_op jit(solution)/shard_map/ppermute | solution.py:274
  137.7 10.6 %collective-permute-start.10 = (bf16[128,5120]{1,0:T(8,128)(2,1)}, bf16[128,5120]{1,0:T(8,128)(2,1)}, u32[]{:S(2)}, u32[]{:S(2)}) collective-permute-start(bf16[128,5120]{1,0:T(8,128)(2,1)} %get-tuple-element.80), channel_id=1, source_target_pairs={{0,16},{16,0},{32,48},{48,32},{64,80},{80,64},{96,112},{112,96},{1... | collective-permute-start | bytes 3932168 | tf_op jit(solution)/shard_map/ppermute | solution.py:274
  140.3 8.0 %collective-permute-start.11 = (bf16[128,5120]{1,0:T(8,128)(2,1)}, bf16[128,5120]{1,0:T(8,128)(2,1)S(1)}, u32[]{:S(2)}, u32[]{:S(2)}) collective-permute-start(bf16[128,5120]{1,0:T(8,128)(2,1)} %get-tuple-element.81), channel_id=1, source_target_pairs={{0,16},{16,0},{32,48},{48,32},{64,80},{80,64},{96,112},{112,96},{1... | collective-permute-start | bytes 3932168 | tf_op jit(solution)/shard_map/ppermute | solution.py:274
  140.3 14.3 %collective-permute-start.8 = (bf16[64,5120]{1,0:T(8,128)(2,1)}, bf16[64,5120]{1,0:T(8,128)(2,1)}, u32[]{:S(2)}, u32[]{:S(2)}) collective-permute-start(bf16[64,5120]{1,0:T(8,128)(2,1)} %collective-permute-done.5.refs_0_), channel_id=1, source_target_pairs={{0,16},{16,0},{32,48},{48,32},{64,80},{80,64},{96,112},{112,96},{1... | collective-permute-start | bytes 1966088 | tf_op jit(solution)/shard_map/ppermute | solution.py:274
  140.9 13.7 %collective-permute-start.9 = (bf16[64,5120]{1,0:T(8,128)(2,1)}, bf16[64,5120]{1,0:T(8,128)(2,1)}, u32[]{:S(2)}, u32[]{:S(2)}) collective-permute-start(bf16[64,5120]{1,0:T(8,128)(2,1)} %collective-permute-done.6.refs_1_), channel_id=1, source_target_pairs={{0,16},{16,0},{32,48},{48,32},{64,80},{80,64},{96,112},{112,96},{1... | collective-permute-start | bytes 1966088 | tf_op jit(solution)/shard_map/ppermute | solution.py:274
  142.4 28.2 %all-to-all-start.4 = ((bf16[16,72,640]{2,1,0:T(8,128)(2,1)}), bf16[16,72,640]{2,1,0:T(8,128)(2,1)S(1)}, u32[]{:S(2)}, u32[]{:S(2)}) async-start(bf16[16,72,640]{2,1,0:T(8,128)(2,1)} %broadcast_in_dim.62), calls=%async_computation.4 | async-start | bytes 2949120 | tf_op jit(solution)/shard_map/all_to_all | solution.py:21
  148.2 60.0 %all-gather.8.cloned.1.call-start = ((), (), s32[]{:S(2)}) async-start(), calls=%async_computation.9 | async-start | bytes 2949120 | tf_op jit(solution)/shard_map/all_gather | solution.py:398
  148.3 4.0 %copy-start.14 = (bf16[64,5120]{1,0:T(8,128)(2,1)S(1)}, bf16[64,5120]{1,0:T(8,128)(2,1)}, u32[]{:S(2)}) copy-start(bf16[64,5120]{1,0:T(8,128)(2,1)} %get-tuple-element.79) | copy-start | bytes 1966084
  148.3 5.0 %copy-start.8 = (bf16[128,5120]{1,0:T(8,128)(2,1)}, bf16[128,5120]{1,0:T(8,128)(2,1)S(1)}, u32[]{:S(2)}) copy-start(bf16[128,5120]{1,0:T(8,128)(2,1)S(1)} %collective-permute-done.11) | copy-start | bytes 3932164
  151.1 3.1 %copy-start.3 = (bf16[160,5120]{1,0:T(8,128)(2,1)S(1)}, bf16[160,5120]{1,0:T(8,128)(2,1)}, u32[]{:S(2)}) copy-start(bf16[160,5120]{1,0:T(8,128)(2,1)} %reshape.206) | copy-start | bytes 4915204
  151.1 19.5 %collective-permute-start.13 = (bf16[64,5120]{1,0:T(8,128)(2,1)}, bf16[64,5120]{1,0:T(8,128)(2,1)}, u32[]{:S(2)}, u32[]{:S(2)}) collective-permute-start(bf16[64,5120]{1,0:T(8,128)(2,1)} %add_convert_fusion.6), channel_id=1, source_target_pairs={{0,96},{16,112},{32,0},{48,16},{64,32},{80,48},{96,64},{112,80},{1... | collective-permute-start | bytes 1966088 | tf_op jit(solution)/shard_map/ppermute | solution.py:269
  153.3 17.3 %collective-permute-start.12 = (bf16[64,5120]{1,0:T(8,128)(2,1)}, bf16[64,5120]{1,0:T(8,128)(2,1)}, u32[]{:S(2)}, u32[]{:S(2)}) collective-permute-start(bf16[64,5120]{1,0:T(8,128)(2,1)} %add_convert_fusion.7), channel_id=1, source_target_pairs={{0,32},{16,48},{32,64},{48,80},{64,96},{80,112},{96,0},{112,16},{1... | collective-permute-start | bytes 1966088 | tf_op jit(solution)/shard_map/ppermute | solution.py:269
  170.6 5.0 %collective-permute-start.14 = (bf16[128,5120]{1,0:T(8,128)(2,1)}, bf16[128,5120]{1,0:T(8,128)(2,1)}, u32[]{:S(2)}, u32[]{:S(2)}) collective-permute-start(bf16[128,5120]{1,0:T(8,128)(2,1)} %get-tuple-element.93), channel_id=1, source_target_pairs={{0,16},{16,0},{32,48},{48,32},{64,80},{80,64},{96,112},{112,96},{1... | collective-permute-start | bytes 3932168 | tf_op jit(solution)/shard_map/ppermute | solution.py:274
  175.5 79.1 %reduce-scatter.2.cloned.1.call-start = ((), (), s32[]{:S(2)}) async-start(), calls=%async_computation.10 | async-start | bytes 2949120 | tf_op jit(solution)/shard_map/reduce_scatter | solution.py:404
  175.6 24.5 %copy-start.13 = (bf16[64,5120]{1,0:T(8,128)(2,1)S(1)}, bf16[64,5120]{1,0:T(8,128)(2,1)}, u32[]{:S(2)}) copy-start(bf16[64,5120]{1,0:T(8,128)(2,1)} %get-tuple-element.94) | copy-start | bytes 1966084
  177.6 22.4 %collective-permute-start.16 = (bf16[64,5120]{1,0:T(8,128)(2,1)S(1)}, bf16[64,5120]{1,0:T(8,128)(2,1)S(1)}, u32[]{:S(2)}, u32[]{:S(2)}) collective-permute-start(bf16[64,5120]{1,0:T(8,128)(2,1)S(1)} %get-tuple-element.110), channel_id=1, source_target_pairs={{0,96},{16,112},{32,0},{48,16},{64,32},{80,48},{96,64},{112,80},{1... | collective-permute-start | bytes 1966088 | tf_op jit(solution)/shard_map/ppermute | solution.py:269
  178.9 25.0 %collective-permute-start.15 = (bf16[64,5120]{1,0:T(8,128)(2,1)S(1)}, bf16[64,5120]{1,0:T(8,128)(2,1)S(1)}, u32[]{:S(2)}, u32[]{:S(2)}) collective-permute-start(bf16[64,5120]{1,0:T(8,128)(2,1)S(1)} %get-tuple-element.111), channel_id=1, source_target_pairs={{0,32},{16,48},{32,64},{48,80},{64,96},{80,112},{96,0},{112,16},{1... | collective-permute-start | bytes 1966088 | tf_op jit(solution)/shard_map/ppermute | solution.py:269
  200.1 3.8 %copy-start.9 = (bf16[128,5120]{1,0:T(8,128)(2,1)S(1)}, bf16[128,5120]{1,0:T(8,128)(2,1)}, u32[]{:S(2)}) copy-start(bf16[128,5120]{1,0:T(8,128)(2,1)} %copy-done.8) | copy-start | bytes 3932164
  200.1 3.8 %copy-start.12 = (bf16[64,5120]{1,0:T(8,128)(2,1)S(1)}, bf16[64,5120]{1,0:T(8,128)(2,1)}, u32[]{:S(2)}) copy-start(bf16[64,5120]{1,0:T(8,128)(2,1)} %get-tuple-element.91) | copy-start | bytes 1966084
  217.3 21.5 %copy-start.10 = (bf16[128,5120]{1,0:T(8,128)(2,1)S(1)}, bf16[128,5120]{1,0:T(8,128)(2,1)}, u32[]{:S(2)}) copy-start(bf16[128,5120]{1,0:T(8,128)(2,1)} %get-tuple-element.88) | copy-start | bytes 3932164
  217.3 19.8 %collective-permute-start.17 = (bf16[64,5120]{1,0:T(8,128)(2,1)}, bf16[64,5120]{1,0:T(8,128)(2,1)S(1)}, u32[]{:S(2)}, u32[]{:S(2)}) collective-permute-start(bf16[64,5120]{1,0:T(8,128)(2,1)} %add_convert_fusion.4), channel_id=1, source_target_pairs={{0,32},{16,48},{32,64},{48,80},{64,96},{80,112},{96,0},{112,16},{1... | collective-permute-start | bytes 1966088 | tf_op jit(solution)/shard_map/ppermute | solution.py:269
  218.0 20.8 %collective-permute-start.18 = (bf16[64,5120]{1,0:T(8,128)(2,1)}, bf16[64,5120]{1,0:T(8,128)(2,1)S(1)}, u32[]{:S(2)}, u32[]{:S(2)}) collective-permute-start(bf16[64,5120]{1,0:T(8,128)(2,1)} %add_convert_fusion.2), channel_id=1, source_target_pairs={{0,96},{16,112},{32,0},{48,16},{64,32},{80,48},{96,64},{112,80},{1... | collective-permute-start | bytes 1966088 | tf_op jit(solution)/shard_map/ppermute | solution.py:269
  262.1 5.8 %copy-start.7 = (bf16[128,5120]{1,0:T(8,128)(2,1)S(1)}, bf16[128,5120]{1,0:T(8,128)(2,1)}, u32[]{:S(2)}) copy-start(bf16[128,5120]{1,0:T(8,128)(2,1)} %param.12) | copy-start | bytes 3932164
  262.1 33.9 %all-to-all-start.5 = ((bf16[16,400,128]{2,1,0:T(8,128)(2,1)}), bf16[16,400,128]{2,1,0:T(8,128)(2,1)}, u32[]{:S(2)}, u32[]{:S(2)}) async-start(bf16[16,400,128]{2,1,0:T(8,128)(2,1)} %reshape.207), calls=%async_computation.6 | async-start | bytes 3276800 | tf_op jit(solution)/shard_map/all_to_all | solution.py:21
  270.0 29.8 %copy-start.4 = (f32[128,5120]{1,0:T(8,128)S(1)}, f32[128,5120]{1,0:T(8,128)}, u32[]{:S(2)}) copy-start(f32[128,5120]{1,0:T(8,128)} %convolution_select_fusion) | copy-start | bytes 7864324
  (2 other events, 1.8 us)
Sparse Core Ops, SparseCore 0:
  9.1 28.4 all-gather.3
  39.3 38.7 all-gather.5
  175.6 32.5 all-gather.7
  217.5 37.0 reduce-scatter.1

commit v4 on v2

--- a/solution.py
+++ b/solution.py
@@ -396,9 +396,9 @@
     take = (jnp.arange(rows_b, dtype=I32)[:, None] == jnp.where(mine_img, img_rank, -1)[None, :]).astype(BF16)
     visual, chunk_b = visual_chunk(visual_blocks, norm_gain, router, named_img, take, overflow)
     gathered_b = lax.all_gather(chunk_b, "dp", axis=0, tiled=True)
+    gathered_b, pass_up, pass_down = tie(gathered_b, pass_up, pass_down)
     on_above = add(above_top, above_too[:half], pass_up)
     on_below = add(below_low, below_too[half:], pass_down)
-    gathered_b, on_above, on_below = tie(gathered_b, on_above, on_below)
     from_below_top, from_above_low = ring(on_above, 1), ring(on_below, -1)
     (part_b,) = run([gathered_b], (gathered_b.shape[0],))
     done_b = lax.psum_scatter(part_b, "dp", scatter_dimension=0, tiled=True)

time: 310 us -> 314 us (1.013)
    ppermute x10, waiting for transfers between devices: 48.6 us -> 52.4 us  [ring(): lax.ppermute(value, 'dp', [(i, (i + 2 * step) % size) for i in range(size)])]
  transfers between devices with their start and end apart: 29 -> 29, of which waited for: 18 -> 18; matrix products, arithmetic and copies ran while one was open for 13% -> 13% of each run, Pallas kernels for 14% -> 13%
where the time goes in v4:
time: 314 us; the launch traced here: 313 us
  waiting for transfers between devices  133 us (42%)
  starting transfers between devices  54.1 us (17%)
  Pallas kernels  52.6 us (17%)
  local copies, waits for them, and re-layouts  22.3 us (7%)
  other arithmetic  18.6 us (6%)
  matrix products  16.4 us (5%)
  between operations  15 us (5%)
    ppermute x10, waiting for transfers between devices, ring(): lax.ppermute(value, 'dp', [(i, (i + 2 * step) % size) for i in range(size)])  52.4 us
    all_to_all x6, waiting for transfers between devices, exchange(): return lax.all_to_all(blocks, 'expert', 0, 0, tiled=True)  47.1 us
    pallas_call x4, Pallas kernels, expert_part(): pl.pallas_call(functools.partial(expert_kernel, len(blocks)), in_specs=[a...  43.2 us
    all_to_all x6, starting transfers between devices, exchange(): return lax.all_to_all(blocks, 'expert', 0, 0, tiled=True)  37.1 us
    dot_general x11, matrix products, mm(): return jnp.dot(a, b, preferred_element_type=F32)  13.4 us
    all_gather x1, waiting for transfers between devices, adapter_first(): first = lax.all_gather(fc1, 'dp', axis=2, tiled=True)  12.3 us
    reduce_scatter x1, waiting for transfers between devices, on_device(): done_b = lax.psum_scatter(part_b, 'dp', scatter_dimension=0, tiled=True)  11.1 us
    convert_element_type x6, other arithmetic, add(): return total.astype(BF16)  10.3 us
  transfers between devices with their start and end apart: 29, of which 18 were waited for; matrix products, arithmetic and copies ran while one was open for 13% of the time, Pallas kernels for 13%

profile of v4, /device:TPU:17, one launch (start us, length us, event | category | flops | bytes accessed | tf_op | source)
XLA Modules:
  0.0 312.5 jit_solution(13287529610218585924)
XLA Ops:
  11.2 1.7 fusion.2
  17.2 7.7 %all-to-all-start = ((bf16[16,408,128]{2,1,0:T(8,128)(2,1)}), bf16[16,408,128]{2,1,0:T(8,128)(2,1)S(1)}, u32[]{:S(2)}, u32[]{:S(2)}) async-start(bf16[16,408,128]{2,1,0:T(8,128)(2,1)} %pad_maximum_fusion), calls=%async_computation | async-start | bytes 3342336 | tf_op jit(solution)/shard_map/all_to_all | solution.py:21
  25.3 12.3 %all-gather.4.cloned.1.call-done = bf16[4,88,4096]{2,1,0:T(8,128)(2,1)} async-done(((bf16[4,88,512]{2,1,0:T(8,128)(2,1)}), bf16[4,88,4096]{2,1,0:T(8,128)(2,1)}) %all-gather.4.cloned.1.call-update) | async-done | bytes 2883600 | tf_op jit(solution)/shard_map/all_gather | solution.py:51
  37.6 2.6 convolution_convert_fusion.3
  41.4 7.9 %all-to-all-done = bf16[16,408,128]{2,1,0:T(8,128)(2,1)S(1)} async-done(((bf16[16,408,128]{2,1,0:T(8,128)(2,1)}), bf16[16,408,128]{2,1,0:T(8,128)(2,1)S(1)}, u32[]{:S(2)}, u32[]{:S(2)}) %all-to-all-start) | async-done | bytes 1671200 | tf_op jit(solution)/shard_map/all_to_all | solution.py:21
  51.8 4.7 %all-to-all-start.1 = ((bf16[16,144,256]{2,1,0:T(8,128)(2,1)}), bf16[16,144,256]{2,1,0:T(8,128)(2,1)S(1)}, u32[]{:S(2)}, u32[]{:S(2)}) async-start(bf16[16,144,256]{2,1,0:T(8,128)(2,1)} %bitcast.53), calls=%async_computation.1 | async-start | bytes 2359296 | tf_op jit(solution)/shard_map/all_to_all | solution.py:21
  56.6 1.6 reshape.206
  61.1 2.0 convolution_convert_fusion.1.refs_0_
  63.0 1.6 collective-permute-start
  66.1 7.3 %all-to-all-done.1.blocks_ref = bf16[16,144,256]{2,1,0:T(8,128)(2,1)S(1)} async-done(((bf16[16,144,256]{2,1,0:T(8,128)(2,1)}), bf16[16,144,256]{2,1,0:T(8,128)(2,1)S(1)}, u32[]{:S(2)}, u32[]{:S(2)}) %all-to-all-start.1) | async-done | bytes 1179680 | tf_op jit(solution)/shard_map/all_to_all | solution.py:21
  73.4 4.8 %all-gather.6.cloned.1.call-done.weights_ref = bf16[2048,1152]{1,0:T(8,128)(2,1)} async-done(((bf16[256,1152]{1,0:T(8,128)(2,1)}), bf16[2048,1152]{1,0:T(8,128)(2,1)}) %all-gather.6.cloned.1.call-update) | async-done | bytes 4718608 | tf_op jit(solution)/shard_map/all_gather | solution.py:329
  78.2 3.6 %layer.2 = bf16[16,144,256]{2,1,0:T(8,128)(2,1)} custom-call(bf16[16,144,256]{2,1,0:T(8,128)(2,1)S(1)} %all-to-all-done.1.blocks_ref, bf16[2048,1152]{1,0:T(8,128)(2,1)} %all-gather.6.cloned.1.call-done.weights_ref), custom_call_target="tpu_custom_call" | custom-call | flops 301989888 | bytes 4456448 | tf_op jit(solution)/shard_map/layer/pallas_call | solution.py:88
  81.8 6.5 %all-to-all-start.2 = ((bf16[16,144,256]{2,1,0:T(8,128)(2,1)}), bf16[16,144,256]{2,1,0:T(8,128)(2,1)S(1)}, u32[]{:S(2)}, u32[]{:S(2)}) async-start(bf16[16,144,256]{2,1,0:T(8,128)(2,1)} %layer.2), calls=%async_computation.2 | async-start | bytes 2359296 | tf_op jit(solution)/shard_map/all_to_all | solution.py:21
  88.3 9.2 %expert_part.4 = (bf16[128,5120]{1,0:T(8,128)(2,1)}, bf16[128,5120]{1,0:T(8,128)(2,1)}) custom-call(bf16[128,5120]{1,0:T(8,128)(2,1)} %copy-done.5, bf16[128,5120]{1,0:T(8,128)(2,1)} %collective-permute-done.refs_1_, bf16[5120,512]{1,0:T(8,128)(2,1)} %bitcast.40, bf16[5120,512]{1,0:T(8,128)(2,1)} %bitcast.44, bf16[512,5120]{1,0:T(8,128)(2,1)} %bitcast.48), custom_call_target="tpu_custom_call" | custom-call | flops 2013265920 | bytes 10485760 | tf_op jit(solution)/shard_map/expert_part/pallas_call | solution.py:240
  97.5 2.4 collective-permute-done.2.refs_2_
  100.5 2.0 slice.57
  102.5 2.0 slice.58
  106.8 4.0 %layer.3 = bf16[16,72,640]{2,1,0:T(8,128)(2,1)} custom-call(bf16[16,144,256]{2,1,0:T(8,128)(2,1)S(1)} %all-to-all-done.2.blocks_ref, bf16[2048,1152]{1,0:T(8,128)(2,1)} %all-gather.6.cloned.1.call-done.weights_ref), custom_call_target="tpu_custom_call" | custom-call | flops 377487360 | bytes 4980736 | tf_op jit(solution)/shard_map/layer/pallas_call | solution.py:88
  110.8 5.8 %all-to-all-start.3 = ((bf16[16,72,640]{2,1,0:T(8,128)(2,1)}), bf16[16,72,640]{2,1,0:T(8,128)(2,1)S(1)}, u32[]{:S(2)}, u32[]{:S(2)}) async-start(bf16[16,72,640]{2,1,0:T(8,128)(2,1)} %layer.3), calls=%async_computation.3 | async-start | bytes 2949120 | tf_op jit(solution)/shard_map/all_to_all | solution.py:21
  116.6 1.6 collective-permute-start.7
  118.2 2.3 collective-permute-done.6.refs_1_
  120.8 15.8 %expert_part.5 = (bf16[64,5120]{1,0:T(8,128)(2,1)}, bf16[64,5120]{1,0:T(8,128)(2,1)}, bf16[128,5120]{1,0:T(8,128)(2,1)}, bf16[64,5120]{1,0:T(8,128)(2,1)}, bf16[...) custom-call(bf16[128,5120]{1,0:T(8,128)(2,1)} %collective-permute-done.1.refs_0_, ...), custom_call_target="tpu_custom_call" | custom-call | flops 8053063680 | bytes 26214400 | tf_op jit(solution)/shard_map/expert_part/pallas_call | solution.py:240
  137.7 2.5 collective-permute-start.10
  143.4 5.8 %all-to-all-start.4 = ((bf16[16,72,640]{2,1,0:T(8,128)(2,1)}), bf16[16,72,640]{2,1,0:T(8,128)(2,1)S(1)}, u32[]{:S(2)}, u32[]{:S(2)}) async-start(bf16[16,72,640]{2,1,0:T(8,128)(2,1)} %broadcast_in_dim.62), calls=%async_computation.4 | async-start | bytes 2949120 | tf_op jit(solution)/shard_map/all_to_all | solution.py:21
  149.3 2.6 add_convert_fusion.6
  153.1 2.1 add_convert_fusion.7
  155.8 9.2 %expert_part.6 = (bf16[64,5120]{1,0:T(8,128)(2,1)}, bf16[64,5120]{1,0:T(8,128)(2,1)}, bf16[128,5120]{1,0:T(8,128)(2,1)}) custom-call(bf16[64,5120]{1,0:T(8,128)(2,1)} %collective-permute-done.5.refs_0_, bf16[64,5120]{1,0:T(8,128)(2,1)} %collective-permute-done.6.refs_1_, bf16[64,5120]{1,0:T(8,128)(2,1)} %collective-permute-done.8.refs_2_, ...), custom_call_target="tpu_custom_call" | custom-call | flops 4026531840 | bytes 20971520 | tf_op jit(solution)/shard_map/expert_part/pallas_call | solution.py:240
  165.0 6.6 %all-to-all-done.4.blocks_ref = bf16[16,72,640]{2,1,0:T(8,128)(2,1)S(1)} async-done(((bf16[16,72,640]{2,1,0:T(8,128)(2,1)}), bf16[16,72,640]{2,1,0:T(8,128)(2,1)S(1)}, u32[]{:S(2)}, u32[]{:S(2)}) %all-to-all-start.4) | async-done | bytes 1474592 | tf_op jit(solution)/shard_map/all_to_all | solution.py:21
  171.6 1.8 visual_chunk.1
  174.2 2.1 collective-permute-start.14
  176.2 2.9 collective-permute-done.14
  179.1 1.6 add_convert_fusion.4
  182.2 22.6 %collective-permute-done.16 = bf16[64,5120]{1,0:T(8,128)(2,1)S(1)} collective-permute-done((bf16[64,5120]{1,0:T(8,128)(2,1)S(1)}, bf16[64,5120]{1,0:T(8,128)(2,1)S(1)}, u32[]{:S(2)}, u32[]{:S(2)}) %collective-permute-start.16) | collective-permute-done | bytes 655392 | tf_op jit(solution)/shard_map/ppermute | solution.py:269
  204.8 3.8 %collective-permute-done.15 = bf16[64,5120]{1,0:T(8,128)(2,1)} collective-permute-done((bf16[64,5120]{1,0:T(8,128)(2,1)S(1)}, bf16[64,5120]{1,0:T(8,128)(2,1)}, u32[]{:S(2)}, u32[]{:S(2)}) %collective-permute-start.15) | collective-permute-done | bytes 655392 | tf_op jit(solution)/shard_map/ppermute | solution.py:269
  208.6 1.9 all-gather.8.cloned.1.call-done.refs_0_
  210.6 9.1 %expert_part.7 = bf16[256,5120]{1,0:T(8,128)(2,1)} custom-call(bf16[256,5120]{1,0:T(8,128)(2,1)} %all-gather.8.cloned.1.call-done.refs_0_, bf16[5120,512]{1,0:T(8,128)(2,1)} %bitcast.43, bf16[5120,512]{1,0:T(8,128)(2,1)} %bitcast.47, bf16[512,5120]{1,0:T(8,128)(2,1)} %bitcast.51), custom_call_target="tpu_custom_call" | custom-call | flops 4026531840 | bytes 20971520 | tf_op jit(solution)/shard_map/expert_part/pallas_call | solution.py:240
  220.7 1.7 add_convert_fusion.3
  224.6 18.3 %collective-permute-done.17 = bf16[64,5120]{1,0:T(8,128)(2,1)S(1)} collective-permute-done((bf16[64,5120]{1,0:T(8,128)(2,1)S(1)}, bf16[64,5120]{1,0:T(8,128)(2,1)S(1)}, u32[]{:S(2)}, u32[]{:S(2)}) %collective-permute-start.17) | collective-permute-done | bytes 655392 | tf_op jit(solution)/shard_map/ppermute | solution.py:269
  242.9 2.8 collective-permute-done.18
  245.7 2.1 add_convert_fusion.2
  247.8 11.1 %reduce-scatter.2.cloned.1.call-done = bf16[32,5120]{1,0:T(8,128)(2,1)} async-done(((bf16[256,5120]{1,0:T(8,128)(2,1)}), bf16[32,5120]{1,0:T(8,128)(2,1)}) %reduce-scatter.2.cloned.1.call-update) | async-done | bytes 327696 | tf_op jit(solution)/shard_map/reduce_scatter | solution.py:404
  260.5 1.8 fusion
  262.3 3.8 %reshape.207 = bf16[16,400,128]{2,1,0:T(8,128)(2,1)} reshape(bf16[160,5120]{1,0:T(8,128)(2,1)} %fusion) | data formatting | bytes 3276800 | tf_op jit(solution)/shard_map/reshape | solution.py:410
  266.0 6.6 %all-to-all-start.5 = ((bf16[16,400,128]{2,1,0:T(8,128)(2,1)}), bf16[16,400,128]{2,1,0:T(8,128)(2,1)}, u32[]{:S(2)}, u32[]{:S(2)}) async-start(bf16[16,400,128]{2,1,0:T(8,128)(2,1)} %reshape.207), calls=%async_computation.6 | async-start | bytes 3276800 | tf_op jit(solution)/shard_map/all_to_all | solution.py:21
  272.7 2.1 convolution_select_fusion
  274.8 24.4 %all-to-all-done.5 = bf16[16,400,128]{2,1,0:T(8,128)(2,1)} async-done(((bf16[16,400,128]{2,1,0:T(8,128)(2,1)}), bf16[16,400,128]{2,1,0:T(8,128)(2,1)}, u32[]{:S(2)}, u32[]{:S(2)}) %all-to-all-start.5) | async-done | bytes 1638432 | tf_op jit(solution)/shard_map/all_to_all | solution.py:21
  299.2 3.8 %reshape.208 = bf16[160,5120]{1,0:T(8,128)(2,1)} reshape(bf16[16,400,128]{2,1,0:T(8,128)(2,1)} %all-to-all-done.5) | data formatting | bytes 3276800 | tf_op jit(solution)/shard_map/reshape | solution.py:410
  302.9 3.0 fusion.1
  (140 shorter events, 32.2 us)
Async XLA Ops:
  6.5 6.3 %copy-start.26 = (s32[128,1]{0,1:T(1,128)S(1)}, s32[128,1]{0,1:T(1,128)}, u32[]{:S(2)}) copy-start(s32[128,1]{0,1:T(1,128)} %param.20) | copy-start | bytes 1540
  6.5 6.3 %copy-start.6 = (bf16[128,5120]{1,0:T(8,128)(2,1)S(1)}, bf16[128,5120]{1,0:T(8,128)(2,1)}, u32[]{:S(2)}) copy-start(bf16[128,5120]{1,0:T(8,128)(2,1)} %param.12) | copy-start | bytes 3932164
  6.5 6.3 %copy-start.1 = (bf16[5120,16]{0,1:T(8,128)(2,1)S(1)}, bf16[5120,16]{0,1:T(8,128)(2,1)}, u32[]{:S(2)}) copy-start(bf16[5120,16]{0,1:T(8,128)(2,1)} %param.19) | copy-start | bytes 491524
  6.5 31.1 %all-gather.4.cloned.1.call-start = ((), (), s32[]{:S(2)}) async-start(), calls=%async_computation.7 | async-start | bytes 3244032 | tf_op jit(solution)/shard_map/all_gather | solution.py:51
  7.3 71.0 %all-gather.6.cloned.1.call-start = ((), (), s32[]{:S(2)}) async-start(), calls=%async_computation.8 | async-start | bytes 5308416 | tf_op jit(solution)/shard_map/all_gather | solution.py:329
  8.7 4.7 %copy-start.20 = (pred[128]{0:T(512)(128)(4,1)}, pred[128]{0:T(512)(128)(4,1)S(1)}, u32[]{:S(2)}) copy-start(pred[128]{0:T(512)(128)(4,1)S(1)} %get-tuple-element.106) | copy-start | bytes 388
  8.7 4.7 %copy-start.22 = (s32[128]{0:T(128)}, s32[128]{0:T(128)S(1)}, u32[]{:S(2)}) copy-start(s32[128]{0:T(128)S(1)} %get-tuple-element.107) | copy-start | bytes 1540
  17.2 7.8 %copy-start.18 = (bf16[1,24,24,88]{3,2,1,0:T(8,128)(2,1)S(1)}, bf16[1,24,24,88]{3,2,1,0:T(8,128)(2,1)}, u32[]{:S(2)}) copy-start(bf16[1,24,24,88]{3,2,1,0:T(8,128)(2,1)} %param.13) | copy-start | bytes 304132
  17.2 32.0 %all-to-all-start = ((bf16[16,408,128]{2,1,0:T(8,128)(2,1)}), bf16[16,408,128]{2,1,0:T(8,128)(2,1)S(1)}, u32[]{:S(2)}, u32[]{:S(2)}) async-start(bf16[16,408,128]{2,1,0:T(8,128)(2,1)} %pad_maximum_fusion), calls=%async_computation | async-start | bytes 3342336 | tf_op jit(solution)/shard_map/all_to_all | solution.py:21
  51.8 4.7 %slice-start = ((bf16[16,408,128]{2,1,0:T(8,128)(2,1)}), bf16[16,400,128]{2,1,0:T(8,128)(2,1)S(1)}, s32[]{:S(2)}) async-start(bf16[16,408,128]{2,1,0:T(8,128)(2,1)} %copy-done.2), calls=%async_computation.11 | async-start | bytes 3276800 | tf_op jit(solution)/shard_map/slice | solution.py:328
  51.8 21.5 %all-to-all-start.1 = ((bf16[16,144,256]{2,1,0:T(8,128)(2,1)}), bf16[16,144,256]{2,1,0:T(8,128)(2,1)S(1)}, u32[]{:S(2)}, u32[]{:S(2)}) async-start(bf16[16,144,256]{2,1,0:T(8,128)(2,1)} %bitcast.53), calls=%async_computation.1 | async-start | bytes 2359296 | tf_op jit(solution)/shard_map/all_to_all | solution.py:21
  63.0 18.8 %copy-start.5 = (bf16[128,5120]{1,0:T(8,128)(2,1)}, bf16[128,5120]{1,0:T(8,128)(2,1)S(1)}, u32[]{:S(2)}) copy-start(bf16[128,5120]{1,0:T(8,128)(2,1)S(1)} %convolution_convert_fusion.1.refs_0_) | copy-start | bytes 3932164
  63.0 25.3 %collective-permute-start = (bf16[128,5120]{1,0:T(8,128)(2,1)S(1)}, bf16[128,5120]{1,0:T(8,128)(2,1)}, u32[]{:S(2)}, u32[]{:S(2)}) collective-permute-start(bf16[128,5120]{1,0:T(8,128)(2,1)S(1)} %convolution_convert_fusion.1.refs_0_), channel_id=1, source_target_pairs={{0,16},{16,0},{32,48},{48,32},{64,80},{80,64},{96,112},{112,96},{1... | collective-permute-start | bytes 3932168 | tf_op jit(solution)/shard_map/ppermute | solution.py:274
  64.7 35.3 %collective-permute-start.2 = (bf16[128,5120]{1,0:T(8,128)(2,1)S(1)}, bf16[128,5120]{1,0:T(8,128)(2,1)}, u32[]{:S(2)}, u32[]{:S(2)}) collective-permute-start(bf16[128,5120]{1,0:T(8,128)(2,1)S(1)} %convolution_convert_fusion.1.refs_0_), channel_id=1, source_target_pairs={{0,96},{16,112},{32,0},{48,16},{64,32},{80,48},{96,64},{112,80},{1... | collective-permute-start | bytes 3932168 | tf_op jit(solution)/shard_map/ppermute | solution.py:269
  64.8 35.1 %collective-permute-start.1 = (bf16[128,5120]{1,0:T(8,128)(2,1)S(1)}, bf16[128,5120]{1,0:T(8,128)(2,1)}, u32[]{:S(2)}, u32[]{:S(2)}) collective-permute-start(bf16[128,5120]{1,0:T(8,128)(2,1)S(1)} %convolution_convert_fusion.1.refs_0_), channel_id=1, source_target_pairs={{0,32},{16,48},{32,64},{48,80},{64,96},{80,112},{96,0},{112,16},{1... | collective-permute-start | bytes 3932168 | tf_op jit(solution)/shard_map/ppermute | solution.py:269
  81.8 24.9 %all-to-all-start.2 = ((bf16[16,144,256]{2,1,0:T(8,128)(2,1)}), bf16[16,144,256]{2,1,0:T(8,128)(2,1)S(1)}, u32[]{:S(2)}, u32[]{:S(2)}) async-start(bf16[16,144,256]{2,1,0:T(8,128)(2,1)} %layer.2), calls=%async_computation.2 | async-start | bytes 2359296 | tf_op jit(solution)/shard_map/all_to_all | solution.py:21
  99.9 20.8 %collective-permute-start.3 = (bf16[128,5120]{1,0:T(8,128)(2,1)}, bf16[128,5120]{1,0:T(8,128)(2,1)}, u32[]{:S(2)}, u32[]{:S(2)}) collective-permute-start(bf16[128,5120]{1,0:T(8,128)(2,1)} %collective-permute-done.1.refs_0_), channel_id=1, source_target_pairs={{0,16},{16,0},{32,48},{48,32},{64,80},{80,64},{96,112},{112,96},{1... | collective-permute-start | bytes 3932168 | tf_op jit(solution)/shard_map/ppermute | solution.py:274
  100.5 20.3 %collective-permute-start.4 = (bf16[128,5120]{1,0:T(8,128)(2,1)}, bf16[128,5120]{1,0:T(8,128)(2,1)}, u32[]{:S(2)}, u32[]{:S(2)}) collective-permute-start(bf16[128,5120]{1,0:T(8,128)(2,1)} %collective-permute-done.2.refs_2_), channel_id=1, source_target_pairs={{0,16},{16,0},{32,48},{48,32},{64,80},{80,64},{96,112},{112,96},{1... | collective-permute-start | bytes 3932168 | tf_op jit(solution)/shard_map/ppermute | solution.py:274
  104.4 16.1 %collective-permute-start.6 = (bf16[64,5120]{1,0:T(8,128)(2,1)}, bf16[64,5120]{1,0:T(8,128)(2,1)}, u32[]{:S(2)}, u32[]{:S(2)}) collective-permute-start(bf16[64,5120]{1,0:T(8,128)(2,1)} %slice.58), channel_id=1, source_target_pairs={{0,96},{16,112},{32,0},{48,16},{64,32},{80,48},{96,64},{112,80},{1... | collective-permute-start | bytes 1966088 | tf_op jit(solution)/shard_map/ppermute | solution.py:269
  105.0 15.8 %collective-permute-start.5 = (bf16[64,5120]{1,0:T(8,128)(2,1)}, bf16[64,5120]{1,0:T(8,128)(2,1)}, u32[]{:S(2)}, u32[]{:S(2)}) collective-permute-start(bf16[64,5120]{1,0:T(8,128)(2,1)} %slice.57), channel_id=1, source_target_pairs={{0,32},{16,48},{32,64},{48,80},{64,96},{80,112},{96,0},{112,16},{1... | collective-permute-start | bytes 1966088 | tf_op jit(solution)/shard_map/ppermute | solution.py:269
  110.8 26.0 %all-to-all-start.3 = ((bf16[16,72,640]{2,1,0:T(8,128)(2,1)}), bf16[16,72,640]{2,1,0:T(8,128)(2,1)S(1)}, u32[]{:S(2)}, u32[]{:S(2)}) async-start(bf16[16,72,640]{2,1,0:T(8,128)(2,1)} %layer.3), calls=%async_computation.3 | async-start | bytes 2949120 | tf_op jit(solution)/shard_map/all_to_all | solution.py:21
  116.6 23.7 %copy-start.19 = (bf16[5120]{0:T(1024)(128)(2,1)S(1)}, bf16[5120]{0:T(1024)(128)(2,1)}, u32[]{:S(2)}) copy-start(bf16[5120]{0:T(1024)(128)(2,1)} %param.18) | copy-start | bytes 30724
  116.6 20.0 %collective-permute-start.7 = (bf16[128,5120]{1,0:T(8,128)(2,1)}, bf16[128,5120]{1,0:T(8,128)(2,1)S(1)}, u32[]{:S(2)}, u32[]{:S(2)}) collective-permute-start(bf16[128,5120]{1,0:T(8,128)(2,1)} %get-tuple-element.70), channel_id=1, source_target_pairs={{0,16},{16,0},{32,48},{48,32},{64,80},{80,64},{96,112},{112,96},{1... | collective-permute-start | bytes 3932168 | tf_op jit(solution)/shard_map/ppermute | solution.py:274
  137.7 11.6 %collective-permute-start.10 = (bf16[128,5120]{1,0:T(8,128)(2,1)}, bf16[128,5120]{1,0:T(8,128)(2,1)S(1)}, u32[]{:S(2)}, u32[]{:S(2)}) collective-permute-start(bf16[128,5120]{1,0:T(8,128)(2,1)} %get-tuple-element.80), channel_id=1, source_target_pairs={{0,16},{16,0},{32,48},{48,32},{64,80},{80,64},{96,112},{112,96},{1... | collective-permute-start | bytes 3932168 | tf_op jit(solution)/shard_map/ppermute | solution.py:274
  140.2 9.1 %collective-permute-start.11 = (bf16[128,5120]{1,0:T(8,128)(2,1)}, bf16[128,5120]{1,0:T(8,128)(2,1)}, u32[]{:S(2)}, u32[]{:S(2)}) collective-permute-start(bf16[128,5120]{1,0:T(8,128)(2,1)} %get-tuple-element.81), channel_id=1, source_target_pairs={{0,16},{16,0},{32,48},{48,32},{64,80},{80,64},{96,112},{112,96},{1... | collective-permute-start | bytes 3932168 | tf_op jit(solution)/shard_map/ppermute | solution.py:274
  141.3 14.5 %collective-permute-start.8 = (bf16[64,5120]{1,0:T(8,128)(2,1)}, bf16[64,5120]{1,0:T(8,128)(2,1)}, u32[]{:S(2)}, u32[]{:S(2)}) collective-permute-start(bf16[64,5120]{1,0:T(8,128)(2,1)} %collective-permute-done.5.refs_0_), channel_id=1, source_target_pairs={{0,16},{16,0},{32,48},{48,32},{64,80},{80,64},{96,112},{112,96},{1... | collective-permute-start | bytes 1966088 | tf_op jit(solution)/shard_map/ppermute | solution.py:274
  141.9 14.0 %collective-permute-start.9 = (bf16[64,5120]{1,0:T(8,128)(2,1)}, bf16[64,5120]{1,0:T(8,128)(2,1)}, u32[]{:S(2)}, u32[]{:S(2)}) collective-permute-start(bf16[64,5120]{1,0:T(8,128)(2,1)} %collective-permute-done.6.refs_1_), channel_id=1, source_target_pairs={{0,16},{16,0},{32,48},{48,32},{64,80},{80,64},{96,112},{112,96},{1... | collective-permute-start | bytes 1966088 | tf_op jit(solution)/shard_map/ppermute | solution.py:274
  143.4 28.2 %all-to-all-start.4 = ((bf16[16,72,640]{2,1,0:T(8,128)(2,1)}), bf16[16,72,640]{2,1,0:T(8,128)(2,1)S(1)}, u32[]{:S(2)}, u32[]{:S(2)}) async-start(bf16[16,72,640]{2,1,0:T(8,128)(2,1)} %broadcast_in_dim.62), calls=%async_computation.4 | async-start | bytes 2949120 | tf_op jit(solution)/shard_map/all_to_all | solution.py:21
  149.2 61.4 %all-gather.8.cloned.1.call-start = ((), (), s32[]{:S(2)}) async-start(), calls=%async_computation.9 | async-start | bytes 2949120 | tf_op jit(solution)/shard_map/all_gather | solution.py:398
  149.3 3.8 %copy-start.15 = (bf16[64,5120]{1,0:T(8,128)(2,1)S(1)}, bf16[64,5120]{1,0:T(8,128)(2,1)}, u32[]{:S(2)}) copy-start(bf16[64,5120]{1,0:T(8,128)(2,1)} %get-tuple-element.79) | copy-start | bytes 1966084
  149.3 5.9 %copy-start.8 = (bf16[128,5120]{1,0:T(8,128)(2,1)}, bf16[128,5120]{1,0:T(8,128)(2,1)S(1)}, u32[]{:S(2)}) copy-start(bf16[128,5120]{1,0:T(8,128)(2,1)S(1)} %collective-permute-done.10) | copy-start | bytes 3932164
  151.9 3.6 %copy-start.3 = (bf16[160,5120]{1,0:T(8,128)(2,1)S(1)}, bf16[160,5120]{1,0:T(8,128)(2,1)}, u32[]{:S(2)}) copy-start(bf16[160,5120]{1,0:T(8,128)(2,1)} %reshape.206) | copy-start | bytes 4915204
  151.9 19.7 %collective-permute-start.13 = (bf16[64,5120]{1,0:T(8,128)(2,1)}, bf16[64,5120]{1,0:T(8,128)(2,1)}, u32[]{:S(2)}, u32[]{:S(2)}) collective-permute-start(bf16[64,5120]{1,0:T(8,128)(2,1)} %add_convert_fusion.6), channel_id=1, source_target_pairs={{0,96},{16,112},{32,0},{48,16},{64,32},{80,48},{96,64},{112,80},{1... | collective-permute-start | bytes 1966088 | tf_op jit(solution)/shard_map/ppermute | solution.py:269
  155.2 16.4 %collective-permute-start.12 = (bf16[64,5120]{1,0:T(8,128)(2,1)}, bf16[64,5120]{1,0:T(8,128)(2,1)}, u32[]{:S(2)}, u32[]{:S(2)}) collective-permute-start(bf16[64,5120]{1,0:T(8,128)(2,1)} %add_convert_fusion.7), channel_id=1, source_target_pairs={{0,32},{16,48},{32,64},{48,80},{64,96},{80,112},{96,0},{112,16},{1... | collective-permute-start | bytes 1966088 | tf_op jit(solution)/shard_map/ppermute | solution.py:269
  174.1 84.8 %reduce-scatter.2.cloned.1.call-start = ((), (), s32[]{:S(2)}) async-start(), calls=%async_computation.10 | async-start | bytes 2949120 | tf_op jit(solution)/shard_map/reduce_scatter | solution.py:404
  174.2 4.9 %collective-permute-start.14 = (bf16[128,5120]{1,0:T(8,128)(2,1)}, bf16[128,5120]{1,0:T(8,128)(2,1)S(1)}, u32[]{:S(2)}, u32[]{:S(2)}) collective-permute-start(bf16[128,5120]{1,0:T(8,128)(2,1)} %get-tuple-element.93), channel_id=1, source_target_pairs={{0,16},{16,0},{32,48},{48,32},{64,80},{80,64},{96,112},{112,96},{1... | collective-permute-start | bytes 3932168 | tf_op jit(solution)/shard_map/ppermute | solution.py:274
  180.7 24.1 %collective-permute-start.16 = (bf16[64,5120]{1,0:T(8,128)(2,1)S(1)}, bf16[64,5120]{1,0:T(8,128)(2,1)S(1)}, u32[]{:S(2)}, u32[]{:S(2)}) collective-permute-start(bf16[64,5120]{1,0:T(8,128)(2,1)S(1)} %get-tuple-element.110), channel_id=1, source_target_pairs={{0,96},{16,112},{32,0},{48,16},{64,32},{80,48},{96,64},{112,80},{1... | collective-permute-start | bytes 1966088 | tf_op jit(solution)/shard_map/ppermute | solution.py:269
  181.9 26.7 %collective-permute-start.15 = (bf16[64,5120]{1,0:T(8,128)(2,1)S(1)}, bf16[64,5120]{1,0:T(8,128)(2,1)}, u32[]{:S(2)}, u32[]{:S(2)}) collective-permute-start(bf16[64,5120]{1,0:T(8,128)(2,1)S(1)} %get-tuple-element.111), channel_id=1, source_target_pairs={{0,32},{16,48},{32,64},{48,80},{64,96},{80,112},{96,0},{112,16},{1... | collective-permute-start | bytes 1966088 | tf_op jit(solution)/shard_map/ppermute | solution.py:269
  222.4 20.5 %collective-permute-start.17 = (bf16[64,5120]{1,0:T(8,128)(2,1)S(1)}, bf16[64,5120]{1,0:T(8,128)(2,1)S(1)}, u32[]{:S(2)}, u32[]{:S(2)}) collective-permute-start(bf16[64,5120]{1,0:T(8,128)(2,1)S(1)} %add_convert_fusion.3), channel_id=1, source_target_pairs={{0,32},{16,48},{32,64},{48,80},{64,96},{80,112},{96,0},{112,16},{1... | collective-permute-start | bytes 1966088 | tf_op jit(solution)/shard_map/ppermute | solution.py:269
  223.1 22.5 %copy-start.10 = (bf16[128,5120]{1,0:T(8,128)(2,1)S(1)}, bf16[128,5120]{1,0:T(8,128)(2,1)}, u32[]{:S(2)}) copy-start(bf16[128,5120]{1,0:T(8,128)(2,1)} %get-tuple-element.88) | copy-start | bytes 3932164
  223.1 22.5 %copy-start.12 = (bf16[128,5120]{1,0:T(8,128)(2,1)S(1)}, bf16[128,5120]{1,0:T(8,128)(2,1)}, u32[]{:S(2)}) copy-start(bf16[128,5120]{1,0:T(8,128)(2,1)} %copy-done.11) | copy-start | bytes 3932164
  223.4 22.3 %collective-permute-start.18 = (bf16[64,5120]{1,0:T(8,128)(2,1)S(1)}, bf16[64,5120]{1,0:T(8,128)(2,1)S(1)}, u32[]{:S(2)}, u32[]{:S(2)}) collective-permute-start(bf16[64,5120]{1,0:T(8,128)(2,1)S(1)} %add_convert_fusion.1), channel_id=1, source_target_pairs={{0,96},{16,112},{32,0},{48,16},{64,32},{80,48},{96,64},{112,80},{1... | collective-permute-start | bytes 1966088 | tf_op jit(solution)/shard_map/ppermute | solution.py:269
  266.0 6.6 %copy-start.7 = (bf16[128,5120]{1,0:T(8,128)(2,1)S(1)}, bf16[128,5120]{1,0:T(8,128)(2,1)}, u32[]{:S(2)}) copy-start(bf16[128,5120]{1,0:T(8,128)(2,1)} %param.12) | copy-start | bytes 3932164
  266.0 6.6 %copy-start.21 = (pred[128]{0:T(512)(128)(4,1)S(1)}, pred[128]{0:T(512)(128)(4,1)}, u32[]{:S(2)}) copy-start(pred[128]{0:T(512)(128)(4,1)} %copy-done.20) | copy-start | bytes 388
  266.0 6.6 %copy-start.23 = (s32[128]{0:T(128)S(1)}, s32[128]{0:T(128)}, u32[]{:S(2)}) copy-start(s32[128]{0:T(128)} %copy-done.22) | copy-start | bytes 1540
  266.0 33.1 %all-to-all-start.5 = ((bf16[16,400,128]{2,1,0:T(8,128)(2,1)}), bf16[16,400,128]{2,1,0:T(8,128)(2,1)}, u32[]{:S(2)}, u32[]{:S(2)}) async-start(bf16[16,400,128]{2,1,0:T(8,128)(2,1)} %reshape.207), calls=%async_computation.6 | async-start | bytes 3276800 | tf_op jit(solution)/shard_map/all_to_all | solution.py:21
  274.8 28.2 %copy-start.4 = (f32[128,5120]{1,0:T(8,128)S(1)}, f32[128,5120]{1,0:T(8,128)}, u32[]{:S(2)}) copy-start(f32[128,5120]{1,0:T(8,128)} %convolution_select_fusion) | copy-start | bytes 7864324
  274.8 28.2 %copy-start.25 = (s32[128]{0:T(128)S(1)}, s32[128]{0:T(128)}, u32[]{:S(2)}) copy-start(s32[128]{0:T(128)} %copy-done.24) | copy-start | bytes 1540
  (9 other events, 12.3 us)
Sparse Core Ops, SparseCore 0:
  9.1 28.4 all-gather.3
  39.3 38.8 all-gather.5
  174.2 36.2 all-gather.7
  219.8 39.0 reduce-scatter.1
